TPU v7x, 32 devices: a whole 2x2x4 slice. The times are simulated.
32 devices in a mesh: rep: 8 (over z, y), ep: 4 (over x, core).
Axes of the slice: x: 2, y: 2, z: 4, core: 2. Of those that a mesh axis runs over, the one named last changes fastest.
Arguments:
- tokens: bfloat16 [16384, 1536], P(('rep', 'ep')), may hold values from -6 to 6
- norm_attn: bfloat16 [1536], replicated, may hold values from 0.099609375 to 1.8984375
- w_query: bfloat16 [1536, 1536], replicated, may hold values from -0.15625 to 0.15625
- key_projection: bfloat16 [1536, 512], replicated, may hold values from -0.15625 to 0.15625
- value_projection: bfloat16 [1536, 512], replicated, may hold values from -0.15625 to 0.15625
- w_out: bfloat16 [1536, 1536], replicated, may hold values from -2.5 to 2.5
- norm_ffn: bfloat16 [1536], replicated, may hold values from 0.099609375 to 1.8984375
- w_router: bfloat16 [1536, 20], replicated, may hold values from -0.078125 to 0.078125
- w_gate: bfloat16 [20, 1536, 512], P('ep'), may hold values from -0.15625 to 0.15625
- w_up: bfloat16 [20, 1536, 512], P('ep'), may hold values from -0.15625 to 0.15625
- w_down: bfloat16 [20, 512, 1536], P('ep'), may hold values from -3 to 3
- routes: int32 [16384, 8], P(('rep', 'ep')), may hold values from 0 to 19, as said below
- cotangent: bfloat16 [16384, 1536], P(('rep', 'ep')), may hold values from -6 to 6
Outputs:
- mixed: bfloat16 [16384, 1536], P(('rep', 'ep'))
- d_input: float32 [16384, 1536], P(('rep', 'ep'))
- grad_norm_attn: float32 [1536], P('ep')
- grad_query: float32 [1536, 1536], P('ep')
- grad_key: float32 [1536, 512], P('ep')
- grad_value: float32 [1536, 512], P('ep')
- grad_out: float32 [1536, 1536], P('ep')
- grad_norm_ffn: float32 [1536], P('ep')
- grad_router: float32 [1536, 20], P('ep')
- grad_gate: float32 [20, 1536, 512], P('ep')
- grad_up: float32 [20, 1536, 512], P('ep')
- grad_down: float32 [20, 512, 1536], P('ep')
Inputs may be any that keep to these rules, and one draw needn't show every extreme that they name: `routes`: each row names 8 different experts. In each aligned block of 512 rows (the rows of one device) no expert is named by more than 384 rows, and in each group of 4 consecutive such blocks one expert is named by exactly 384 rows of every block of the group.
All inputs are finite; a program needn't handle non-finite values.
Results may differ from a plain program's by a relative error of at most 0.02.
Values may be sent and summed in bfloat16 or wider, within the bound.
A program may use at most 448 MiB of HBM per device.

v0:
```python
import math

import jax
import jax.numpy as jnp
from jax import lax
from jax.sharding import PartitionSpec as P

QUERY_HEADS = 24
KEY_VALUE_HEADS = 8
HEAD_SIZE = 64
TOPK = 8
SEQUENCE_TOKENS = 512
BLOCK = 256
CAP = 384


epsilon = 1e-06
masked_value = -1e30


def rope_tables(token_count, width):
    half_width = width // 2
    places = (jnp.arange(token_count) % SEQUENCE_TOKENS).astype(jnp.float32)
    rates = jnp.exp(jnp.arange(half_width, dtype=jnp.float32) * (-2.0 * math.log(10000.0) / width))
    angles = places[:, None] * rates[None, :]
    return (jnp.cos(angles)[:, None, :], jnp.sin(angles)[:, None, :])


def apply_rotary(field, cosine_table, sine_table):
    half_width = field.shape[-1] // 2
    first = field[..., :half_width]
    second = field[..., half_width:]
    return jnp.concatenate(
        [first * cosine_table - second * sine_table, second * cosine_table + first * sine_table], -1
    )


def invert_rotary(field, cosine_table, sine_table):
    half_width = field.shape[-1] // 2
    first = field[..., :half_width]
    second = field[..., half_width:]
    return jnp.concatenate(
        [first * cosine_table + second * sine_table, second * cosine_table - first * sine_table], -1
    )


def norm_forward(field, gain):
    inverse = lax.rsqrt(jnp.mean(field * field, -1, keepdims=True) + epsilon)
    normal = field * inverse
    return ((normal * gain.astype(jnp.float32)).astype(jnp.bfloat16), normal, inverse)


def norm_backward(d_normed, normal, inverse, gain):
    scaled = d_normed * gain.astype(jnp.float32)
    d_field = inverse * (scaled - normal * jnp.mean(scaled * normal, -1, keepdims=True))
    return (d_field, jnp.sum(d_normed * normal, 0))


def score_block(queries, key_rows):
    places = jnp.arange(SEQUENCE_TOKENS) // BLOCK
    allowed = places[None, :] <= places[:, None]
    scores = jnp.einsum(
        "qhgd,khd->hgqk", queries, key_rows, preferred_element_type=jnp.float32
    ) * HEAD_SIZE ** (-0.5)
    return jnp.where(allowed, scores, masked_value)


def attend(pack):
    queries, key_rows, value_rows = pack
    scores = score_block(queries, key_rows)
    highest = jnp.max(scores, -1, keepdims=True)
    shifted = jnp.exp(scores - highest)
    totals = jnp.sum(shifted, -1, keepdims=True)
    probs_bf = (shifted / totals).astype(jnp.bfloat16)
    head_mix = jnp.einsum(
        "hgqk,khd->qhgd", probs_bf, value_rows, preferred_element_type=jnp.float32
    )
    return (head_mix.astype(jnp.bfloat16), highest + jnp.log(totals))


def attend_back(pack):
    queries, key_rows, value_rows, d_mix, log_totals = pack
    factor = HEAD_SIZE ** (-0.5)
    scores = score_block(queries, key_rows)
    probs_f = jnp.exp(scores - log_totals)
    probs_bf = probs_f.astype(jnp.bfloat16)
    d_probs = jnp.einsum("qhgd,khd->hgqk", d_mix, value_rows, preferred_element_type=jnp.float32)
    centre = jnp.sum(probs_f * d_probs, -1, keepdims=True)
    d_scores = (probs_f * (d_probs - centre)).astype(jnp.bfloat16)
    d_queries = (
        jnp.einsum("hgqk,khd->qhgd", d_scores, key_rows, preferred_element_type=jnp.float32)
        * factor
    )
    d_keys = (
        jnp.einsum("hgqk,qhgd->khd", d_scores, queries, preferred_element_type=jnp.float32) * factor
    )
    d_values = jnp.einsum("hgqk,qhgd->khd", probs_bf, d_mix, preferred_element_type=jnp.float32)
    return (d_queries, d_keys, d_values)


def expert_forward(rows, gate_w, up_w, down_w):
    gate_pre = jnp.einsum("erd,edf->erf", rows, gate_w, preferred_element_type=jnp.float32)
    up_pre = jnp.einsum("erd,edf->erf", rows, up_w, preferred_element_type=jnp.float32)
    hidden = (jax.nn.silu(gate_pre) * up_pre).astype(jnp.bfloat16)
    result = jnp.einsum("erf,efd->erd", hidden, down_w, preferred_element_type=jnp.float32).astype(
        jnp.bfloat16
    )
    return (result, gate_pre, up_pre, hidden)


def expert_backward(rows, gate_w, up_w, down_w, gate_pre, up_pre, hidden, d_result):
    d_hidden = jnp.einsum("erd,efd->erf", d_result, down_w, preferred_element_type=jnp.float32)
    grad_down = jnp.einsum("erf,erd->efd", hidden, d_result, preferred_element_type=jnp.float32)
    sigma = jax.nn.sigmoid(gate_pre)
    swish = gate_pre * sigma
    d_gate_pre = (d_hidden * up_pre * sigma * (1.0 + gate_pre * (1.0 - sigma))).astype(jnp.bfloat16)
    d_up_pre = (d_hidden * swish).astype(jnp.bfloat16)
    grad_gate = jnp.einsum("erd,erf->edf", rows, d_gate_pre, preferred_element_type=jnp.float32)
    grad_up = jnp.einsum("erd,erf->edf", rows, d_up_pre, preferred_element_type=jnp.float32)
    d_rows = jnp.einsum("erf,edf->erd", d_gate_pre, gate_w, preferred_element_type=jnp.float32)
    d_rows = d_rows + jnp.einsum("erf,edf->erd", d_up_pre, up_w, preferred_element_type=jnp.float32)
    return (d_rows.astype(jnp.bfloat16), grad_gate, grad_up, grad_down)


def pack_rows(rows, target, experts_all, width):
    buffer = jnp.zeros((experts_all * CAP, width), jnp.bfloat16).at[target].set(rows)
    return buffer.reshape(experts_all, CAP, width)


def unpack_rows(buffer, target, token_count, width):
    return buffer.reshape(-1, width)[target].reshape(token_count, TOPK, width)


def per_device(
    tokens,
    norm_attn,
    w_query,
    key_projection,
    value_projection,
    w_out,
    norm_ffn,
    w_router,
    w_gate,
    w_up,
    w_down,
    routes,
    cotangent,
):
    token_count = tokens.shape[0]
    width = tokens.shape[1]
    experts_all = w_router.shape[1]
    query_groups = QUERY_HEADS // KEY_VALUE_HEADS
    sequence_total = token_count // SEQUENCE_TOKENS
    x_float = tokens.astype(jnp.float32)
    hidden_first, normal_one, inverse_one = norm_forward(x_float, norm_attn)
    query_unrotated = jnp.dot(hidden_first, w_query, preferred_element_type=jnp.float32)
    key_unrotated = jnp.dot(hidden_first, key_projection, preferred_element_type=jnp.float32)
    value_row_block = jnp.dot(
        hidden_first, value_projection, preferred_element_type=jnp.float32
    ).astype(jnp.bfloat16)
    cosine_table, sine_table = rope_tables(token_count, HEAD_SIZE)
    query_rotated = apply_rotary(
        query_unrotated.reshape(token_count, QUERY_HEADS, HEAD_SIZE), cosine_table, sine_table
    ).astype(jnp.bfloat16)
    key_rotated = apply_rotary(
        key_unrotated.reshape(token_count, KEY_VALUE_HEADS, HEAD_SIZE), cosine_table, sine_table
    ).astype(jnp.bfloat16)
    query_sequence = query_rotated.reshape(
        sequence_total, SEQUENCE_TOKENS, KEY_VALUE_HEADS, query_groups, HEAD_SIZE
    )
    key_sequence = key_rotated.reshape(sequence_total, SEQUENCE_TOKENS, KEY_VALUE_HEADS, HEAD_SIZE)
    value_sequence = value_row_block.reshape(
        sequence_total, SEQUENCE_TOKENS, KEY_VALUE_HEADS, HEAD_SIZE
    )
    attn_seq, log_totals = lax.map(attend, (query_sequence, key_sequence, value_sequence))
    attn_flat = attn_seq.reshape(token_count, QUERY_HEADS * HEAD_SIZE)
    branch = jnp.dot(attn_flat, w_out, preferred_element_type=jnp.float32)
    resid = x_float + branch
    h_two, normal_two, inverse_two = norm_forward(resid, norm_ffn)
    logits = jnp.dot(h_two, w_router, preferred_element_type=jnp.float32)
    router_probs = jax.nn.softmax(logits, -1)
    expert_ids = jnp.arange(experts_all)
    choose = (routes[:, :, None] == expert_ids[None, None, :]).astype(jnp.float32)
    gates = jnp.sum(choose * router_probs[:, None, :], -1)
    flat_routes = routes.reshape(-1)
    matches = (flat_routes[:, None] == expert_ids[None, :]).astype(jnp.int32)
    slot_of = jnp.sum((jnp.cumsum(matches, 0) - 1) * matches, 1)
    target = flat_routes * CAP + slot_of
    send_buf = pack_rows(jnp.repeat(h_two, TOPK, axis=0), target, experts_all, width)
    recv_rows = lax.all_to_all(send_buf, "ep", split_axis=0, concat_axis=1, tiled=True)
    y_buf, gate_pre, up_pre, hidden = expert_forward(recv_rows, w_gate, w_up, w_down)
    back_y = lax.all_to_all(y_buf, "ep", split_axis=1, concat_axis=0, tiled=True)
    y_rows = unpack_rows(back_y, target, token_count, width)
    moe_sum = jnp.sum(gates[:, :, None] * y_rows.astype(jnp.float32), 1)
    mixed = (resid + moe_sum).astype(jnp.bfloat16)
    d_out = cotangent.astype(jnp.float32)
    d_gates = jnp.einsum("tkd,td->tk", y_rows, cotangent, preferred_element_type=jnp.float32)
    d_router = jnp.sum(choose * d_gates[:, :, None], 1)
    d_logits = (
        router_probs * (d_router - jnp.sum(router_probs * d_router, -1, keepdims=True))
    ).astype(jnp.bfloat16)
    grad_router = jnp.einsum("td,te->de", h_two, d_logits, preferred_element_type=jnp.float32)
    d_htwo = jnp.einsum("te,de->td", d_logits, w_router, preferred_element_type=jnp.float32)
    d_y = (
        (gates[:, :, None] * d_out[:, None, :])
        .astype(jnp.bfloat16)
        .reshape(token_count * TOPK, width)
    )
    d_send = pack_rows(d_y, target, experts_all, width)
    d_recv = lax.all_to_all(d_send, "ep", split_axis=0, concat_axis=1, tiled=True)
    d_rows_held, grad_gate, grad_up, grad_down = expert_backward(
        recv_rows, w_gate, w_up, w_down, gate_pre, up_pre, hidden, d_recv
    )
    back_rows = lax.all_to_all(d_rows_held, "ep", split_axis=1, concat_axis=0, tiled=True)
    d_htwo = d_htwo + jnp.sum(
        unpack_rows(back_rows, target, token_count, width).astype(jnp.float32), 1
    )
    d_resid_norm, grad_norm_ffn = norm_backward(d_htwo, normal_two, inverse_two, norm_ffn)
    d_resid = d_out + d_resid_norm
    d_branch = d_resid.astype(jnp.bfloat16)
    grad_out = jnp.einsum("ta,td->ad", attn_flat, d_branch, preferred_element_type=jnp.float32)
    attention_gradient = jnp.einsum(
        "td,ad->ta", d_branch, w_out, preferred_element_type=jnp.float32
    ).astype(jnp.bfloat16)
    attention_gradient = attention_gradient.reshape(
        sequence_total, SEQUENCE_TOKENS, KEY_VALUE_HEADS, query_groups, HEAD_SIZE
    )
    d_q_rot, rotated_key_gradient, value_sequence_gradient = lax.map(
        attend_back, (query_sequence, key_sequence, value_sequence, attention_gradient, log_totals)
    )
    d_q_pre = (
        invert_rotary(
            d_q_rot.reshape(token_count, QUERY_HEADS, HEAD_SIZE), cosine_table, sine_table
        )
        .reshape(token_count, QUERY_HEADS * HEAD_SIZE)
        .astype(jnp.bfloat16)
    )
    d_k_pre = (
        invert_rotary(
            rotated_key_gradient.reshape(token_count, KEY_VALUE_HEADS, HEAD_SIZE),
            cosine_table,
            sine_table,
        )
        .reshape(token_count, KEY_VALUE_HEADS * HEAD_SIZE)
        .astype(jnp.bfloat16)
    )
    value_rows_gradient = value_sequence_gradient.reshape(
        token_count, KEY_VALUE_HEADS * HEAD_SIZE
    ).astype(jnp.bfloat16)
    grad_query = jnp.einsum("td,tq->dq", hidden_first, d_q_pre, preferred_element_type=jnp.float32)
    grad_key = jnp.einsum("td,tq->dq", hidden_first, d_k_pre, preferred_element_type=jnp.float32)
    grad_value = jnp.einsum(
        "td,tq->dq", hidden_first, value_rows_gradient, preferred_element_type=jnp.float32
    )
    d_hone = jnp.einsum("tq,dq->td", d_q_pre, w_query, preferred_element_type=jnp.float32)
    d_hone = d_hone + jnp.einsum(
        "tq,dq->td", d_k_pre, key_projection, preferred_element_type=jnp.float32
    )
    d_hone = d_hone + jnp.einsum(
        "tq,dq->td", value_rows_gradient, value_projection, preferred_element_type=jnp.float32
    )
    d_x_norm, grad_norm_attn = norm_backward(d_hone, normal_one, inverse_one, norm_attn)
    d_input = d_resid + d_x_norm
    part_na, part_q, part_k, part_v, part_o, part_nf, part_r = (
        lax.psum_scatter(
            grad_norm_attn.astype(jnp.bfloat16), "ep", scatter_dimension=0, tiled=True
        ).astype(jnp.float32),
        lax.psum_scatter(
            grad_query.astype(jnp.bfloat16), "ep", scatter_dimension=0, tiled=True
        ).astype(jnp.float32),
        lax.psum_scatter(
            grad_key.astype(jnp.bfloat16), "ep", scatter_dimension=0, tiled=True
        ).astype(jnp.float32),
        lax.psum_scatter(
            grad_value.astype(jnp.bfloat16), "ep", scatter_dimension=0, tiled=True
        ).astype(jnp.float32),
        lax.psum_scatter(
            grad_out.astype(jnp.bfloat16), "ep", scatter_dimension=0, tiled=True
        ).astype(jnp.float32),
        lax.psum_scatter(
            grad_norm_ffn.astype(jnp.bfloat16), "ep", scatter_dimension=0, tiled=True
        ).astype(jnp.float32),
        lax.psum_scatter(
            grad_router.astype(jnp.bfloat16), "ep", scatter_dimension=0, tiled=True
        ).astype(jnp.float32),
    )
    part_gate, part_up, part_down = (grad_gate, grad_up, grad_down)
    sum_na, sum_q, sum_k, sum_v, sum_o, sum_nf, sum_r = lax.psum(
        (part_na, part_q, part_k, part_v, part_o, part_nf, part_r), "rep"
    )
    share_gate, share_up, share_down = (
        lax.psum_scatter(part_gate, "rep", scatter_dimension=1, tiled=True),
        lax.psum_scatter(part_up, "rep", scatter_dimension=1, tiled=True),
        lax.psum_scatter(part_down, "rep", scatter_dimension=2, tiled=True),
    )
    full_gate, full_up, full_down = (
        lax.all_gather(share_gate.astype(jnp.bfloat16), "rep", axis=1, tiled=True).astype(
            share_gate.dtype
        ),
        lax.all_gather(share_up.astype(jnp.bfloat16), "rep", axis=1, tiled=True).astype(
            share_up.dtype
        ),
        lax.all_gather(share_down.astype(jnp.bfloat16), "rep", axis=2, tiled=True).astype(
            share_down.dtype
        ),
    )
    return (
        mixed,
        d_input,
        sum_na,
        sum_q,
        sum_k,
        sum_v,
        sum_o,
        sum_nf,
        sum_r,
        full_gate,
        full_up,
        full_down,
    )


def solution(mesh):
    placed = (
        P(("rep", "ep"), None),
        P(),
        P(),
        P(),
        P(),
        P(),
        P(),
        P(),
        P("ep", None, None),
        P("ep", None, None),
        P("ep", None, None),
        P(("rep", "ep"), None),
        P(("rep", "ep"), None),
    )
    return jax.shard_map(
        per_device,
        mesh=mesh,
        in_specs=placed,
        out_specs=(
            P(("rep", "ep"), None),
            P(("rep", "ep"), None),
            P("ep"),
            P("ep", None),
            P("ep", None),
            P("ep", None),
            P("ep", None),
            P("ep"),
            P("ep", None),
            P("ep", None, None),
            P("ep", None, None),
            P("ep", None, None),
        ),
        check_vma=False,
    )
```

profile of v0, /device:TPU:0, one launch (start us, length us, event | category | flops | bytes accessed | tf_op | source)
XLA Modules:
  0.0 2776.9 jit_solution(4677663683264362506)
XLA Ops:
  74.2 32.5 %scatter_custom_fusion = bf16[7680,1536]{1,0:T(8,128)(2,1)} fusion(s32[4096]{0:T(1024)S(1)} %bitcast.201, bf16[]{:T(256)} %constant.121.clone.1, bf16[512,1536]{1,0:T(8,128)(2,1)S(1)} %multiply_convert_fusion.3), kind=kCustom, calls=%fused_computation.29 | custom fusion | bytes 25165826 | tf_op jit(solution)/shard_map/scatter | solution.py:126
  106.7 262.0 %all_to_all.66 = bf16[20,384,1536]{2,1,0:T(8,128)(2,1)S(1)} all-to-all(bf16[20,384,1536]{2,1,0:T(8,128)(2,1)} %bitcast.173), channel_id=1, replica_groups=mesh['rep'=8,'ep'=4] {'ep'}, dimensions={0} | all-to-all | bytes 47185920 | tf_op jit(solution)/shard_map/all_to_all | solution.py:190
  376.7 22.3 fusion.71
  399.0 29.6 %multiply_convert_fusion.2 = (bf16[5,1536,512]{2,1,0:T(8,128)(2,1)}, f32[5,1536,512]{2,1,0:T(8,128)}) fusion(f32[5,1536,512]{2,1,0:T(8,128)} %fusion.71, bf16[5,1536,1536]{2,1,0:T(8,128)(2,1)} %bitcast.175, bf16[5,1536,512]{2,1,0:T(8,128)(2,1)} %param.22), kind=kOutput, calls=%fused_computation.23 | convolution fusion | flops 12103188480 | bytes 70778880 | tf_op jit(solution)/shard_map/erd,edf->erf/dot_general | solution.py:103
  448.5 27.3 copy.92
  491.3 402.7 %all-to-all-done.1 = bf16[5,1536,1536]{2,0,1:T(8,128)(2,1)} async-done(((bf16[5,1536,1536]{2,0,1:T(8,128)(2,1)}), bf16[5,1536,1536]{2,0,1:T(8,128)(2,1)}, u32[]{:S(2)}, u32[]{:S(2)}) %all-to-all-start.1) | async-done | bytes 23592992 | tf_op jit(solution)/shard_map/all_to_all | solution.py:192
  894.1 28.5 %copy.93 = bf16[5,4,384,1536]{3,2,0,1:T(8,128)(2,1)} copy(bf16[5,4,384,1536]{3,0,2,1:T(8,128)(2,1)} %bitcast.20) | data formatting | bytes 47185920 | tf_op jit(solution)/shard_map/all_to_all | solution.py:192
  922.6 36.2 %gather_fusion = bf16[4096,1536]{1,0:T(8,128)(2,1)} fusion(bf16[7680,1536]{1,0:T(8,128)(2,1)} %bitcast.169, s32[4096]{0:T(1024)S(1)} %broadcast_clamp_fusion), kind=kCustom, calls=%fused_computation | custom fusion | bytes 25182208 | tf_op jit(solution)/shard_map/gather | solution.py:131
  976.4 33.3 %scatter_custom_fusion.1 = bf16[7680,1536]{1,0:T(8,128)(2,1)} fusion(s32[4096]{0:T(1024)S(1)} %bitcast.203, bf16[4096,1536]{1,0:T(8,128)(2,1)} %fusion.3, bf16[]{:T(256)} %constant.121.clone.1), kind=kCustom, calls=%fused_computation.33 | custom fusion | bytes 23593472 | tf_op jit(solution)/shard_map/scatter | solution.py:126
  1009.8 261.4 %all_to_all.67 = bf16[20,384,1536]{2,1,0:T(8,128)(2,1)S(1)} all-to-all(bf16[20,384,1536]{2,1,0:T(8,128)(2,1)} %bitcast.170), channel_id=1, replica_groups=mesh['rep'=8,'ep'=4] {'ep'}, dimensions={0} | all-to-all | bytes 47185920 | tf_op jit(solution)/shard_map/all_to_all | solution.py:210
  1300.3 29.0 %multiply_convert_fusion = (bf16[5,1536,512]{2,1,0:T(8,128)(2,1)}, bf16[5,1536,512]{2,1,0:T(8,128)(2,1)}) fusion(f32[5,1536,512]{2,1,0:T(8,128)} %fusion.71, f32[5,1536,512]{2,1,0:T(8,128)} %get-tuple-element.139, bf16[5,1536,1536]{2,1,0:T(8,128)(2,1)} %bitcast.179, bf16[5,512,1536]{2,1,0:T(8,128)(2,1)} %param.23), kind=kOutput, calls=%fused_computation.21 | convolution fusion | flops 12130713600 | bytes 78643200 | tf_op jit(solution)/shard_map/erd,efd->erf/dot_general | solution.py:112
  1373.0 24.3 fusion.72
  1397.3 30.6 %add_convert_fusion = bf16[5,1536,1536]{2,1,0:T(8,128)(2,1)} fusion(f32[5,1536,1536]{2,1,0:T(8,128)} %fusion.72, bf16[5,1536,512]{2,1,0:T(8,128)(2,1)} %get-tuple-element.120, bf16[5,1536,512]{2,1,0:T(8,128)(2,1)} %param.22), kind=kOutput, calls=%fused_computation.4 | convolution fusion | flops 12103188480 | bytes 86507520 | tf_op jit(solution)/shard_map/erf,edf->erd/dot_general | solution.py:121
  1427.9 27.3 copy.96
  1484.9 390.5 %all-to-all-done.3 = bf16[5,1536,1536]{2,0,1:T(8,128)(2,1)} async-done(((bf16[5,1536,1536]{2,0,1:T(8,128)(2,1)}), bf16[5,1536,1536]{2,0,1:T(8,128)(2,1)}, u32[]{:S(2)}, u32[]{:S(2)}) %all-to-all-start.3) | async-done | bytes 23592992 | tf_op jit(solution)/shard_map/all_to_all | solution.py:214
  1875.5 28.9 %copy.97 = bf16[5,4,384,1536]{3,2,0,1:T(8,128)(2,1)} copy(bf16[5,4,384,1536]{3,0,2,1:T(8,128)(2,1)} %bitcast.31) | data formatting | bytes 47185920 | tf_op jit(solution)/shard_map/all_to_all | solution.py:214
  1904.4 36.1 %gather_fusion.1 = bf16[4096,1536]{1,0:T(8,128)(2,1)} fusion(bf16[7680,1536]{1,0:T(8,128)(2,1)} %bitcast.168, s32[4096]{0:T(1024)S(1)} %copy-done.42), kind=kCustom, calls=%fused_computation.1 | custom fusion | bytes 25182208 | tf_op jit(solution)/shard_map/gather | solution.py:131
  1998.6 22.7 fusion.2
  2114.4 31.3 %reduce-scatter.13.cloned.1.call-done = bf16[384,512]{1,0:T(8,128)(2,1)} async-done(((bf16[1536,512]{1,0:T(8,128)(2,1)}), bf16[384,512]{1,0:T(8,128)(2,1)}) %reduce-scatter.13.cloned.1.call-update) | async-done | bytes 393232 | tf_op jit(solution)/shard_map/reduce_scatter | solution.py:271
  2145.7 50.4 %reduce-scatter.17.cloned.1.call-done = bf16[384,1536]{1,0:T(8,128)(2,1)} async-done(((bf16[1536,1536]{1,0:T(8,128)(2,1)}), bf16[384,1536]{1,0:T(8,128)(2,1)}) %reduce-scatter.17.cloned.1.call-update) | async-done | bytes 1179664 | tf_op jit(solution)/shard_map/reduce_scatter | solution.py:277
  2196.1 50.6 %reduce-scatter.11.cloned.1.call-done = bf16[384,1536]{1,0:T(8,128)(2,1)} async-done(((bf16[1536,1536]{1,0:T(8,128)(2,1)}), bf16[384,1536]{1,0:T(8,128)(2,1)}) %reduce-scatter.11.cloned.1.call-update) | async-done | bytes 1179664 | tf_op jit(solution)/shard_map/reduce_scatter | solution.py:268
  2246.6 310.2 %all-reduce.5 = (f32[384]{0:T(512)}, f32[384,1536]{1,0:T(8,128)}, f32[384,512]{1,0:T(8,128)}, f32[384,512]{1,0:T(8,128)}, f32[384,1536]{1,0:T(8,128)}, /*index=5*/f32[384]{0:T(512)}, f32[384,20]{0,1:T(8,128)}) all-reduce(f32[384]{0:T(512)S(1)} %get-tuple-element.147, ...), channel_id=1, replica_groups=mesh['rep'=8,'ep'=4] {'rep'}, use_global_device_ids=true, to_apply=%region_21.22 | all-reduce | flops 1581312 | bytes 9489408 | tf_op jit(solution)/shard_map/psum | solution.py:288
  2568.3 71.0 %all-gather.6.cloned.1.call-done = bf16[5,1536,512]{2,1,0:T(8,128)(2,1)} async-done(((bf16[5,192,512]{2,1,0:T(8,128)(2,1)}), bf16[5,1536,512]{2,1,0:T(8,128)(2,1)}) %all-gather.6.cloned.1.call-update) | async-done | bytes 7864336 | tf_op jit(solution)/shard_map/all_gather | solution.py:300
  2650.9 107.8 %all-gather.4.cloned.1.call-done = bf16[5,1536,512]{2,1,0:T(8,128)(2,1)} async-done(((bf16[5,192,512]{2,1,0:T(8,128)(2,1)}), bf16[5,1536,512]{2,1,0:T(8,128)(2,1)}) %all-gather.4.cloned.1.call-update) | async-done | bytes 7864336 | tf_op jit(solution)/shard_map/all_gather | solution.py:297
  (250 shorter events, 414.4 us)
Async XLA Ops:
  12.5 59.9 %copy-start.43 = (f32[1536]{0:T(1024)}, f32[1536]{0:T(1024)S(1)}, u32[]{:S(2)}) copy-start(f32[1536]{0:T(1024)S(1)} %convert_element_type.213) | copy-start | bytes 18436
  13.0 43.9 %copy-start.12 = (pred[512,512]{0,1:T(8,128)(4,1)}, pred[512,512]{0,1:T(8,128)(4,1)S(1)}, u32[]{:S(2)}) copy-start(pred[512,512]{0,1:T(8,128)(4,1)S(1)} %broadcast_compare_fusion) | copy-start | bytes 786436
  29.9 27.0 copy-start.34
  45.5 23.6 slice-start
  72.2 34.5 %copy-start.49 = (f32[512]{0:T(512)}, f32[512]{0:T(512)S(1)}, u32[]{:S(2)}) copy-start(f32[512]{0:T(512)S(1)} %add_rsqrt_fusion) | copy-start | bytes 6148
  74.2 415.9 %copy-start.3 = (bf16[512,1536]{1,0:T(8,128)(2,1)}, bf16[512,1536]{1,0:T(8,128)(2,1)S(1)}, u32[]{:S(2)}) copy-start(bf16[512,1536]{1,0:T(8,128)(2,1)S(1)} %multiply_convert_fusion.3) | copy-start | bytes 4718596
  475.8 418.3 %all-to-all-start.1 = ((bf16[5,1536,1536]{2,0,1:T(8,128)(2,1)}), bf16[5,1536,1536]{2,0,1:T(8,128)(2,1)}, u32[]{:S(2)}, u32[]{:S(2)}) async-start(bf16[5,1536,1536]{2,0,1:T(8,128)(2,1)} %copy.92), calls=%async_computation.1 | async-start | bytes 75497472 | tf_op jit(solution)/shard_map/all_to_all | solution.py:192
  486.3 1569.1 %reduce-scatter.23.cloned.1.call-start = ((), (), s32[]{:S(2)}) async-start(), calls=%async_computation.20 | async-start | bytes 17694720 | tf_op jit(solution)/shard_map/reduce_scatter | solution.py:294
  490.7 431.9 %copy-start.47 = (f32[512]{0:T(512)}, f32[512]{0:T(512)S(1)}, u32[]{:S(2)}) copy-start(f32[512]{0:T(512)S(1)} %get-tuple-element.140) | copy-start | bytes 6148
  490.8 431.8 %copy-start.51 = (f32[512]{0:T(512)}, f32[512]{0:T(512)S(1)}, u32[]{:S(2)}) copy-start(f32[512]{0:T(512)S(1)} %fusion.47) | copy-start | bytes 6148
  491.3 431.3 %copy-start.41 = (s32[4096]{0:T(1024)}, s32[4096]{0:T(1024)S(1)}, u32[]{:S(2)}) copy-start(s32[4096]{0:T(1024)S(1)} %broadcast_clamp_fusion) | copy-start | bytes 49156
  922.6 36.2 %copy-start.10 = (bf16[512,1536]{1,0:T(8,128)(2,1)S(1)}, bf16[512,1536]{1,0:T(8,128)(2,1)}, u32[]{:S(2)}) copy-start(bf16[512,1536]{1,0:T(8,128)(2,1)} %param.25) | copy-start | bytes 4718596
  1300.2 757.9 %reduce-scatter.21.cloned.1.call-start = ((), (), s32[]{:S(2)}) async-start(), calls=%async_computation.18 | async-start | bytes 17694720 | tf_op jit(solution)/shard_map/reduce_scatter | solution.py:293
  1351.0 710.4 %reduce-scatter.19.cloned.1.call-start = ((), (), s32[]{:S(2)}) async-start(), calls=%async_computation.16 | async-start | bytes 17694720 | tf_op jit(solution)/shard_map/reduce_scatter | solution.py:292
  1455.2 420.2 %all-to-all-start.3 = ((bf16[5,1536,1536]{2,0,1:T(8,128)(2,1)}), bf16[5,1536,1536]{2,0,1:T(8,128)(2,1)}, u32[]{:S(2)}, u32[]{:S(2)}) async-start(bf16[5,1536,1536]{2,0,1:T(8,128)(2,1)} %copy.96), calls=%async_computation.3 | async-start | bytes 75497472 | tf_op jit(solution)/shard_map/all_to_all | solution.py:214
  1465.9 617.8 %reduce-scatter.25.cloned.1.call-start = ((), (), s32[]{:S(2)}) async-start(), calls=%async_computation.22 | async-start | bytes 491520
  1471.4 643.0 %reduce-scatter.15.cloned.1.call-start = ((), (), s32[]{:S(2)}) async-start(), calls=%async_computation.14 | async-start | bytes 1966080 | tf_op jit(solution)/shard_map/reduce_scatter | solution.py:274
  1875.5 28.9 %copy-start.42 = (s32[4096]{0:T(1024)S(1)}, s32[4096]{0:T(1024)}, u32[]{:S(2)}) copy-start(s32[4096]{0:T(1024)} %copy-done.41) | copy-start | bytes 49156
  1998.5 147.2 %reduce-scatter.13.cloned.1.call-start = ((), (), s32[]{:S(2)}) async-start(), calls=%async_computation.13 | async-start | bytes 1966080 | tf_op jit(solution)/shard_map/reduce_scatter | solution.py:271
  2033.3 162.7 %reduce-scatter.17.cloned.1.call-start = ((), (), s32[]{:S(2)}) async-start(), calls=%async_computation.15 | async-start | bytes 5898240 | tf_op jit(solution)/shard_map/reduce_scatter | solution.py:277
  2040.8 205.8 %reduce-scatter.11.cloned.1.call-start = ((), (), s32[]{:S(2)}) async-start(), calls=%async_computation.12 | async-start | bytes 5898240 | tf_op jit(solution)/shard_map/reduce_scatter | solution.py:268
  2055.3 501.5 %all-gather.8.cloned.1.call-start = ((), (), s32[]{:S(2)}) async-start(), calls=%async_computation.21 | async-start | bytes 8847360 | tf_op jit(solution)/shard_map/all_gather | solution.py:303
  2058.1 581.2 %all-gather.6.cloned.1.call-start = ((), (), s32[]{:S(2)}) async-start(), calls=%async_computation.19 | async-start | bytes 8847360 | tf_op jit(solution)/shard_map/all_gather | solution.py:300
  2060.8 697.8 %all-gather.4.cloned.1.call-start = ((), (), s32[]{:S(2)}) async-start(), calls=%async_computation.17 | async-start | bytes 8847360 | tf_op jit(solution)/shard_map/all_gather | solution.py:297
  (52 other events, 466.9 us)
Sparse Core Ops, SparseCore 0:
  1300.4 252.2 reduce-scatter.22
  1556.8 250.2 reduce-scatter.20
  1811.2 250.1 reduce-scatter.18
  2063.8 19.9 reduce-scatter.24
  2086.1 28.1 reduce-scatter.14
  2117.5 28.1 reduce-scatter.12
  2148.2 47.8 reduce-scatter.16
  2198.8 47.8 reduce-scatter.10
  2248.8 246.0 all-gather.7
  2497.5 141.6 all-gather.5
  2642.0 116.5 all-gather.3
where the time goes:
time: 2790 us; the launch traced here: 2780 us
  waiting for transfers between devices  1130 us (41%)
  blocking collectives  840 us (30%)
  matrix products  339 us (12%)
  local copies, waits for them, and re-layouts  295 us (11%)
  other arithmetic  133 us (5%)
    all_to_all x1, waiting for transfers between devices, per_device(): lax.all_to_all(y_buf, 'ep', split_axis=1, concat_axis=0, tiled=True)  403 us
    all_to_all x1, waiting for transfers between devices, per_device(): lax.all_to_all(d_rows_held, 'ep', split_axis=1, concat_axis=0, tiled=True)  391 us
    psum x1, blocking collectives, per_device(): lax.psum((part_na, part_q, part_k, part_v, part_o, part_nf, part_r), 'rep')  310 us
    all_to_all x1, blocking collectives, per_device(): lax.all_to_all(send_buf, 'ep', split_axis=0, concat_axis=1, tiled=True)  262 us
    all_to_all x1, blocking collectives, per_device(): lax.all_to_all(d_send, 'ep', split_axis=0, concat_axis=1, tiled=True)  261 us
    all_gather x1, waiting for transfers between devices, per_device(): lax.all_gather(share_gate.astype(jnp.bfloat16), 'rep', axis=1, tiled=True)  108 us
    gather x2, local copies, waits for them, and re-layouts, unpack_rows(): return buffer.reshape(-1, width)[target].reshape(token_count, TOPK, width)  72.3 us
    all_gather x1, waiting for transfers between devices, per_device(): lax.all_gather(share_up.astype(jnp.bfloat16), 'rep', axis=1, tiled=True)  71 us
  transfers between devices with their start and end apart: 13, of which 10 were waited for; matrix products, arithmetic and copies ran while one was open for 14% of the time, Pallas kernels for 0%

commit v1 on v0

--- a/solution.py
+++ b/solution.py
@@ -11,7 +11,6 @@
 TOPK = 8
 SEQUENCE_TOKENS = 512
 BLOCK = 256
-CAP = 384
 
 
 epsilon = 1e-06
@@ -96,39 +95,6 @@
     )
     d_values = jnp.einsum("hgqk,qhgd->khd", probs_bf, d_mix, preferred_element_type=jnp.float32)
     return (d_queries, d_keys, d_values)
-
-
-def expert_forward(rows, gate_w, up_w, down_w):
-    gate_pre = jnp.einsum("erd,edf->erf", rows, gate_w, preferred_element_type=jnp.float32)
-    up_pre = jnp.einsum("erd,edf->erf", rows, up_w, preferred_element_type=jnp.float32)
-    hidden = (jax.nn.silu(gate_pre) * up_pre).astype(jnp.bfloat16)
-    result = jnp.einsum("erf,efd->erd", hidden, down_w, preferred_element_type=jnp.float32).astype(
-        jnp.bfloat16
-    )
-    return (result, gate_pre, up_pre, hidden)
-
-
-def expert_backward(rows, gate_w, up_w, down_w, gate_pre, up_pre, hidden, d_result):
-    d_hidden = jnp.einsum("erd,efd->erf", d_result, down_w, preferred_element_type=jnp.float32)
-    grad_down = jnp.einsum("erf,erd->efd", hidden, d_result, preferred_element_type=jnp.float32)
-    sigma = jax.nn.sigmoid(gate_pre)
-    swish = gate_pre * sigma
-    d_gate_pre = (d_hidden * up_pre * sigma * (1.0 + gate_pre * (1.0 - sigma))).astype(jnp.bfloat16)
-    d_up_pre = (d_hidden * swish).astype(jnp.bfloat16)
-    grad_gate = jnp.einsum("erd,erf->edf", rows, d_gate_pre, preferred_element_type=jnp.float32)
-    grad_up = jnp.einsum("erd,erf->edf", rows, d_up_pre, preferred_element_type=jnp.float32)
-    d_rows = jnp.einsum("erf,edf->erd", d_gate_pre, gate_w, preferred_element_type=jnp.float32)
-    d_rows = d_rows + jnp.einsum("erf,edf->erd", d_up_pre, up_w, preferred_element_type=jnp.float32)
-    return (d_rows.astype(jnp.bfloat16), grad_gate, grad_up, grad_down)
-
-
-def pack_rows(rows, target, experts_all, width):
-    buffer = jnp.zeros((experts_all * CAP, width), jnp.bfloat16).at[target].set(rows)
-    return buffer.reshape(experts_all, CAP, width)
-
-
-def unpack_rows(buffer, target, token_count, width):
-    return buffer.reshape(-1, width)[target].reshape(token_count, TOPK, width)
 
 
 def per_device(
@@ -152,6 +118,7 @@
     query_groups = QUERY_HEADS // KEY_VALUE_HEADS
     sequence_total = token_count // SEQUENCE_TOKENS
     x_float = tokens.astype(jnp.float32)
+    cot_all = lax.all_gather(cotangent, "ep", axis=0, tiled=True)
     hidden_first, normal_one, inverse_one = norm_forward(x_float, norm_attn)
     query_unrotated = jnp.dot(hidden_first, w_query, preferred_element_type=jnp.float32)
     key_unrotated = jnp.dot(hidden_first, key_projection, preferred_element_type=jnp.float32)
@@ -180,41 +147,64 @@
     logits = jnp.dot(h_two, w_router, preferred_element_type=jnp.float32)
     router_probs = jax.nn.softmax(logits, -1)
     expert_ids = jnp.arange(experts_all)
-    choose = (routes[:, :, None] == expert_ids[None, None, :]).astype(jnp.float32)
-    gates = jnp.sum(choose * router_probs[:, None, :], -1)
-    flat_routes = routes.reshape(-1)
-    matches = (flat_routes[:, None] == expert_ids[None, :]).astype(jnp.int32)
-    slot_of = jnp.sum((jnp.cumsum(matches, 0) - 1) * matches, 1)
-    target = flat_routes * CAP + slot_of
-    send_buf = pack_rows(jnp.repeat(h_two, TOPK, axis=0), target, experts_all, width)
-    recv_rows = lax.all_to_all(send_buf, "ep", split_axis=0, concat_axis=1, tiled=True)
-    y_buf, gate_pre, up_pre, hidden = expert_forward(recv_rows, w_gate, w_up, w_down)
-    back_y = lax.all_to_all(y_buf, "ep", split_axis=1, concat_axis=0, tiled=True)
-    y_rows = unpack_rows(back_y, target, token_count, width)
-    moe_sum = jnp.sum(gates[:, :, None] * y_rows.astype(jnp.float32), 1)
-    mixed = (resid + moe_sum).astype(jnp.bfloat16)
+    chosen = jnp.max((routes[:, :, None] == jnp.arange(experts_all)[None, None, :]).astype(jnp.float32), 1)
+    combine = chosen * router_probs
+    h_all = lax.all_gather(h_two, "ep", axis=0, tiled=True)
+    combine_all = lax.all_gather(combine, "ep", axis=0, tiled=True)
+    holder = lax.axis_index("ep")
+    held = w_gate.shape[0]
+    weight = lax.dynamic_slice_in_dim(combine_all, holder * held, held, 1)
+    y_part = jnp.zeros((h_all.shape[0], width), jnp.float32)
+    dh_part = jnp.zeros((h_all.shape[0], width), jnp.float32)
+    d_router_cols, grads = [], []
+    gh_list, dg_list, du_list = [], [], []
+    for e in range(held):
+        gate_pre = jnp.dot(h_all, w_gate[e], preferred_element_type=jnp.float32)
+        up_pre = jnp.dot(h_all, w_up[e], preferred_element_type=jnp.float32)
+        back = jnp.einsum("td,fd->tf", cot_all, w_down[e], preferred_element_type=jnp.float32)
+        column = weight[:, e : e + 1]
+        sigma = jax.nn.sigmoid(gate_pre)
+        swish = gate_pre * sigma
+        hidden = (swish * up_pre).astype(jnp.bfloat16).astype(jnp.float32)
+        d_router_cols.append(jnp.sum(hidden * back, -1))
+        d_hidden = column * back
+        dg = (d_hidden * up_pre * sigma * (1.0 + gate_pre * (1.0 - sigma))).astype(jnp.bfloat16)
+        du = (d_hidden * swish).astype(jnp.bfloat16)
+        gh = (column * hidden).astype(jnp.bfloat16)
+        gh_list.append(gh)
+        dg_list.append(dg)
+        du_list.append(du)
+        grads.append(
+            (
+                jnp.einsum("td,tf->df", h_all, dg, preferred_element_type=jnp.float32).astype(jnp.bfloat16),
+                jnp.einsum("td,tf->df", h_all, du, preferred_element_type=jnp.float32).astype(jnp.bfloat16),
+                jnp.einsum("tf,td->fd", gh, cot_all, preferred_element_type=jnp.float32).astype(jnp.bfloat16),
+            )
+        )
+    gh_all, dg_all, du_all = (jnp.concatenate(v, 1) for v in (gh_list, dg_list, du_list))
+    y_part = jnp.dot(gh_all, w_down.reshape(-1, width), preferred_element_type=jnp.float32).astype(jnp.bfloat16)
+    wg_t = jnp.transpose(w_gate, (1, 0, 2)).reshape(width, -1)
+    wu_t = jnp.transpose(w_up, (1, 0, 2)).reshape(width, -1)
+    dh_part = (
+        jnp.einsum("tf,df->td", dg_all, wg_t, preferred_element_type=jnp.float32)
+        + jnp.einsum("tf,df->td", du_all, wu_t, preferred_element_type=jnp.float32)
+    ).astype(jnp.bfloat16)
+    d_router_held = jnp.stack(d_router_cols, 1)
+    d_router_wide = lax.dynamic_update_slice_in_dim(
+        jnp.zeros((h_all.shape[0], experts_all), jnp.float32), d_router_held, holder * held, 1
+    )
+    d_router = chosen * lax.psum_scatter(d_router_wide, "ep", scatter_dimension=0, tiled=True)
+    dh_sum = lax.psum_scatter(dh_part, "ep", scatter_dimension=0, tiled=True)
+    moe_sum = lax.psum_scatter(y_part, "ep", scatter_dimension=0, tiled=True)
+    mixed = (resid + moe_sum.astype(jnp.float32)).astype(jnp.bfloat16)
     d_out = cotangent.astype(jnp.float32)
-    d_gates = jnp.einsum("tkd,td->tk", y_rows, cotangent, preferred_element_type=jnp.float32)
-    d_router = jnp.sum(choose * d_gates[:, :, None], 1)
     d_logits = (
         router_probs * (d_router - jnp.sum(router_probs * d_router, -1, keepdims=True))
     ).astype(jnp.bfloat16)
     grad_router = jnp.einsum("td,te->de", h_two, d_logits, preferred_element_type=jnp.float32)
     d_htwo = jnp.einsum("te,de->td", d_logits, w_router, preferred_element_type=jnp.float32)
-    d_y = (
-        (gates[:, :, None] * d_out[:, None, :])
-        .astype(jnp.bfloat16)
-        .reshape(token_count * TOPK, width)
-    )
-    d_send = pack_rows(d_y, target, experts_all, width)
-    d_recv = lax.all_to_all(d_send, "ep", split_axis=0, concat_axis=1, tiled=True)
-    d_rows_held, grad_gate, grad_up, grad_down = expert_backward(
-        recv_rows, w_gate, w_up, w_down, gate_pre, up_pre, hidden, d_recv
-    )
-    back_rows = lax.all_to_all(d_rows_held, "ep", split_axis=1, concat_axis=0, tiled=True)
-    d_htwo = d_htwo + jnp.sum(
-        unpack_rows(back_rows, target, token_count, width).astype(jnp.float32), 1
-    )
+    d_htwo = d_htwo + dh_sum.astype(jnp.float32)
+    grad_gate, grad_up, grad_down = (jnp.stack([g[i] for g in grads]) for i in range(3))
     d_resid_norm, grad_norm_ffn = norm_backward(d_htwo, normal_two, inverse_two, norm_ffn)
     d_resid = d_out + d_resid_norm
     d_branch = d_resid.astype(jnp.bfloat16)
@@ -295,13 +285,13 @@
     )
     full_gate, full_up, full_down = (
         lax.all_gather(share_gate.astype(jnp.bfloat16), "rep", axis=1, tiled=True).astype(
-            share_gate.dtype
+            jnp.float32
         ),
         lax.all_gather(share_up.astype(jnp.bfloat16), "rep", axis=1, tiled=True).astype(
-            share_up.dtype
+            jnp.float32
         ),
         lax.all_gather(share_down.astype(jnp.bfloat16), "rep", axis=2, tiled=True).astype(
-            share_down.dtype
+            jnp.float32
         ),
     )
     return (

time: 2790 us -> 1610 us (0.58)
  blocking collectives: 840 us -> 322 us
  waiting for transfers between devices: 1130 us -> 672 us
  local copies, waits for them, and re-layouts: 295 us -> 87.7 us
  matrix products: 339 us -> 382 us
    all_to_all x2 -> x0, waiting for transfers between devices: 793 us -> none  [the longest x1 403 us: per_device(): lax.all_to_all(y_buf, 'ep', split_axis=1, concat_axis=0, tiled=True)]
    all_to_all x2 -> x0, blocking collectives: 523 us -> none  [the longest x1 262 us: per_device(): lax.all_to_all(send_buf, 'ep', split_axis=0, concat_axis=1, tiled=True)]
    reduce_scatter x1, waiting for transfers between devices: 0.02 us -> 143 us  [per_device(): lax.psum_scatter(part_up, 'rep', scatter_dimension=1, tiled=True)]
    unnamed x12 -> x18, waiting for transfers between devices: 18.6 us -> 158 us
    all_gather x1, waiting for transfers between devices: 108 us -> 0.01 us  [per_device(): lax.all_gather(share_gate.astype(jnp.bfloat16), 'rep', axis=1, tiled=True)]
    all_gather x1, waiting for transfers between devices: 0.01 us -> 107 us  [per_device(): lax.all_gather(share_down.astype(jnp.bfloat16), 'rep', axis=2, tiled=True)]
    all_to_all x4 -> x0, local copies, waits for them, and re-layouts: 73.4 us -> none  [the longest x1 28.9 us: per_device(): lax.all_to_all(d_rows_held, 'ep', split_axis=1, concat_axis=0, tiled=True)]
    gather x2 -> x0, local copies, waits for them, and re-layouts: 72.3 us -> none  [unpack_rows(): return buffer.reshape(-1, width)[target].reshape(token_count, TOPK, width)]
  transfers between devices with their start and end apart: 13 -> 16, of which waited for: 10 -> 11; matrix products, arithmetic and copies ran while one was open for 14% -> 24% of each run, Pallas kernels for 0% -> 0%
where the time goes in v1:
time: 1610 us; the launch traced here: 1600 us
  waiting for transfers between devices  672 us (42%)
  matrix products  382 us (24%)
  blocking collectives  322 us (20%)
  other arithmetic  118 us (7%)
  local copies, waits for them, and re-layouts  87.7 us (5%)
  between operations  16.6 us (1%)
    psum x1, blocking collectives, per_device(): lax.psum((part_na, part_q, part_k, part_v, part_o, part_nf, part_r), 'rep')  310 us
    unnamed x18, waiting for transfers between devices  158 us
    reduce_scatter x1, waiting for transfers between devices, per_device(): lax.psum_scatter(part_up, 'rep', scatter_dimension=1, tiled=True)  143 us
    all_gather x1, waiting for transfers between devices, per_device(): lax.all_gather(share_down.astype(jnp.bfloat16), 'rep', axis=2, tiled=True)  107 us
    unnamed x251, local copies, waits for them, and re-layouts  82.6 us
    all_gather x1, waiting for transfers between devices, per_device(): lax.all_gather(share_up.astype(jnp.bfloat16), 'rep', axis=1, tiled=True)  69.8 us
    reduce_scatter x1, waiting for transfers between devices, per_device(): lax.psum_scatter(grad_query.astype(jnp.bfloat16), 'ep', scatter_dimension...  50.8 us
    reduce_scatter x1, waiting for transfers between devices, per_device(): lax.psum_scatter(grad_out.astype(jnp.bfloat16), 'ep', scatter_dimension=0...  50.6 us
  transfers between devices with their start and end apart: 16, of which 11 were waited for; matrix products, arithmetic and copies ran while one was open for 24% of the time, Pallas kernels for 0%

profile of v1, /device:TPU:0, one launch (start us, length us, event | category | flops | bytes accessed | tf_op | source)
XLA Modules:
  0.0 1600.0 jit_solution(1905756668507000208)
XLA Ops:
  29.2 11.4 fusion.3
  40.7 12.0 fusion.76
  59.8 48.4 %all-gather.6.cloned.1.call-done = bf16[2048,1536]{1,0:T(8,128)(2,1)} async-done(((bf16[512,1536]{1,0:T(8,128)(2,1)}), bf16[2048,1536]{1,0:T(8,128)(2,1)}) %all-gather.6.cloned.1.call-update) | async-done | bytes 6291472 | tf_op jit(solution)/shard_map/all_gather | solution.py:152
  166.7 12.4 fusion.15
  293.0 21.8 %fusion.159 = f32[2048,1536]{1,0:T(8,128)} fusion(bf16[2048,2560]{0,1:T(8,128)(2,1)} %get-tuple-element.126, bf16[1536,2560]{0,1:T(8,128)(2,1)S(1)} %bitcast.298), kind=kOutput, calls=%fused_computation.266 | convolution fusion | flops 16106127360 | bytes 30932992 | tf_op jit(solution)/shard_map/tf,df->td/dot_general | solution.py:189
  314.9 21.4 %add_convert_fusion = bf16[2048,1536]{1,0:T(8,128)(2,1)} fusion(f32[2048,1536]{1,0:T(8,128)} %fusion.159, bf16[2048,2560]{0,1:T(8,128)(2,1)S(1)} %copy-done.66, bf16[1536,2560]{0,1:T(8,128)(2,1)S(1)} %bitcast.295), kind=kOutput, calls=%fused_computation.13 | convolution fusion | flops 16112418816 | bytes 37224448 | tf_op jit(solution)/shard_map/tf,df->td/dot_general | solution.py:190
  336.3 22.3 %convolution_convert_fusion.2 = bf16[2048,1536]{1,0:T(8,128)(2,1)} fusion(bf16[2048,2560]{0,1:T(8,128)(2,1)} %get-tuple-element.152, bf16[2560,1536]{1,0:T(8,128)(2,1)} %bitcast.331), kind=kOutput, calls=%fused_computation.18 | convolution fusion | flops 16109273088 | bytes 24641536 | tf_op jit(solution)/shard_map/dot_general | solution.py:185
  449.0 15.5 copy.79
  464.6 13.7 copy.82
  502.0 22.2 %fusion = (f32[8,3,512]{2,1,0:T(4,128)S(1)}, f32[8,512,512,3]{2,1,3,0:T(8,128)}) fusion(f32[8,3,512]{2,1,0:T(4,128)S(1)} %log_add_fusion, f32[8,512,512,3]{2,1,3,0:T(8,128)} %get-tuple-element.160, pred[512,512]{0,1:T(8,128)(4,1)S(1)} %copy-done.10, bf16[512,8,64,1]{0,2,3,1:T(8,128)(2,1)} %bitcast.313, bf16[512,8,3,64]{0,3,2,1:T(8,128)(2,1)S(1)} %bitcast.299), kind=kOutput, calls=%fused_computation.2 | convolution fusion | flops 836751360 | bytes 52789248 | tf_op jit(solution)/shard_map/while/body/eval_jaxpr/qhgd,khd->hgqk/dot_general | solution.py:86
  524.2 23.1 %fusion.2 = bf16[8,3,512,512]{2,3,1,0:T(8,128)(2,1)} fusion(f32[8,512,512,3]{2,1,3,0:T(8,128)} %get-tuple-element.172, f32[8,3,512]{2,1,0:T(4,128)S(1)} %get-tuple-element.171, f32[8,3,512]{2,1,0:T(4,128)S(1)} %log_add_fusion, f32[8,512,512,3]{2,1,3,0:T(8,128)} %get-tuple-element.160, pred[512,512]{0,1:T(8,128)(4,1)S(1)} %copy-done.10), kind=kLoop, calls=%fused_computation.4 | loop fusion | flops 37748736 | bytes 63275008 | tf_op jit(solution)/shard_map/while/body/eval_jaxpr/convert_element_type | solution.py:88
  559.6 12.2 fusion.127
  599.9 143.3 %reduce-scatter.32.cloned.1.call-done = bf16[5,192,512]{2,1,0:T(8,128)(2,1)} async-done(((bf16[5,1536,512]{2,1,0:T(8,128)(2,1)}), bf16[5,192,512]{2,1,0:T(8,128)(2,1)}) %reduce-scatter.32.cloned.1.call-update) | async-done | bytes 983056 | tf_op jit(solution)/shard_map/reduce_scatter | solution.py:283
  743.5 142.5 %reduce-scatter.36.cloned.1.call-done = bf16[192,2560]{1,0:T(8,128)(2,1)} async-done(((bf16[1536,2560]{1,0:T(8,128)(2,1)}), bf16[192,2560]{1,0:T(8,128)(2,1)}) %reduce-scatter.36.cloned.1.call-update) | async-done | bytes 983056
  893.4 15.0 reduce-scatter.34.cloned.1.call-done
  939.6 30.9 %reduce-scatter.26.cloned.1.call-done = bf16[384,512]{1,0:T(8,128)(2,1)} async-done(((bf16[1536,512]{1,0:T(8,128)(2,1)}), bf16[384,512]{1,0:T(8,128)(2,1)}) %reduce-scatter.26.cloned.1.call-update) | async-done | bytes 393232 | tf_op jit(solution)/shard_map/reduce_scatter | solution.py:264
  970.5 50.8 %reduce-scatter.22.cloned.1.call-done = bf16[384,1536]{1,0:T(8,128)(2,1)} async-done(((bf16[1536,1536]{1,0:T(8,128)(2,1)}), bf16[384,1536]{1,0:T(8,128)(2,1)}) %reduce-scatter.22.cloned.1.call-update) | async-done | bytes 1179664 | tf_op jit(solution)/shard_map/reduce_scatter | solution.py:258
  1021.3 50.6 %reduce-scatter.28.cloned.1.call-done = bf16[384,1536]{1,0:T(8,128)(2,1)} async-done(((bf16[1536,1536]{1,0:T(8,128)(2,1)}), bf16[384,1536]{1,0:T(8,128)(2,1)}) %reduce-scatter.28.cloned.1.call-update) | async-done | bytes 1179664 | tf_op jit(solution)/shard_map/reduce_scatter | solution.py:267
  1071.9 310.1 %all-reduce.5 = (f32[384]{0:T(512)}, f32[384,1536]{1,0:T(8,128)}, f32[384,512]{1,0:T(8,128)}, f32[384,512]{1,0:T(8,128)}, f32[384,1536]{1,0:T(8,128)}, /*index=5*/f32[384]{0:T(512)}, f32[384,20]{0,1:T(8,128)}) all-reduce(f32[384]{0:T(512)S(1)} %dynamic-slice_convert_fusion.1, ...), channel_id=1, replica_groups=mesh['rep'=8,'ep'=4] {'rep'}, use_global_device_ids=true, to_apply=%region_21.22 | all-reduce | flops 1581312 | bytes 9489408 | tf_op jit(solution)/shard_map/psum | solution.py:278
  1382.0 11.2 convert_element_type.368
  1393.2 69.8 %all-gather.12.cloned.1.call-done = bf16[5,1536,512]{2,1,0:T(8,128)(2,1)} async-done(((bf16[5,192,512]{2,1,0:T(8,128)(2,1)}), bf16[5,1536,512]{2,1,0:T(8,128)(2,1)}) %all-gather.12.cloned.1.call-update) | async-done | bytes 7864336 | tf_op jit(solution)/shard_map/all_gather | solution.py:290
  1463.0 11.6 convert_element_type.374
  1474.6 107.0 %all-gather.14.cloned.1.call-done = bf16[5,512,1536]{1,2,0:T(8,128)(2,1)} async-done(((bf16[5,512,192]{1,2,0:T(8,128)(2,1)}), bf16[5,512,1536]{1,2,0:T(8,128)(2,1)}) %all-gather.14.cloned.1.call-update) | async-done | bytes 7864336 | tf_op jit(solution)/shard_map/all_gather | solution.py:293
  1581.6 11.4 copy.67
  (383 shorter events, 392.8 us)
Async XLA Ops:
  7.2 101.0 %all-gather.6.cloned.1.call-start = ((), (), s32[]{:S(2)}) async-start(), calls=%async_computation.11 | async-start | bytes 7864320 | tf_op jit(solution)/shard_map/all_gather | solution.py:152
  10.6 30.0 %copy-start.9 = (pred[512,512]{0,1:T(8,128)(4,1)}, pred[512,512]{0,1:T(8,128)(4,1)S(1)}, u32[]{:S(2)}) copy-start(pred[512,512]{0,1:T(8,128)(4,1)S(1)} %broadcast_compare_fusion) | copy-start | bytes 786436
  13.3 27.4 %copy-start.63 = (bf16[512,512]{0,1:T(8,128)(2,1)}, bf16[512,512]{0,1:T(8,128)(2,1)S(1)}, u32[]{:S(2)}) copy-start(bf16[512,512]{0,1:T(8,128)(2,1)S(1)} %convolution_convert_fusion.22) | copy-start | bytes 1572868
  29.2 23.5 %slice-start.16 = ((s8[4718592]{0:T(1024)(128)(4,1)}), s8[4194304]{0:T(1024)(128)(4,1)S(1)}, s32[]{:S(2)}) async-start(s8[4718592]{0:T(1024)(128)(4,1)} %bitcast.340), calls=%async_computation.43 | async-start | bytes 8388608
  59.0 107.7 %all-gather.8.cloned.1.call-start = ((), (), s32[]{:S(2)}) async-start(), calls=%async_computation.13 | async-start | bytes 7864320 | tf_op jit(solution)/shard_map/all_gather | solution.py:121
  59.7 179.1 %reduce-scatter.18.cloned.1.call-start = ((), (), s32[]{:S(2)}) async-start(), calls=%async_computation.14 | async-start | bytes 245760 | tf_op jit(solution)/shard_map/reduce_scatter | solution.py:196
  216.7 264.6 %reduce-scatter.20.cloned.1.call-start = ((), (), s32[]{:S(2)}) async-start(), calls=%async_computation.15 | async-start | bytes 7864320 | tf_op jit(solution)/shard_map/reduce_scatter | solution.py:197
  246.5 28.5 %copy-start.82 = (f32[2048,1]{0,1:T(1,128)}, f32[2048,1]{0,1:T(1,128)S(1)}, u32[]{:S(2)}) copy-start(f32[2048,1]{0,1:T(1,128)S(1)} %get-tuple-element.147) | copy-start | bytes 24580
  246.5 37.1 %copy-start.80 = (f32[2048,1]{0,1:T(1,128)}, f32[2048,1]{0,1:T(1,128)S(1)}, u32[]{:S(2)}) copy-start(f32[2048,1]{0,1:T(1,128)S(1)} %get-tuple-element.146) | copy-start | bytes 24580
  284.6 30.2 %slice-start.4 = ((s8[7864320]{0:T(1024)(128)(4,1)}), s8[4194304]{0:T(1024)(128)(4,1)S(1)}, s32[]{:S(2)}) async-start(s8[7864320]{0:T(1024)(128)(4,1)} %bitcast.293), calls=%async_computation.31 | async-start | bytes 8388608
  336.3 150.3 %reduce-scatter.16.cloned.1.call-start = ((), (), s32[]{:S(2)}) async-start(), calls=%async_computation.12 | async-start | bytes 7864320 | tf_op jit(solution)/shard_map/reduce_scatter | solution.py:198
  358.7 241.1 %reduce-scatter.30.cloned.1.call-start = ((), (), s32[]{:S(2)}) async-start(), calls=%async_computation.20 | async-start | bytes 8847360 | tf_op jit(solution)/shard_map/reduce_scatter | solution.py:282
  388.6 354.6 %reduce-scatter.32.cloned.1.call-start = ((), (), s32[]{:S(2)}) async-start(), calls=%async_computation.22 | async-start | bytes 8847360 | tf_op jit(solution)/shard_map/reduce_scatter | solution.py:283
  418.4 467.5 %reduce-scatter.36.cloned.1.call-start = ((), (), s32[]{:S(2)}) async-start(), calls=%async_computation.26 | async-start | bytes 8847360
  478.3 430.1 %reduce-scatter.34.cloned.1.call-start = ((), (), s32[]{:S(2)}) async-start(), calls=%async_computation.25 | async-start | bytes 491520
  479.1 45.0 %copy-start.62 = (f32[8,3,512]{2,1,0:T(4,128)}, f32[8,3,512]{2,1,0:T(4,128)S(1)}, u32[]{:S(2)}) copy-start(f32[8,3,512]{2,1,0:T(4,128)S(1)} %log_add_fusion) | copy-start | bytes 147460
  481.1 458.5 %reduce-scatter.24.cloned.1.call-start = ((), (), s32[]{:S(2)}) async-start(), calls=%async_computation.17 | async-start | bytes 1966080 | tf_op jit(solution)/shard_map/reduce_scatter | solution.py:261
  559.3 411.1 %reduce-scatter.26.cloned.1.call-start = ((), (), s32[]{:S(2)}) async-start(), calls=%async_computation.18 | async-start | bytes 1966080 | tf_op jit(solution)/shard_map/reduce_scatter | solution.py:264
  574.9 446.4 %reduce-scatter.22.cloned.1.call-start = ((), (), s32[]{:S(2)}) async-start(), calls=%async_computation.16 | async-start | bytes 5898240 | tf_op jit(solution)/shard_map/reduce_scatter | solution.py:258
  588.4 483.5 %reduce-scatter.28.cloned.1.call-start = ((), (), s32[]{:S(2)}) async-start(), calls=%async_computation.19 | async-start | bytes 5898240 | tf_op jit(solution)/shard_map/reduce_scatter | solution.py:267
  595.8 296.4 %copy-start.102 = (u32[32]{0:T(128)S(1)}, u32[32]{0:T(128)}, u32[]{:S(2)}) copy-start(u32[32]{0:T(128)} %constant.122) | copy-start | bytes 388
  595.8 786.2 %all-gather.10.cloned.1.call-start = ((), (), s32[]{:S(2)}) async-start(), calls=%async_computation.21 | async-start | bytes 8847360 | tf_op jit(solution)/shard_map/all_gather | solution.py:287
  599.9 863.1 %all-gather.12.cloned.1.call-start = ((), (), s32[]{:S(2)}) async-start(), calls=%async_computation.23 | async-start | bytes 8847360 | tf_op jit(solution)/shard_map/all_gather | solution.py:290
  743.2 838.4 %all-gather.14.cloned.1.call-start = ((), (), s32[]{:S(2)}) async-start(), calls=%async_computation.24 | async-start | bytes 8847360 | tf_op jit(solution)/shard_map/all_gather | solution.py:293
  (113 other events, 953.2 us)
Sparse Core Ops, SparseCore 0:
  59.1 49.0 all-gather.5
  109.7 46.3 all-gather.7
  216.9 19.7 reduce-scatter.17
  336.4 58.3 reduce-scatter.19
  397.4 58.3 reduce-scatter.15
  459.8 139.9 reduce-scatter.29
  604.0 139.0 reduce-scatter.31
  746.8 139.0 reduce-scatter.35
  888.5 19.8 reduce-scatter.33
  911.4 28.1 reduce-scatter.23
  942.3 28.1 reduce-scatter.25
  973.4 47.8 reduce-scatter.21
  1024.0 47.8 reduce-scatter.27
  1073.9 246.2 all-gather.9
  1322.3 140.6 all-gather.11
  1465.0 116.5 all-gather.13

commit v2 on v1

--- a/solution.py
+++ b/solution.py
@@ -1,8 +1,11 @@
+import functools
 import math
 
 import jax
 import jax.numpy as jnp
 from jax import lax
+from jax.experimental import pallas as pl
+from jax.experimental.pallas import tpu as pltpu
 from jax.sharding import PartitionSpec as P
 
 QUERY_HEADS = 24
@@ -11,6 +14,7 @@
 TOPK = 8
 SEQUENCE_TOKENS = 512
 BLOCK = 256
+EARLY = 2
 
 
 epsilon = 1e-06
@@ -95,6 +99,258 @@
     )
     d_values = jnp.einsum("hgqk,qhgd->khd", probs_bf, d_mix, preferred_element_type=jnp.float32)
     return (d_queries, d_keys, d_values)
+
+
+SLOTS = 3
+
+
+def ring_device(place, count):
+    back = place // (count // 2)
+    return (1 - back) * 2 * place + back * (2 * (count - 1 - place) + 1)
+
+
+def ring_kernel(count, shapes, *refs):
+    total = len(shapes)
+    sources, sums = refs[:total], refs[total : 2 * total]
+    held, terms = refs[2 * total : 3 * total], refs[3 * total : 4 * total]
+    arrived, sent, loaded, stored, credit = refs[4 * total :]
+    here = lax.axis_index("rep")
+    odd = here % 2
+    rank = here // 2 + odd * (count - 1 - 2 * (here // 2))
+    after = ring_device((rank + 1) % count, count)
+    before = ring_device((rank + count - 1) % count, count)
+    hops = 2 * (count - 1)
+
+    barrier = pltpu.get_barrier_semaphore()
+    for neighbour in (before, after):
+        pl.semaphore_signal(barrier, inc=1, device_id={"rep": neighbour})
+    pl.semaphore_wait(barrier, 2)
+
+    streams = [(index, way) for index in range(total) for way in (0, 1)]
+
+    def columns(index, way):
+        half = shapes[index][1] // 2
+        return pl.ds(way * half, half)
+
+    def send(index, way, hop):
+        stream = 2 * index + way
+        source = (hop + SLOTS - 1) % SLOTS
+        slot = hop % SLOTS
+        return pltpu.make_async_remote_copy(
+            src_ref=held[index].at[way, source],
+            dst_ref=held[index].at[way, slot],
+            send_sem=sent.at[stream, slot],
+            recv_sem=arrived.at[stream, slot],
+            device_id={"rep": before if way else after},
+        )
+
+    def load(index, way, hop):
+        step = hop + 2
+        chunk = (rank + step) % count if way else (rank + 2 * count - step) % count
+        return pltpu.make_async_copy(
+            sources[index].at[chunk, :, columns(index, way)],
+            terms[index].at[way, hop % 2],
+            loaded.at[2 * index + way, hop % 2],
+        )
+
+    def first(index, way):
+        chunk = (rank + 1) % count if way else (rank + count - 1) % count
+        return pltpu.make_async_copy(
+            sources[index].at[chunk, :, columns(index, way)],
+            held[index].at[way, SLOTS - 1],
+            stored.at[2 * index + way, SLOTS - 1],
+        )
+
+    def store(index, way, hop):
+        step = hop - (count - 2)
+        chunk = (rank + step) % count if way else (rank + count - step) % count
+        return pltpu.make_async_copy(
+            held[index].at[way, hop % SLOTS],
+            sums[index].at[chunk, :, columns(index, way)],
+            stored.at[2 * index + way, hop % SLOTS],
+        )
+
+    def release(index, way):
+        pl.semaphore_signal(
+            credit.at[2 * index + way], inc=1, device_id={"rep": after if way else before}
+        )
+
+    for index, way in streams:
+        first(index, way).start()
+    for index, way in streams:
+        load(index, way, 0).start()
+        load(index, way, 1).start()
+    for index, way in streams:
+        first(index, way).wait()
+        send(index, way, 0).start()
+
+    def take(index, way, hop):
+        send(index, way, hop).wait_recv()
+        send(index, way, hop).wait_send()
+
+    def pass_on(index, way, hop):
+        @pl.when(hop + 1 >= 2)
+        def _():
+            pl.semaphore_wait(credit.at[2 * index + way], 1)
+
+        send(index, way, hop + 1).start()
+
+    def add_step(hop, carry):
+        for index, way in streams:
+            take(index, way, hop)
+
+            @pl.when(hop <= hops - 3)
+            def _():
+                release(index, way)
+
+            load(index, way, hop).wait()
+            slot = hop % SLOTS
+            held[index][way, slot] = (
+                held[index][way, slot].astype(jnp.float32)
+                + terms[index][way, hop % 2].astype(jnp.float32)
+            ).astype(jnp.bfloat16)
+            pass_on(index, way, hop)
+
+            @pl.when(hop + 2 <= count - 2)
+            def _():
+                load(index, way, hop + 2).start()
+
+            @pl.when(hop == count - 2)
+            def _():
+                store(index, way, hop).start()
+
+        return carry
+
+    def hand_step(hop, carry):
+        for index, way in streams:
+            take(index, way, hop)
+            store(index, way, hop - 1).wait()
+
+            @pl.when(hop <= hops - 3)
+            def _():
+                release(index, way)
+
+            @pl.when(hop + 1 < hops)
+            def _():
+                pass_on(index, way, hop)
+
+            store(index, way, hop).start()
+
+        return carry
+
+    lax.fori_loop(0, count - 1, add_step, 0)
+    lax.fori_loop(count - 1, hops, hand_step, 0)
+    for index, way in streams:
+        store(index, way, hops - 1).wait()
+
+
+def ring_sum(sources):
+    count = sources[0].shape[0]
+    shapes = [source.shape[1:] for source in sources]
+    total = len(shapes)
+    size = sum(source.size for source in sources)
+    halves = [(rows, columns // 2) for rows, columns in shapes]
+    return pl.pallas_call(
+        functools.partial(ring_kernel, count, shapes),
+        out_shape=[jax.ShapeDtypeStruct(source.shape, source.dtype) for source in sources],
+        in_specs=[pl.BlockSpec(memory_space=pl.ANY)] * total,
+        out_specs=[pl.BlockSpec(memory_space=pl.ANY)] * total,
+        scratch_shapes=[pltpu.VMEM((2, SLOTS) + half, jnp.bfloat16) for half in halves]
+        + [pltpu.VMEM((2, 2) + half, jnp.bfloat16) for half in halves]
+        + [
+            pltpu.SemaphoreType.DMA((2 * total, SLOTS)),
+            pltpu.SemaphoreType.DMA((2 * total, SLOTS)),
+            pltpu.SemaphoreType.DMA((2 * total, 2)),
+            pltpu.SemaphoreType.DMA((2 * total, SLOTS)),
+            pltpu.SemaphoreType.REGULAR((2 * total,)),
+        ],
+        compiler_params=pltpu.CompilerParams(
+            collective_id=0, has_side_effects=True, vmem_limit_bytes=48 * 2**20
+        ),
+        cost_estimate=pl.CostEstimate(flops=2 * size, bytes_accessed=8 * size, transcendentals=0),
+        name="ring_sum",
+    )(*sources)
+
+
+def finish_kernel(*refs):
+    units, (gate, up, down) = refs[:-3], refs[-3:]
+    for index, unit in enumerate(units):
+
+        @pl.when(pl.program_id(0) == index)
+        def _():
+            rows = unit.shape[1] // 3
+            cut = rows * unit.shape[2] // down.shape[2]
+            columns = unit.shape[2]
+            for k in range(unit.shape[0]):
+                gate[0, k * rows : (k + 1) * rows] = unit[k, :rows].astype(jnp.float32)
+                up[0, k * rows : (k + 1) * rows] = unit[k, rows : 2 * rows].astype(jnp.float32)
+                for j in range(down.shape[2] // columns):
+                    start = 2 * rows + j * cut
+                    down[0, k * cut : (k + 1) * cut, j * columns : (j + 1) * columns] = unit[
+                        k, start : start + cut
+                    ].astype(jnp.float32)
+
+
+def finish(units, width):
+    experts = len(units)
+    count, rows3, columns = units[0].shape
+    rows = rows3 // 3
+    pair = 2
+    last = count // pair - 1
+
+    def place(index):
+        def chunk(e, c):
+            return (jnp.where(e == index, c, jnp.where(e < index, 0, last)), 0, 0)
+
+        return chunk
+
+    return pl.pallas_call(
+        finish_kernel,
+        grid=(experts, count // pair),
+        in_specs=[pl.BlockSpec((pair, rows3, columns), place(index)) for index in range(experts)],
+        out_specs=[
+            pl.BlockSpec((1, pair * rows, columns), lambda e, c: (e, c, 0)),
+            pl.BlockSpec((1, pair * rows, columns), lambda e, c: (e, c, 0)),
+            pl.BlockSpec((1, pair * rows * columns // width, width), lambda e, c: (e, c, 0)),
+        ],
+        out_shape=[
+            jax.ShapeDtypeStruct((experts, width, columns), jnp.float32),
+            jax.ShapeDtypeStruct((experts, width, columns), jnp.float32),
+            jax.ShapeDtypeStruct((experts, columns, width), jnp.float32),
+        ],
+        name="finish",
+        compiler_params=pltpu.CompilerParams(vmem_limit_bytes=48 * 2**20),
+    )(*units)
+
+
+def swap_core(value):
+    return lax.ppermute(value, "ep", [(0, 1), (1, 0), (2, 3), (3, 2)])
+
+
+def swap_chip(value):
+    return lax.ppermute(value, "ep", [(0, 2), (2, 0), (1, 3), (3, 1)])
+
+
+def gather_group(block):
+    far = swap_chip(block)
+    return (block, swap_core(block), far, swap_core(far))
+
+
+def in_order(blocks, place):
+    stacked = jnp.stack(blocks)
+    return jnp.concatenate(
+        [lax.dynamic_index_in_dim(stacked, place ^ k, 0, keepdims=False) for k in range(len(blocks))], 0
+    )
+
+
+def add_bf(a, b):
+    return (a.astype(jnp.float32) + b.astype(jnp.float32)).astype(jnp.bfloat16)
+
+
+def scatter_group(blocks):
+    near = add_bf(blocks[0], swap_core(blocks[1]))
+    far = add_bf(blocks[2], swap_core(blocks[3]))
+    return near.astype(jnp.float32) + swap_chip(far).astype(jnp.float32)
 
 
 def per_device(
@@ -118,7 +374,8 @@
     query_groups = QUERY_HEADS // KEY_VALUE_HEADS
     sequence_total = token_count // SEQUENCE_TOKENS
     x_float = tokens.astype(jnp.float32)
-    cot_all = lax.all_gather(cotangent, "ep", axis=0, tiled=True)
+    cot_blocks = gather_group(cotangent)
+    cot_all = jnp.concatenate(cot_blocks, 0)
     hidden_first, normal_one, inverse_one = norm_forward(x_float, norm_attn)
     query_unrotated = jnp.dot(hidden_first, w_query, preferred_element_type=jnp.float32)
     key_unrotated = jnp.dot(hidden_first, key_projection, preferred_element_type=jnp.float32)
@@ -149,14 +406,13 @@
     expert_ids = jnp.arange(experts_all)
     chosen = jnp.max((routes[:, :, None] == jnp.arange(experts_all)[None, None, :]).astype(jnp.float32), 1)
     combine = chosen * router_probs
-    h_all = lax.all_gather(h_two, "ep", axis=0, tiled=True)
-    combine_all = lax.all_gather(combine, "ep", axis=0, tiled=True)
+    h_all = jnp.concatenate(gather_group(h_two), 0)
+    combine_all = jnp.concatenate(gather_group(combine), 0)
     holder = lax.axis_index("ep")
     held = w_gate.shape[0]
+    replicas = lax.axis_size("rep")
     weight = lax.dynamic_slice_in_dim(combine_all, holder * held, held, 1)
-    y_part = jnp.zeros((h_all.shape[0], width), jnp.float32)
-    dh_part = jnp.zeros((h_all.shape[0], width), jnp.float32)
-    d_router_cols, grads = [], []
+    d_router_cols, units = [], []
     gh_list, dg_list, du_list = [], [], []
     for e in range(held):
         gate_pre = jnp.dot(h_all, w_gate[e], preferred_element_type=jnp.float32)
@@ -174,37 +430,57 @@
         gh_list.append(gh)
         dg_list.append(dg)
         du_list.append(du)
-        grads.append(
-            (
-                jnp.einsum("td,tf->df", h_all, dg, preferred_element_type=jnp.float32).astype(jnp.bfloat16),
-                jnp.einsum("td,tf->df", h_all, du, preferred_element_type=jnp.float32).astype(jnp.bfloat16),
-                jnp.einsum("tf,td->fd", gh, cot_all, preferred_element_type=jnp.float32).astype(jnp.bfloat16),
-            )
-        )
-    gh_all, dg_all, du_all = (jnp.concatenate(v, 1) for v in (gh_list, dg_list, du_list))
-    y_part = jnp.dot(gh_all, w_down.reshape(-1, width), preferred_element_type=jnp.float32).astype(jnp.bfloat16)
-    wg_t = jnp.transpose(w_gate, (1, 0, 2)).reshape(width, -1)
-    wu_t = jnp.transpose(w_up, (1, 0, 2)).reshape(width, -1)
-    dh_part = (
-        jnp.einsum("tf,df->td", dg_all, wg_t, preferred_element_type=jnp.float32)
-        + jnp.einsum("tf,df->td", du_all, wu_t, preferred_element_type=jnp.float32)
+        gate_grad = jnp.einsum("td,tf->df", h_all, dg, preferred_element_type=jnp.float32)
+        up_grad = jnp.einsum("td,tf->df", h_all, du, preferred_element_type=jnp.float32)
+        down_grad = jnp.einsum("tf,td->fd", gh, cot_all, preferred_element_type=jnp.float32)
+        hidden_units = down_grad.shape[0]
+        rows = width // replicas
+        down_cut = down_grad.astype(jnp.bfloat16).reshape(replicas, hidden_units // replicas, width // hidden_units, hidden_units)
+        down_cut = jnp.transpose(down_cut, (0, 2, 1, 3)).reshape(replicas, rows, hidden_units)
+        unit = jnp.concatenate(
+            [
+                gate_grad.astype(jnp.bfloat16).reshape(replicas, rows, hidden_units),
+                up_grad.astype(jnp.bfloat16).reshape(replicas, rows, hidden_units),
+                down_cut,
+            ],
+            1,
+        )
+        h_all, cot_all, unit = lax.optimization_barrier((h_all, cot_all, unit))
+        units.append(unit)
+    totals = [
+        lax.all_gather(
+            lax.psum_scatter(unit, "rep", scatter_dimension=0, tiled=True), "rep", axis=0, tiled=True
+        )
+        for unit in units[:EARLY]
+    ]
+
+    def blocks_of(value):
+        return [value[k * token_count : (k + 1) * token_count] for k in range(4)]
+
+    dh_part = sum(
+        jnp.einsum("tf,df->td", dg_list[e], w_gate[e], preferred_element_type=jnp.float32)
+        + jnp.einsum("tf,df->td", du_list[e], w_up[e], preferred_element_type=jnp.float32)
+        for e in range(held)
+    ).astype(jnp.bfloat16)
+    y_part = sum(
+        jnp.dot(gh_list[e], w_down[e], preferred_element_type=jnp.float32) for e in range(held)
     ).astype(jnp.bfloat16)
     d_router_held = jnp.stack(d_router_cols, 1)
     d_router_wide = lax.dynamic_update_slice_in_dim(
         jnp.zeros((h_all.shape[0], experts_all), jnp.float32), d_router_held, holder * held, 1
     )
-    d_router = chosen * lax.psum_scatter(d_router_wide, "ep", scatter_dimension=0, tiled=True)
-    dh_sum = lax.psum_scatter(dh_part, "ep", scatter_dimension=0, tiled=True)
-    moe_sum = lax.psum_scatter(y_part, "ep", scatter_dimension=0, tiled=True)
-    mixed = (resid + moe_sum.astype(jnp.float32)).astype(jnp.bfloat16)
+    router_blocks = blocks_of(d_router_wide)
+    d_router = router_blocks[0] + swap_core(router_blocks[1])
+    d_router = chosen * (d_router + swap_chip(router_blocks[2] + swap_core(router_blocks[3])))
+    dh_sum = scatter_group(blocks_of(dh_part))
+    mixed = (resid + scatter_group(blocks_of(y_part))).astype(jnp.bfloat16)
     d_out = cotangent.astype(jnp.float32)
     d_logits = (
         router_probs * (d_router - jnp.sum(router_probs * d_router, -1, keepdims=True))
     ).astype(jnp.bfloat16)
     grad_router = jnp.einsum("td,te->de", h_two, d_logits, preferred_element_type=jnp.float32)
     d_htwo = jnp.einsum("te,de->td", d_logits, w_router, preferred_element_type=jnp.float32)
-    d_htwo = d_htwo + dh_sum.astype(jnp.float32)
-    grad_gate, grad_up, grad_down = (jnp.stack([g[i] for g in grads]) for i in range(3))
+    d_htwo = d_htwo + dh_sum
     d_resid_norm, grad_norm_ffn = norm_backward(d_htwo, normal_two, inverse_two, norm_ffn)
     d_resid = d_out + d_resid_norm
     d_branch = d_resid.astype(jnp.bfloat16)
@@ -251,49 +527,41 @@
     )
     d_x_norm, grad_norm_attn = norm_backward(d_hone, normal_one, inverse_one, norm_attn)
     d_input = d_resid + d_x_norm
-    part_na, part_q, part_k, part_v, part_o, part_nf, part_r = (
-        lax.psum_scatter(
-            grad_norm_attn.astype(jnp.bfloat16), "ep", scatter_dimension=0, tiled=True
-        ).astype(jnp.float32),
-        lax.psum_scatter(
-            grad_query.astype(jnp.bfloat16), "ep", scatter_dimension=0, tiled=True
-        ).astype(jnp.float32),
-        lax.psum_scatter(
-            grad_key.astype(jnp.bfloat16), "ep", scatter_dimension=0, tiled=True
-        ).astype(jnp.float32),
-        lax.psum_scatter(
-            grad_value.astype(jnp.bfloat16), "ep", scatter_dimension=0, tiled=True
-        ).astype(jnp.float32),
-        lax.psum_scatter(
-            grad_out.astype(jnp.bfloat16), "ep", scatter_dimension=0, tiled=True
-        ).astype(jnp.float32),
-        lax.psum_scatter(
-            grad_norm_ffn.astype(jnp.bfloat16), "ep", scatter_dimension=0, tiled=True
-        ).astype(jnp.float32),
-        lax.psum_scatter(
-            grad_router.astype(jnp.bfloat16), "ep", scatter_dimension=0, tiled=True
-        ).astype(jnp.float32),
-    )
-    part_gate, part_up, part_down = (grad_gate, grad_up, grad_down)
-    sum_na, sum_q, sum_k, sum_v, sum_o, sum_nf, sum_r = lax.psum(
-        (part_na, part_q, part_k, part_v, part_o, part_nf, part_r), "rep"
-    )
-    share_gate, share_up, share_down = (
-        lax.psum_scatter(part_gate, "rep", scatter_dimension=1, tiled=True),
-        lax.psum_scatter(part_up, "rep", scatter_dimension=1, tiled=True),
-        lax.psum_scatter(part_down, "rep", scatter_dimension=2, tiled=True),
-    )
-    full_gate, full_up, full_down = (
-        lax.all_gather(share_gate.astype(jnp.bfloat16), "rep", axis=1, tiled=True).astype(
-            jnp.float32
-        ),
-        lax.all_gather(share_up.astype(jnp.bfloat16), "rep", axis=1, tiled=True).astype(
-            jnp.float32
-        ),
-        lax.all_gather(share_down.astype(jnp.bfloat16), "rep", axis=2, tiled=True).astype(
-            jnp.float32
-        ),
-    )
+    def group_part(value):
+        quarter = value.shape[0] // 4
+        cut = value.reshape(4, quarter, value.shape[1])
+        blocks = [lax.dynamic_index_in_dim(cut, holder ^ k, 0, keepdims=False) for k in range(4)]
+        return scatter_group(blocks).astype(jnp.bfloat16)
+
+    def in_chunks(parts):
+        wide = jnp.concatenate(parts, 1)
+        chunk_rows = -(-wide.shape[0] // (8 * replicas)) * 8
+        wide = jnp.pad(wide, ((0, chunk_rows * replicas - wide.shape[0]), (0, 0)))
+        return wide.reshape(replicas, chunk_rows, wide.shape[1])
+
+    def out_of_chunks(total):
+        return total.reshape(-1, total.shape[2])[: width // 4].astype(jnp.float32)
+
+    lanes = 128
+    filler = jnp.zeros((width, lanes - experts_all - 1), jnp.float32)
+    part_o = group_part(
+        jnp.concatenate([grad_out, grad_router, grad_norm_ffn[:, None], filler], 1).astype(jnp.bfloat16)
+    )
+    part_qkv = group_part(
+        jnp.concatenate(
+            [grad_query, grad_key, grad_value, grad_norm_attn[:, None], jnp.zeros((width, lanes - 1))], 1
+        ).astype(jnp.bfloat16)
+    )
+    dense = in_chunks([part_o, part_qkv])
+    *late, dense = ring_sum([*units[EARLY:], dense])
+    dense = out_of_chunks(dense)
+    key_width = grad_key.shape[1]
+    edges = []
+    for part in (width, experts_all, 1, lanes - experts_all - 1, width, key_width, key_width, 1):
+        edges.append(part + (edges[-1] if edges else 0))
+    sum_o, sum_r, sum_nf, _, sum_q, sum_k, sum_v, sum_na, _ = jnp.split(dense, edges, 1)
+    sum_nf, sum_na = (sum_nf[:, 0], sum_na[:, 0])
+    full_gate, full_up, full_down = finish(totals + late, width)
     return (
         mixed,
         d_input,

time: 1610 us -> 1210 us (0.75)
  waiting for transfers between devices: 672 us -> 187 us
  Pallas kernels: 0 us -> 360 us
  blocking collectives: 322 us -> 0 us
  matrix products: 382 us -> 442 us
  other arithmetic: 118 us -> 80.8 us
  local copies, waits for them, and re-layouts: 87.7 us -> 106 us
    pallas_call x0 -> x2, Pallas kernels: none -> 360 us  [the longest x1 334 us: ring_sum(): pl.pallas_call(functools.partial(ring_kernel, count, shapes), out_shape=[...]
    psum x1 -> x0, blocking collectives: 310 us -> none  [per_device(): lax.psum((part_na, part_q, part_k, part_v, part_o, part_nf, part_r), 'rep')]
    reduce_scatter x9 -> x2, waiting for transfers between devices: 289 us -> 0.01 us  [per_device(): lax.psum_scatter(unit, 'rep', scatter_dimension=0, tiled=True)]
    all_gather x5 -> x2, waiting for transfers between devices: 225 us -> 0.01 us  [per_device(): lax.all_gather(lax.psum_scatter(unit, 'rep', scatter_dimension=0, tiled=T...]
    ppermute x0 -> x24, waiting for transfers between devices: none -> 187 us  [the longest x8 184 us: swap_chip(): return lax.ppermute(value, 'ep', [(0, 2), (2, 0), (1, 3), (3, 1)])]
    unnamed x18 -> x4, waiting for transfers between devices: 158 us -> 0.07 us
    dot_general x3 -> x15, matrix products: 65.6 us -> 146 us  [the longest x5 62.9 us: per_device(): jnp.einsum('tf,df->td', du_list[e], w_up[e], preferred_element_type=jnp.f...]
    unnamed x251 -> x290, local copies, waits for them, and re-layouts: 82.6 us -> 29.2 us
  transfers between devices with their start and end apart: 16 -> 28, of which waited for: 11 -> 7; matrix products, arithmetic and copies ran while one was open for 24% -> 28% of each run, Pallas kernels for 0% -> 28%
where the time goes in v2:
time: 1210 us
  matrix products  442 us (37%)
  Pallas kernels  360 us (30%)
  waiting for transfers between devices  187 us (15%)
  local copies, waits for them, and re-layouts  106 us (9%)
  other arithmetic  80.8 us (7%)
  between operations  16.3 us (1%)
  starting transfers between devices  14.5 us (1%)
    pallas_call x1, Pallas kernels, ring_sum(): pl.pallas_call(functools.partial(ring_kernel, count, shapes), out_shape=[...  334 us
    ppermute x8, waiting for transfers between devices, swap_chip(): return lax.ppermute(value, 'ep', [(0, 2), (2, 0), (1, 3), (3, 1)])  184 us
    dot_general x5, matrix products, per_device(): jnp.einsum('tf,df->td', du_list[e], w_up[e], preferred_element_type=jnp.f...  62.9 us
    dot_general x5, matrix products, per_device(): jnp.einsum('td,fd->tf', cot_all, w_down[e], preferred_element_type=jnp.fl...  47.5 us
    dot_general x5, matrix products, per_device(): jnp.dot(gh_list[e], w_down[e], preferred_element_type=jnp.float32)  47.5 us
    dot_general x5, matrix products, per_device(): jnp.einsum('tf,df->td', dg_list[e], w_gate[e], preferred_element_type=jnp...  35.2 us
    dot_general x5, matrix products, per_device(): jnp.einsum('td,tf->df', h_all, dg, preferred_element_type=jnp.float32)  33.4 us
    dot_general x5, matrix products, per_device(): up_pre = jnp.dot(h_all, w_up[e], preferred_element_type=jnp.float32)  29.2 us
  transfers between devices with their start and end apart: 28, of which 7 were waited for; matrix products, arithmetic and copies ran while one was open for 28% of the time, Pallas kernels for 28%

profile of v2, /device:TPU:0, one launch (start us, length us, event | category | flops | bytes accessed | tf_op | source)
XLA Modules:
  0.0 1206.9 jit_solution(16231518555836461718)
XLA Ops:
  19.4 10.7 fusion.9
  30.2 11.4 fusion.3
  41.6 12.0 fusion.54
  63.3 32.2 %collective-permute-done.4 = bf16[512,1536]{1,0:T(8,128)(2,1)} collective-permute-done((bf16[512,1536]{1,0:T(8,128)(2,1)S(1)}, bf16[512,1536]{1,0:T(8,128)(2,1)}, u32[]{:S(2)}, u32[]{:S(2)}) %collective-permute-start.4) | collective-permute-done | bytes 1572896 | tf_op jit(solution)/shard_map/ppermute | solution.py:331
  95.5 33.8 %collective-permute-done.1 = f32[512,20]{0,1:T(8,128)S(1)} collective-permute-done((f32[512,20]{0,1:T(8,128)S(1)}, f32[512,20]{0,1:T(8,128)S(1)}, u32[]{:S(2)}, u32[]{:S(2)}) %collective-permute-start.1) | collective-permute-done | bytes 40992 | tf_op jit(solution)/shard_map/ppermute | solution.py:331
  155.2 10.1 fusion.15
  199.7 9.2 fusion.17
  243.3 8.8 fusion.19
  287.6 8.9 fusion.21
  385.1 10.6 fusion.23
  395.8 9.2 fusion.62
  405.0 36.4 %add_convert_fusion = bf16[2048,1536]{1,0:T(8,128)(2,1)S(1)} fusion(f32[2048,1536]{1,0:T(8,128)} %fusion.62, f32[2048,1536]{1,0:T(8,128)} %fusion.73, f32[2048,1536]{1,0:T(8,128)} %fusion.69, f32[2048,1536]{1,0:T(8,128)} %fusion.84, f32[2048,1536]{1,0:T(8,128)} %fusion.80, f32[2048,1536]{1,0:T(8,128)} %fusion.95, f32[2048,1536]{1,0:T(8,128)} %fusion.91, ...), kind=kOutput, calls=%fused_computation.13 | convolution fusion | flops 3252682752 | bytes 123207680 | tf_op jit(solution)/shard_map/tf,df->td/dot_general | solution.py:462
  473.4 19.7 %add_convert_fusion.1 = bf16[2048,1536]{1,0:T(8,128)(2,1)S(1)} fusion(f32[2048,1536]{1,0:T(8,128)} %fusion.43, f32[2048,1536]{1,0:T(8,128)} %fusion.46, f32[2048,1536]{1,0:T(8,128)} %fusion.52, f32[2048,1536]{1,0:T(8,128)} %fusion.49, bf16[2048,512]{0,1:T(8,128)(2,1)} %get-tuple-element.107, f32[2048]{0:T(1024)S(1)} %bitcast.381, ...), kind=kOutput, calls=%fused_computation.14 | convolution fusion | flops 3240099840 | bytes 60301312 | tf_op jit(solution)/shard_map/dot_general | solution.py:466
  517.8 25.4 %collective-permute-done.17 = bf16[512,1536]{1,0:T(8,128)(2,1)S(1)} collective-permute-done((bf16[512,1536]{1,0:T(8,128)(2,1)S(1)}, bf16[512,1536]{1,0:T(8,128)(2,1)S(1)}, u32[]{:S(2)}, u32[]{:S(2)}) %collective-permute-start.17) | collective-permute-done | bytes 1572896 | tf_op jit(solution)/shard_map/ppermute | solution.py:331
  546.4 29.4 %collective-permute-done.11 = bf16[512,1536]{1,0:T(8,128)(2,1)S(1)} collective-permute-done((bf16[512,1536]{1,0:T(8,128)(2,1)S(1)}, bf16[512,1536]{1,0:T(8,128)(2,1)S(1)}, u32[]{:S(2)}, u32[]{:S(2)}) %collective-permute-start.11) | collective-permute-done | bytes 1572896 | tf_op jit(solution)/shard_map/ppermute | solution.py:331
  587.4 21.6 %fusion = (f32[8,3,512]{2,1,0:T(4,128)S(1)}, f32[8,512,512,3]{2,1,3,0:T(8,128)}) fusion(f32[8,3,512]{2,1,0:T(4,128)S(1)} %log_add_fusion, f32[8,512,512,3]{2,1,3,0:T(8,128)} %get-tuple-element.159, pred[512,512]{0,1:T(8,128)(4,1)S(1)} %copy-done.19, bf16[512,8,64,1]{0,2,3,1:T(8,128)(2,1)} %bitcast.365, bf16[512,8,3,64]{0,3,2,1:T(8,128)(2,1)S(1)} %bitcast.325), kind=kOutput, calls=%fused_computation.2 | convolution fusion | flops 836751360 | bytes 52789248 | tf_op jit(solution)/shard_map/while/body/eval_jaxpr/qhgd,khd->hgqk/dot_general | solution.py:90
  609.0 22.4 %fusion.2 = bf16[8,3,512,512]{2,3,1,0:T(8,128)(2,1)} fusion(f32[8,512,512,3]{2,1,3,0:T(8,128)} %get-tuple-element.165, f32[8,3,512]{2,1,0:T(4,128)S(1)} %get-tuple-element.164, f32[8,3,512]{2,1,0:T(4,128)S(1)} %log_add_fusion, f32[8,512,512,3]{2,1,3,0:T(8,128)} %get-tuple-element.159, pred[512,512]{0,1:T(8,128)(4,1)S(1)} %copy-done.19), kind=kLoop, calls=%fused_computation.4 | loop fusion | flops 37748736 | bytes 63275008 | tf_op jit(solution)/shard_map/while/body/eval_jaxpr/convert_element_type | solution.py:92
  631.4 8.5 fusion.144
  654.3 11.5 fusion.145
  682.1 12.5 %concatenate.80 = bf16[4,384,2688]{2,1,0:T(8,128)(2,1)} concatenate(bf16[4,384,1536]{2,1,0:T(8,128)(2,1)} %convolution_convert_fusion, bf16[4,384,512]{2,1,0:T(8,128)(2,1)} %convolution_convert_fusion.20, bf16[4,384,512]{2,1,0:T(8,128)(2,1)S(1)} %convolution_convert_fusion.19, bf16[4,384,1]{2,1,0:T(8,128)(2,1)S(1)} %concatenate.83, bf16[4,384,127]{2,1,0:T(8,128)(2,1)} %broadcast_in_dim.77), dimensions={2} | concatenate | bytes 16515072 | tf_op jit(solution)/shard_map/concatenate | solution.py:551
  724.3 8.6 concatenate.78
  755.8 63.6 %collective-permute-done.20 = bf16[384,1664]{1,0:T(8,128)(2,1)} collective-permute-done((bf16[384,1664]{1,0:T(8,128)(2,1)}, bf16[384,1664]{1,0:T(8,128)(2,1)}, u32[]{:S(2)}, u32[]{:S(2)}) %collective-permute-start.20) | collective-permute-done | bytes 1277984 | tf_op jit(solution)/shard_map/ppermute | solution.py:331
  823.9 334.0 %ring_sum.1 = (bf16[8,576,512]{2,1,0:T(8,128)(2,1)}, bf16[8,576,512]{2,1,0:T(8,128)(2,1)}, bf16[8,576,512]{2,1,0:T(8,128)(2,1)}, bf16[8,48,4352]{2,1,0:T(8,128)(2,1)S(1)}) custom-call(bf16[8,576,512]{2,1,0:T(8,128)(2,1)} %pad_maximum_fusion.3.refs_0_, bf16[8,576,512]{2,1,0:T(8,128)(2,1)} %pad_maximum_fusion.4.refs_1_, ...), custom_call_target="tpu_custom_call" | custom-call | flops 17498112 | bytes 69992448 | tf_op jit(solution)/shard_map/ring_sum/pallas_call | solution.py:253
  1173.9 26.1 %finish.1 = (f32[5,1536,512]{2,1,0:T(8,128)}, f32[5,1536,512]{2,1,0:T(8,128)}, f32[5,512,1536]{2,1,0:T(8,128)}) custom-call(bf16[8,576,512]{2,1,0:T(8,128)(2,1)S(1)} %copy-done.1, bf16[8,576,512]{2,1,0:T(8,128)(2,1)} %all-gather.5.cloned.1.call-done.refs_1_, bf16[8,576,512]{2,1,0:T(8,128)(2,1)} %get-tuple-element.91.refs_2_, ...), custom_call_target="tpu_custom_call" | custom-call | tf_op jit(solution)/shard_map/finish/pallas_call | solution.py:307
  (489 shorter events, 414.1 us)
Async XLA Ops:
  7.2 633.7 %reduce-scatter.3.cloned.1.call-start = ((), (), s32[]{:S(2)}) async-start(), calls=%async_computation.2 | async-start | bytes 5308416 | tf_op jit(solution)/shard_map/reduce_scatter | solution.py:452
  57.2 38.3 %collective-permute-start.4 = (bf16[512,1536]{1,0:T(8,128)(2,1)S(1)}, bf16[512,1536]{1,0:T(8,128)(2,1)}, u32[]{:S(2)}, u32[]{:S(2)}) collective-permute-start(bf16[512,1536]{1,0:T(8,128)(2,1)S(1)} %multiply_convert_fusion.15), channel_id=1, source_target_pairs={{0,2},{2,0},{1,3},{3,1},{4,6},{6,4},{5,7},{7,5},{8,10},{10,8},{9,1... | collective-permute-start | bytes 4718600 | tf_op jit(solution)/shard_map/ppermute | solution.py:331
  60.2 73.9 %collective-permute-start.7 = (bf16[512,1536]{1,0:T(8,128)(2,1)}, bf16[512,1536]{1,0:T(8,128)(2,1)}, u32[]{:S(2)}, u32[]{:S(2)}) collective-permute-start(bf16[512,1536]{1,0:T(8,128)(2,1)} %param.25), channel_id=1, source_target_pairs={{0,2},{2,0},{1,3},{3,1},{4,6},{6,4},{5,7},{7,5},{8,10},{10,8},{9,1... | collective-permute-start | bytes 4718600 | tf_op jit(solution)/shard_map/ppermute | solution.py:331
  60.3 74.2 %collective-permute-start.6 = (bf16[512,1536]{1,0:T(8,128)(2,1)}, bf16[512,1536]{1,0:T(8,128)(2,1)}, u32[]{:S(2)}, u32[]{:S(2)}) collective-permute-start(bf16[512,1536]{1,0:T(8,128)(2,1)} %param.25), channel_id=1, source_target_pairs={{0,1},{1,0},{2,3},{3,2},{4,5},{5,4},{6,7},{7,6},{8,9},{9,8},{10,11... | collective-permute-start | bytes 4718600 | tf_op jit(solution)/shard_map/ppermute | solution.py:327
  61.1 68.3 %collective-permute-start.1 = (f32[512,20]{0,1:T(8,128)S(1)}, f32[512,20]{0,1:T(8,128)S(1)}, u32[]{:S(2)}, u32[]{:S(2)}) collective-permute-start(f32[512,20]{0,1:T(8,128)S(1)} %fusion.172), channel_id=1, source_target_pairs={{0,2},{2,0},{1,3},{3,1},{4,6},{6,4},{5,7},{7,5},{8,10},{10,8},{9,1... | collective-permute-start | bytes 122888 | tf_op jit(solution)/shard_map/ppermute | solution.py:331
  63.1 76.7 %collective-permute-start.3 = (bf16[512,1536]{1,0:T(8,128)(2,1)S(1)}, bf16[512,1536]{1,0:T(8,128)(2,1)}, u32[]{:S(2)}, u32[]{:S(2)}) collective-permute-start(bf16[512,1536]{1,0:T(8,128)(2,1)S(1)} %multiply_convert_fusion.15), channel_id=1, source_target_pairs={{0,1},{1,0},{2,3},{3,2},{4,5},{5,4},{6,7},{7,6},{8,9},{9,8},{10,11... | collective-permute-start | bytes 4718600 | tf_op jit(solution)/shard_map/ppermute | solution.py:327
  95.5 44.3 %collective-permute-start.5 = (bf16[512,1536]{1,0:T(8,128)(2,1)}, bf16[512,1536]{1,0:T(8,128)(2,1)}, u32[]{:S(2)}, u32[]{:S(2)}) collective-permute-start(bf16[512,1536]{1,0:T(8,128)(2,1)} %collective-permute-done.4), channel_id=1, source_target_pairs={{0,1},{1,0},{2,3},{3,2},{4,5},{5,4},{6,7},{7,6},{8,9},{9,8},{10,11... | collective-permute-start | bytes 4718600 | tf_op jit(solution)/shard_map/ppermute | solution.py:327
  134.1 21.0 %collective-permute-start.8 = (bf16[512,1536]{1,0:T(8,128)(2,1)}, bf16[512,1536]{1,0:T(8,128)(2,1)S(1)}, u32[]{:S(2)}, u32[]{:S(2)}) collective-permute-start(bf16[512,1536]{1,0:T(8,128)(2,1)} %collective-permute-done.7), channel_id=1, source_target_pairs={{0,1},{1,0},{2,3},{3,2},{4,5},{5,4},{6,7},{7,6},{8,9},{9,8},{10,11... | collective-permute-start | bytes 4718600 | tf_op jit(solution)/shard_map/ppermute | solution.py:327
  384.5 348.4 %reduce-scatter.5.cloned.1.call-start = ((), (), s32[]{:S(2)}) async-start(), calls=%async_computation.4 | async-start | bytes 5308416 | tf_op jit(solution)/shard_map/reduce_scatter | solution.py:452
  445.3 56.6 %collective-permute-start.16 = (bf16[512,1536]{1,0:T(8,128)(2,1)}, bf16[512,1536]{1,0:T(8,128)(2,1)}, u32[]{:S(2)}, u32[]{:S(2)}) collective-permute-start(bf16[512,1536]{1,0:T(8,128)(2,1)} %get-tuple-element.133), channel_id=1, source_target_pairs={{0,1},{1,0},{2,3},{3,2},{4,5},{5,4},{6,7},{7,6},{8,9},{9,8},{10,11... | collective-permute-start | bytes 4718600 | tf_op jit(solution)/shard_map/ppermute | solution.py:327
  498.5 10.8 collective-permute-start.12
  499.0 47.4 %collective-permute-start.9 = (bf16[512,1536]{1,0:T(8,128)(2,1)}, bf16[512,1536]{1,0:T(8,128)(2,1)S(1)}, u32[]{:S(2)}, u32[]{:S(2)}) collective-permute-start(bf16[512,1536]{1,0:T(8,128)(2,1)} %get-tuple-element.134), channel_id=1, source_target_pairs={{0,1},{1,0},{2,3},{3,2},{4,5},{5,4},{6,7},{7,6},{8,9},{9,8},{10,11... | collective-permute-start | bytes 4718600 | tf_op jit(solution)/shard_map/ppermute | solution.py:327
  499.1 672.4 %all-gather.3.cloned.1.call-start = ((), (), s32[]{:S(2)}) async-start(), calls=%async_computation.3 | async-start | bytes 5308416 | tf_op jit(solution)/shard_map/all_gather | solution.py:451
  500.7 17.2 %collective-permute-start.15 = (bf16[512,1536]{1,0:T(8,128)(2,1)}, bf16[512,1536]{1,0:T(8,128)(2,1)S(1)}, u32[]{:S(2)}, u32[]{:S(2)}) collective-permute-start(bf16[512,1536]{1,0:T(8,128)(2,1)} %get-tuple-element.132), channel_id=1, source_target_pairs={{0,1},{1,0},{2,3},{3,2},{4,5},{5,4},{6,7},{7,6},{8,9},{9,8},{10,11... | collective-permute-start | bytes 4718600 | tf_op jit(solution)/shard_map/ppermute | solution.py:327
  501.9 15.9 %collective-permute-start.14 = (f32[512,20]{0,1:T(8,128)S(1)}, f32[512,20]{0,1:T(8,128)S(1)}, u32[]{:S(2)}, u32[]{:S(2)}) collective-permute-start(f32[512,20]{0,1:T(8,128)S(1)} %slice_add_fusion), channel_id=1, source_target_pairs={{0,2},{2,0},{1,3},{3,1},{4,6},{6,4},{5,7},{7,5},{8,10},{10,8},{9,1... | collective-permute-start | bytes 122888 | tf_op jit(solution)/shard_map/ppermute | solution.py:331
  505.9 37.3 %collective-permute-start.17 = (bf16[512,1536]{1,0:T(8,128)(2,1)S(1)}, bf16[512,1536]{1,0:T(8,128)(2,1)S(1)}, u32[]{:S(2)}, u32[]{:S(2)}) collective-permute-start(bf16[512,1536]{1,0:T(8,128)(2,1)S(1)} %add_convert_fusion.3), channel_id=1, source_target_pairs={{0,2},{2,0},{1,3},{3,1},{4,6},{6,4},{5,7},{7,5},{8,10},{10,8},{9,1... | collective-permute-start | bytes 4718600 | tf_op jit(solution)/shard_map/ppermute | solution.py:331
  509.2 66.6 %collective-permute-start.11 = (bf16[512,1536]{1,0:T(8,128)(2,1)S(1)}, bf16[512,1536]{1,0:T(8,128)(2,1)S(1)}, u32[]{:S(2)}, u32[]{:S(2)}) collective-permute-start(bf16[512,1536]{1,0:T(8,128)(2,1)S(1)} %add_convert_fusion.6), channel_id=1, source_target_pairs={{0,2},{2,0},{1,3},{3,1},{4,6},{6,4},{5,7},{7,5},{8,10},{10,8},{9,1... | collective-permute-start | bytes 4718600 | tf_op jit(solution)/shard_map/ppermute | solution.py:331
  640.9 530.6 %all-gather.5.cloned.1.call-start = ((), (), s32[]{:S(2)}) async-start(), calls=%async_computation.5 | async-start | bytes 5308416 | tf_op jit(solution)/shard_map/all_gather | solution.py:451
  699.2 43.4 %collective-permute-start.22 = (bf16[384,2688]{1,0:T(8,128)(2,1)}, bf16[384,2688]{1,0:T(8,128)(2,1)}, u32[]{:S(2)}, u32[]{:S(2)}) collective-permute-start(bf16[384,2688]{1,0:T(8,128)(2,1)} %get-tuple-element.127), channel_id=1, source_target_pairs={{0,1},{1,0},{2,3},{3,2},{4,5},{5,4},{6,7},{7,6},{8,9},{9,8},{10,11... | collective-permute-start | bytes 6193160 | tf_op jit(solution)/shard_map/ppermute | solution.py:327
  735.0 10.3 collective-permute-start.19
  742.0 13.8 %collective-permute-start.18 = (bf16[384,1664]{1,0:T(8,128)(2,1)S(1)}, bf16[384,1664]{1,0:T(8,128)(2,1)S(1)}, u32[]{:S(2)}, u32[]{:S(2)}) collective-permute-start(bf16[384,1664]{1,0:T(8,128)(2,1)S(1)} %get-tuple-element.136), channel_id=1, source_target_pairs={{0,1},{1,0},{2,3},{3,2},{4,5},{5,4},{6,7},{7,6},{8,9},{9,8},{10,11... | collective-permute-start | bytes 3833864 | tf_op jit(solution)/shard_map/ppermute | solution.py:327
  742.4 78.8 %collective-permute-start.21 = (bf16[384,2688]{1,0:T(8,128)(2,1)S(1)}, bf16[384,2688]{1,0:T(8,128)(2,1)S(1)}, u32[]{:S(2)}, u32[]{:S(2)}) collective-permute-start(bf16[384,2688]{1,0:T(8,128)(2,1)S(1)} %copy-done.29), channel_id=1, source_target_pairs={{0,1},{1,0},{2,3},{3,2},{4,5},{5,4},{6,7},{7,6},{8,9},{9,8},{10,11... | collective-permute-start | bytes 6193160 | tf_op jit(solution)/shard_map/ppermute | solution.py:327
  744.8 76.5 %collective-permute-start.23 = (bf16[384,2688]{1,0:T(8,128)(2,1)S(1)}, bf16[384,2688]{1,0:T(8,128)(2,1)S(1)}, u32[]{:S(2)}, u32[]{:S(2)}) collective-permute-start(bf16[384,2688]{1,0:T(8,128)(2,1)S(1)} %fusion.29), channel_id=1, source_target_pairs={{0,2},{2,0},{1,3},{3,1},{4,6},{6,4},{5,7},{7,5},{8,10},{10,8},{9,1... | collective-permute-start | bytes 6193160 | tf_op jit(solution)/shard_map/ppermute | solution.py:331
  746.7 72.8 %collective-permute-start.20 = (bf16[384,1664]{1,0:T(8,128)(2,1)}, bf16[384,1664]{1,0:T(8,128)(2,1)}, u32[]{:S(2)}, u32[]{:S(2)}) collective-permute-start(bf16[384,1664]{1,0:T(8,128)(2,1)} %fusion.38), channel_id=1, source_target_pairs={{0,2},{2,0},{1,3},{3,1},{4,6},{6,4},{5,7},{7,5},{8,10},{10,8},{9,1... | collective-permute-start | bytes 3833864 | tf_op jit(solution)/shard_map/ppermute | solution.py:331
  (147 other events, 1776.8 us)
Sparse Core Ops, SparseCore 0:
  384.6 96.7 reduce-scatter.2
  499.2 96.9 reduce-scatter.4
  641.1 80.2 all-gather.2
  733.0 80.3 all-gather.4

commit v3 on v2

v3 whole, which is shorter than its diff:
```python
import functools
import math

import jax
import jax.numpy as jnp
from jax import lax
from jax.experimental import pallas as pl
from jax.experimental.pallas import tpu as pltpu
from jax.sharding import PartitionSpec as P

QUERY_HEADS = 24
KEY_VALUE_HEADS = 8
HEAD_SIZE = 64
TOPK = 8
SEQUENCE_TOKENS = 512
BLOCK = 256
EARLY = 1


epsilon = 1e-06
masked_value = -1e30


def rope_tables(token_count):
    half = HEAD_SIZE // 2
    places = (jnp.arange(token_count) % SEQUENCE_TOKENS).astype(jnp.float32)
    rates = jnp.exp(jnp.arange(half, dtype=jnp.float32) * (-2.0 * math.log(10000.0) / HEAD_SIZE))
    angles = places[:, None] * rates[None, :]
    cosine, sine = jnp.cos(angles), jnp.sin(angles)
    return (
        jnp.concatenate([cosine] * 4, 1),
        jnp.concatenate([-sine, sine] * 2, 1),
    )


def contract(left, right, left_dim, right_dim):
    return lax.dot_general(
        left, right, (((left_dim,), (right_dim,)), ((), ())), preferred_element_type=jnp.float32
    )


def whole(array):
    return pl.BlockSpec(
        array.shape, lambda *_: (0,) * array.ndim, pipeline_mode=pl.Buffered(1)
    )


def each(array):
    return pl.BlockSpec((1,) + array.shape[1:], lambda e, *_: (e,) + (0,) * (array.ndim - 1))


VMEM_BYTES = 56 * 2**20


def expert_kernel(tile, h0, h1, c0, c1, gates0, gates1, w_gate, w_up, w_down, gh, dg, du, d_router0, d_router1):
    e = pl.program_id(0)
    tokens, lanes = gates0.shape
    lane = lax.broadcasted_iota(jnp.int32, (tile, lanes), 1)

    @pl.when(e == 0)
    def _():
        d_router0[...] = jnp.zeros_like(d_router0)
        d_router1[...] = jnp.zeros_like(d_router1)

    for base, rows_h, rows_c, gates, d_router in (
        (0, h0, c0, gates0, d_router0),
        (tokens, h1, c1, gates1, d_router1),
    ):
        for start in range(0, tokens, tile):
            rows = slice(start, start + tile)
            out = slice(base + start, base + start + tile)
            entries = rows_h[rows, :]
            gate_pre = contract(entries, w_gate[0], 1, 0)
            up_pre = contract(entries, w_up[0], 1, 0)
            back = contract(rows_c[rows, :], w_down[0], 1, 1)
            column = jnp.sum(jnp.where(lane == e, gates[rows, :], 0.0), 1, keepdims=True)
            sigma = jax.nn.sigmoid(gate_pre)
            swish = gate_pre * sigma
            hidden = (swish * up_pre).astype(jnp.bfloat16).astype(jnp.float32)
            d_router[rows, :] = jnp.where(
                lane == e, jnp.sum(hidden * back, 1, keepdims=True), d_router[rows, :]
            )
            d_hidden = column * back
            dg[0, out, :] = (
                d_hidden * up_pre * (sigma * (1.0 + gate_pre * (1.0 - sigma)))
            ).astype(jnp.bfloat16)
            du[0, out, :] = (d_hidden * swish).astype(jnp.bfloat16)
            gh[0, out, :] = (column * hidden).astype(jnp.bfloat16)


def expert_pass(hs, cots, gates, w_gate, w_up, w_down):
    count, width = hs[0].shape
    tokens = 2 * count
    held, _, hidden_units = w_gate.shape
    part = jax.ShapeDtypeStruct((held, tokens, hidden_units), jnp.bfloat16)
    gate_shape = gates[0].shape
    return pl.pallas_call(
        functools.partial(expert_kernel, 256),
        grid=(held,),
        in_specs=[whole(a) for a in (*hs, *cots, *gates)] + [each(a) for a in (w_gate, w_up, w_down)],
        out_specs=[each(part)] * 3 + [pl.BlockSpec(gate_shape, lambda e: (0, 0))] * 2,
        out_shape=[part] * 3 + [jax.ShapeDtypeStruct(gate_shape, jnp.float32)] * 2,
        compiler_params=pltpu.CompilerParams(vmem_limit_bytes=VMEM_BYTES),
        cost_estimate=pl.CostEstimate(
            flops=6 * held * tokens * width * hidden_units,
            bytes_accessed=6 * held * width * hidden_units,
            transcendentals=held * tokens * hidden_units,
        ),
        name="expert_pass",
    )(*hs, *cots, *gates, w_gate, w_up, w_down)


def weight_kernel(*refs):
    hs, cots, passes, unit = refs[:4], refs[4:8], refs[8:14], refs[14]
    kind = pl.program_id(1)

    def put(lefts, rights):
        count = lefts[0].shape[0]
        result = sum(
            contract(lefts[k][...], rights[k // 2][0, (k % 2) * count : (k % 2 + 1) * count], 0, 0)
            for k in range(4)
        ).astype(jnp.bfloat16)
        rows = unit.shape[3]
        for j in range(unit.shape[1]):
            unit[0, j, 0] = result[j * rows : (j + 1) * rows]

    pl.when(kind == 0)(lambda: put(hs, passes[2:4]))
    pl.when(kind == 1)(lambda: put(hs, passes[4:6]))
    pl.when(kind == 2)(lambda: put(cots, passes[:2]))


def weight_grads(count, first, many, hs, cots, ghs, dgs, dus):
    width = hs[0].shape[1]
    _, tokens, hidden_units = dgs[0].shape
    entry = pl.BlockSpec((1, tokens, hidden_units), lambda e, k: (e + first, 0, 0))
    unit = pl.pallas_call(
        weight_kernel,
        grid=(many, 3),
        in_specs=[whole(hs[0])] * 8 + [entry] * 6,
        out_specs=pl.BlockSpec((1, count, 1, width // count, hidden_units), lambda e, k: (e, 0, k, 0, 0)),
        out_shape=jax.ShapeDtypeStruct((many, count, 3, width // count, hidden_units), jnp.bfloat16),
        compiler_params=pltpu.CompilerParams(vmem_limit_bytes=VMEM_BYTES),
        cost_estimate=pl.CostEstimate(
            flops=12 * many * tokens * width * hidden_units,
            bytes_accessed=6 * many * (width + 2 * tokens) * hidden_units,
            transcendentals=0,
        ),
        name="weight_grads",
    )(*hs, *cots, *ghs, *dgs, *dus)
    return unit.reshape(many, count, 3 * (width // count), hidden_units)


def sum_kernel(right_dim, pairs, *refs):
    lefts, rights, outs, total = refs[:pairs], refs[pairs : 2 * pairs], refs[-3:-1], refs[-1]
    e = pl.program_id(0)
    term = sum(contract(left[0], right[0], 1, right_dim) for left, right in zip(lefts, rights))

    @pl.when(e == 0)
    def _():
        total[...] = term

    @pl.when(e > 0)
    def _():
        total[...] += term

    @pl.when(e == pl.num_programs(0) - 1)
    def _():
        for k, out in enumerate(outs):
            count = out.shape[0]
            out[...] = total[k * count : (k + 1) * count].astype(out.dtype)


def sum_over_experts(lefts, rights, right_dim):
    held, tokens, inner = lefts[0].shape
    width = rights[0].shape[2 - right_dim]
    return pl.pallas_call(
        functools.partial(sum_kernel, right_dim, len(lefts)),
        grid=(held,),
        in_specs=[each(a) for a in lefts] + [each(a) for a in rights],
        out_specs=[pl.BlockSpec((tokens // 2, width), lambda e: (0, 0))] * 2,
        out_shape=[jax.ShapeDtypeStruct((tokens // 2, width), jnp.bfloat16)] * 2,
        scratch_shapes=[pltpu.VMEM((tokens, width), jnp.float32)],
        compiler_params=pltpu.CompilerParams(vmem_limit_bytes=VMEM_BYTES),
        cost_estimate=pl.CostEstimate(
            flops=2 * len(lefts) * held * tokens * width * inner,
            bytes_accessed=2 * len(lefts) * held * (tokens + width) * inner,
            transcendentals=0,
        ),
        name="sum_over_experts",
    )(*lefts, *rights)


def rotate(values, cosine, sine, way):
    lane = lax.broadcasted_iota(jnp.int32, cosine.shape, 1)
    first = lane % HEAD_SIZE < HEAD_SIZE // 2
    lanes = cosine.shape[1]
    half = HEAD_SIZE // 2
    pieces = []
    for start in range(0, values.shape[1], lanes):
        piece = values[:, start : start + lanes]
        other = jnp.where(first, pltpu.roll(piece, lanes - half, 1), pltpu.roll(piece, half, 1))
        pieces.append(piece * cosine + way * (other * sine))
    return jnp.concatenate(pieces, 1)


def heads_of(array, group, rows, queries):
    return jnp.concatenate(
        [
            array[rows, (group * queries + j) * HEAD_SIZE : (group * queries + j + 1) * HEAD_SIZE]
            for j in range(queries)
        ],
        0,
    )


def attention_kernel(
    tokens, norm_attn, w_query, w_key, w_value, cosine, sine, w_out, norm_ffn, w_router, routes,
    normed, queries, keys, values, log_totals, attn, resid, h_two, probs, combine,
):
    count, width = tokens.shape
    field = tokens[...].astype(jnp.float32)
    inverse = lax.rsqrt(jnp.mean(field * field, -1, keepdims=True) + epsilon)
    first = (field * inverse * norm_attn[...].astype(jnp.float32)).astype(jnp.bfloat16)
    normed[...] = first
    queries[...] = rotate(contract(first, w_query[...], 1, 0), cosine[...], sine[...], 1).astype(jnp.bfloat16)
    keys[...] = rotate(contract(first, w_key[...], 1, 0), cosine[...], sine[...], 1).astype(jnp.bfloat16)
    values[...] = contract(first, w_value[...], 1, 0).astype(jnp.bfloat16)
    groups = keys.shape[1] // HEAD_SIZE
    per_group = queries.shape[1] // keys.shape[1]
    lane = lax.broadcasted_iota(jnp.int32, (BLOCK, log_totals.shape[1]), 1)
    for block in range(count // BLOCK):
        rows = slice(block * BLOCK, (block + 1) * BLOCK)
        seen = slice(0, (block + 1) * BLOCK)
        logs = jnp.zeros((BLOCK, log_totals.shape[1]), jnp.float32)
        for group in range(groups):
            cut = slice(group * HEAD_SIZE, (group + 1) * HEAD_SIZE)
            scores = contract(heads_of(queries, group, rows, per_group), keys[seen, cut], 1, 1)
            scores = scores * HEAD_SIZE ** (-0.5)
            highest = jnp.max(scores, -1, keepdims=True)
            shifted = jnp.exp(scores - highest)
            sums = jnp.sum(shifted, -1, keepdims=True)
            probs_bf = (shifted * (1.0 / sums)).astype(jnp.bfloat16)
            mix = contract(probs_bf, values[seen, cut], 1, 0).astype(jnp.bfloat16)
            log_sum = highest + jnp.log(sums)
            for j in range(per_group):
                head = group * per_group + j
                part = slice(j * BLOCK, (j + 1) * BLOCK)
                attn[rows, head * HEAD_SIZE : (head + 1) * HEAD_SIZE] = mix[part]
                logs = jnp.where(lane == head, log_sum[part], logs)
        log_totals[rows, :] = logs
    total = field + contract(attn[...], w_out[...], 1, 0)
    resid[...] = total
    inverse = lax.rsqrt(jnp.mean(total * total, -1, keepdims=True) + epsilon)
    second = (total * inverse * norm_ffn[...].astype(jnp.float32)).astype(jnp.bfloat16)
    h_two[...] = second
    logits = contract(second, w_router[...], 1, 0)
    lane = lax.broadcasted_iota(jnp.int32, logits.shape, 1)
    experts = probs.shape[1]
    logits = jnp.where(lane < experts, logits, masked_value)
    shifted = jnp.exp(logits - jnp.max(logits, -1, keepdims=True))
    soft = shifted / jnp.sum(shifted, -1, keepdims=True)
    chosen = jnp.zeros(logits.shape, jnp.bool_)
    for k in range(routes.shape[1]):
        chosen = chosen | (routes[:, k : k + 1] == lane)
    probs[...] = soft[:, :experts]
    combine[...] = jnp.where(chosen, soft, 0.0)[:, :experts]


LANES = 128


def attention_forward(tokens, norm_attn, w_query, w_key, w_value, cosine, sine, w_out, norm_ffn, w_router, routes):
    count, width = tokens.shape
    experts = w_router.shape[1]
    wide_router = jnp.pad(w_router, ((0, 0), (0, LANES - experts)))
    key_width = w_key.shape[1]
    shape = jax.ShapeDtypeStruct
    return pl.pallas_call(
        attention_kernel,
        out_shape=[
            shape((count, width), jnp.bfloat16),
            shape((count, width), jnp.bfloat16),
            shape((count, key_width), jnp.bfloat16),
            shape((count, key_width), jnp.bfloat16),
            shape((count, LANES), jnp.float32),
            shape((count, width), jnp.bfloat16),
            shape((count, width), jnp.float32),
            shape((count, width), jnp.bfloat16),
            shape((count, experts), jnp.float32),
            shape((count, experts), jnp.float32),
        ],
        compiler_params=pltpu.CompilerParams(vmem_limit_bytes=VMEM_BYTES),
        cost_estimate=pl.CostEstimate(
            flops=6 * count * width * width, bytes_accessed=8 * width * width, transcendentals=24 * count * count
        ),
        name="attention_forward",
    )(
        tokens, norm_attn[None], w_query, w_key, w_value, cosine, sine, w_out, norm_ffn[None], wide_router, routes
    )


def as_lane(row):
    first = lax.broadcasted_iota(jnp.int32, (LANES, row.shape[1]), 0) == 0
    return jnp.where(first, row, 0.0).T.astype(jnp.bfloat16)


def attention_back_kernel(
    dh_own, dh_near, dh_far, d_router, probs, resid, norm_ffn, cotangent, w_router, w_out, h_two, attn,
    queries, keys, values, log_totals, cosine, sine,
    d_resid, d_pre, grad_out, d_branch, d_attn, d_queries, d_keys, d_values,
):
    count, width = resid.shape
    experts = probs.shape[1]
    soft = probs[...]
    to_router = d_router[...]
    d_logits = (soft * (to_router - jnp.sum(soft * to_router, -1, keepdims=True))).astype(jnp.bfloat16)
    d_logits = jnp.concatenate([d_logits, jnp.zeros((count, LANES - experts), jnp.bfloat16)], 1)
    d_normed = (
        dh_own[...].astype(jnp.float32)
        + dh_near[...].astype(jnp.float32)
        + dh_far[...].astype(jnp.float32)
        + contract(d_logits, w_router[...], 1, 1)
    )
    total = resid[...]
    inverse = lax.rsqrt(jnp.mean(total * total, -1, keepdims=True) + epsilon)
    normal = total * inverse
    scaled = d_normed * norm_ffn[...].astype(jnp.float32)
    back = cotangent[...].astype(jnp.float32) + inverse * (
        scaled - normal * jnp.mean(scaled * normal, -1, keepdims=True)
    )
    d_resid[...] = back
    d_branch[...] = back.astype(jnp.bfloat16)
    grad_out[:, :width] = contract(attn[...], d_branch[...], 0, 0).astype(jnp.bfloat16)
    grad_out[:, width : width + LANES] = contract(h_two[...], d_logits, 0, 0).astype(jnp.bfloat16)
    grad_out[:, width + LANES :] = as_lane(jnp.sum(d_normed * normal, 0, keepdims=True))
    d_attn[...] = contract(d_branch[...], w_out[...], 1, 1).astype(jnp.bfloat16)
    groups = keys.shape[1] // HEAD_SIZE
    per_group = queries.shape[1] // keys.shape[1]
    factor = HEAD_SIZE ** (-0.5)
    lane = lax.broadcasted_iota(jnp.int32, (BLOCK, log_totals.shape[1]), 1)
    for block in reversed(range(count // BLOCK)):
        rows = slice(block * BLOCK, (block + 1) * BLOCK)
        seen = slice(0, (block + 1) * BLOCK)
        logs = log_totals[rows, :]
        for group in range(groups):
            cut = slice(group * HEAD_SIZE, (group + 1) * HEAD_SIZE)
            part_q = heads_of(queries, group, rows, per_group)
            part_d = heads_of(d_attn, group, rows, per_group)
            log_sum = jnp.concatenate(
                [
                    jnp.sum(jnp.where(lane == group * per_group + j, logs, 0.0), 1, keepdims=True)
                    for j in range(per_group)
                ],
                0,
            )
            part_k, part_v = keys[seen, cut], values[seen, cut]
            probs_f = jnp.exp(contract(part_q, part_k, 1, 1) * factor - log_sum)
            d_probs = contract(part_d, part_v, 1, 1)
            centre = jnp.sum(probs_f * d_probs, -1, keepdims=True)
            d_scores = (probs_f * (d_probs - centre)).astype(jnp.bfloat16)
            turned = contract(d_scores, part_k, 1, 0) * factor
            for j in range(per_group):
                head = group * per_group + j
                d_queries[rows, head * HEAD_SIZE : (head + 1) * HEAD_SIZE] = turned[j * BLOCK : (j + 1) * BLOCK]
            new_k = contract(d_scores, part_q, 0, 0) * factor
            new_v = contract(probs_f.astype(jnp.bfloat16), part_d, 0, 0)
            if block == count // BLOCK - 1:
                d_keys[seen, cut] = new_k
                d_values[seen, cut] = new_v
            else:
                d_keys[seen, cut] += new_k
                d_values[seen, cut] += new_v
    key_width = keys.shape[1]
    d_pre[:, :width] = rotate(d_queries[...], cosine[...], sine[...], -1).astype(jnp.bfloat16)
    d_pre[:, width : width + key_width] = rotate(d_keys[...], cosine[...], sine[...], -1).astype(jnp.bfloat16)
    d_pre[:, width + key_width :] = d_values[...].astype(jnp.bfloat16)


def attention_back(dh_own, dh_near, dh_far, d_router, probs, resid, norm_ffn, cotangent, w_router, w_out, h_two, attn,
                   queries, keys, values, log_totals, cosine, sine):
    count, width = resid.shape
    key_width = keys.shape[1]
    wide_router = jnp.pad(w_router, ((0, 0), (0, LANES - w_router.shape[1])))
    shape = jax.ShapeDtypeStruct
    return pl.pallas_call(
        attention_back_kernel,
        out_shape=[
            shape((count, width), jnp.float32),
            shape((count, width + 2 * key_width), jnp.bfloat16),
            shape((width, width + 2 * LANES), jnp.bfloat16),
        ],
        scratch_shapes=[
            pltpu.VMEM((count, width), jnp.bfloat16),
            pltpu.VMEM((count, width), jnp.bfloat16),
            pltpu.VMEM((count, width), jnp.float32),
            pltpu.VMEM((count, key_width), jnp.float32),
            pltpu.VMEM((count, key_width), jnp.float32),
        ],
        compiler_params=pltpu.CompilerParams(vmem_limit_bytes=VMEM_BYTES),
        cost_estimate=pl.CostEstimate(
            flops=10 * count * width * width, bytes_accessed=8 * width * width, transcendentals=24 * count * count
        ),
        name="attention_back",
    )(
        dh_own, dh_near, dh_far, d_router, probs, resid, norm_ffn[None], cotangent, wide_router, w_out, h_two, attn,
        queries, keys, values, log_totals, cosine, sine,
    )


def input_kernel(d_pre, normed, tokens, norm_attn, d_resid, w_query, w_key, w_value, d_input, grads):
    width, key_width = w_query.shape[1], w_key.shape[1]
    entries = d_pre[...]
    d_normed = (
        contract(entries[:, :width], w_query[...], 1, 1)
        + contract(entries[:, width : width + key_width], w_key[...], 1, 1)
        + contract(entries[:, width + key_width :], w_value[...], 1, 1)
    )
    field = tokens[...].astype(jnp.float32)
    inverse = lax.rsqrt(jnp.mean(field * field, -1, keepdims=True) + epsilon)
    normal = field * inverse
    scaled = d_normed * norm_attn[...].astype(jnp.float32)
    d_input[...] = d_resid[...] + inverse * (scaled - normal * jnp.mean(scaled * normal, -1, keepdims=True))
    wide = entries.shape[1]
    grads[:, :wide] = contract(normed[...], entries, 0, 0).astype(jnp.bfloat16)
    grads[:, wide : wide + LANES] = as_lane(jnp.sum(d_normed * normal, 0, keepdims=True))
    grads[:, wide + LANES :] = jnp.zeros((width, LANES), jnp.bfloat16)


def input_back(d_pre, normed, tokens, norm_attn, d_resid, w_query, w_key, w_value):
    count, width = tokens.shape
    shape = jax.ShapeDtypeStruct
    return pl.pallas_call(
        input_kernel,
        out_shape=[
            shape((count, width), jnp.float32),
            shape((width, d_pre.shape[1] + 2 * LANES), jnp.bfloat16),
        ],
        compiler_params=pltpu.CompilerParams(vmem_limit_bytes=VMEM_BYTES),
        cost_estimate=pl.CostEstimate(
            flops=8 * count * width * width, bytes_accessed=12 * width * width, transcendentals=0
        ),
        name="input_back",
    )(d_pre, normed, tokens, norm_attn[None], d_resid, w_query, w_key, w_value)


SLOTS = 3


def ring_device(place, count):
    back = place // (count // 2)
    return (1 - back) * 2 * place + back * (2 * (count - 1 - place) + 1)


def ring_kernel(count, many, lag, shapes, *refs):
    dense = len(shapes) - many
    inputs, outputs, rest = refs[: 1 + dense], refs[1 + dense : 2 + 2 * dense], refs[2 + 2 * dense :]
    total = len(shapes)
    held, terms, rest = rest[:total], rest[total : 2 * total], rest[2 * total :]
    own, near, far, joined, rest = (
        rest[:dense], rest[dense : 2 * dense], rest[2 * dense : 3 * dense], rest[3 * dense : 4 * dense], rest[4 * dense :]
    )
    arrived, sent, loaded, stored, near_sent, near_arrived, own_loaded, far_sent, far_arrived, credit = rest
    sources = [inputs[0].at[k] for k in range(many)] + list(joined)
    sums = [outputs[0].at[k] for k in range(many)] + list(outputs[1:])
    here = lax.axis_index("rep")
    odd = here % 2
    rank = here // 2 + odd * (count - 1 - 2 * (here // 2))
    after = ring_device((rank + 1) % count, count)
    before = ring_device((rank + count - 1) % count, count)
    hops = 2 * (count - 1)
    holder = lax.axis_index("ep")
    core = holder + 1 - 2 * (holder % 2)
    chip = (holder + 2) % 4
    far_core = (core + 2) % 4

    barrier = pltpu.get_barrier_semaphore()
    for neighbour in (before, after):
        pl.semaphore_signal(barrier, inc=1, device_id={"rep": neighbour})
    for neighbour in (core, chip):
        pl.semaphore_signal(barrier, inc=1, device_id={"ep": neighbour})
    pl.semaphore_wait(barrier, 4)

    def columns(index, way):
        half = shapes[index][1] // 2
        return pl.ds(way * half, half)

    def send(index, way, hop):
        stream = 2 * index + way
        source = (hop + SLOTS - 1) % SLOTS
        slot = hop % SLOTS
        return pltpu.make_async_remote_copy(
            src_ref=held[index].at[way, source],
            dst_ref=held[index].at[way, slot],
            send_sem=sent.at[stream, slot],
            recv_sem=arrived.at[stream, slot],
            device_id={"rep": before if way else after},
        )

    def load(index, way, hop):
        step = hop + 2
        chunk = (rank + step) % count if way else (rank + 2 * count - step) % count
        return pltpu.make_async_copy(
            sources[index].at[chunk, :, columns(index, way)],
            terms[index].at[way, hop % 2],
            loaded.at[2 * index + way, hop % 2],
        )

    def first(index, way):
        chunk = (rank + 1) % count if way else (rank + count - 1) % count
        return pltpu.make_async_copy(
            sources[index].at[chunk, :, columns(index, way)],
            held[index].at[way, SLOTS - 1],
            stored.at[2 * index + way, SLOTS - 1],
        )

    def store(index, way, hop):
        step = hop - (count - 2)
        chunk = (rank + step) % count if way else (rank + count - step) % count
        return pltpu.make_async_copy(
            held[index].at[way, hop % SLOTS],
            sums[index].at[chunk, :, columns(index, way)],
            stored.at[2 * index + way, hop % SLOTS],
        )

    def release(index, way):
        pl.semaphore_signal(
            credit.at[2 * index + way], inc=1, device_id={"rep": after if way else before}
        )

    def begin(streams):
        for index, way in streams:
            first(index, way).start()
        for index, way in streams:
            load(index, way, 0).start()
            load(index, way, 1).start()
        for index, way in streams:
            first(index, way).wait()
            send(index, way, 0).start()

    def take(index, way, hop):
        send(index, way, hop).wait_recv()
        send(index, way, hop).wait_send()

    def pass_on(index, way, hop):
        @pl.when(hop + 1 >= 2)
        def _():
            pl.semaphore_wait(credit.at[2 * index + way], 1)

        send(index, way, hop + 1).start()

    def add_step(streams, hop):
        for index, way in streams:
            take(index, way, hop)

            @pl.when(hop <= hops - 3)
            def _():
                release(index, way)

            load(index, way, hop).wait()
            slot = hop % SLOTS
            held[index][way, slot] = (
                held[index][way, slot].astype(jnp.float32)
                + terms[index][way, hop % 2].astype(jnp.float32)
            ).astype(jnp.bfloat16)
            pass_on(index, way, hop)

            @pl.when(hop + 2 <= count - 2)
            def _():
                load(index, way, hop + 2).start()

            @pl.when(hop == count - 2)
            def _():
                store(index, way, hop).start()

    def hand_step(streams, hop):
        for index, way in streams:
            take(index, way, hop)
            store(index, way, hop - 1).wait()

            @pl.when(hop <= hops - 3)
            def _():
                release(index, way)

            @pl.when(hop + 1 < hops)
            def _():
                pass_on(index, way, hop)

            store(index, way, hop).start()

    def block(k, index):
        rows = own[k].shape[1]
        return inputs[1 + k].at[pl.ds(pl.multiple_of(index * rows, 8), rows), :]

    def to_core(k, part):
        return pltpu.make_async_remote_copy(
            src_ref=block(k, far_core if part else core),
            dst_ref=near[k].at[part],
            send_sem=near_sent.at[k, part],
            recv_sem=near_arrived.at[k, part],
            device_id={"ep": core},
        )

    def own_block(k, part):
        return pltpu.make_async_copy(
            block(k, chip if part else holder), own[k].at[part], own_loaded.at[k, part]
        )

    def to_chip(k):
        return pltpu.make_async_remote_copy(
            src_ref=own[k].at[1],
            dst_ref=far[k],
            send_sem=far_sent.at[k],
            recv_sem=far_arrived.at[k],
            device_id={"ep": chip},
        )

    pieces = 8

    def send_far():
        for k in range(dense):
            to_core(k, 1).wait_recv()
            own_block(k, 1).wait()
            rows = own[k].shape[1] // pieces
            for j in range(pieces):
                cut = slice(j * rows, (j + 1) * rows)
                own[k][1, cut] = (
                    own[k][1, cut].astype(jnp.float32) + near[k][1, cut].astype(jnp.float32)
                ).astype(jnp.bfloat16)
            to_chip(k).start()

    def join():
        for k in range(dense):
            to_core(k, 0).wait_recv()
            own_block(k, 0).wait()
            to_chip(k).wait_recv()
            to_chip(k).wait_send()
            for part in (0, 1):
                to_core(k, part).wait_send()
            rows = joined[k].shape[1]
            for j in range(count):
                if j * rows < own[k].shape[1]:
                    cut = slice(j * rows, (j + 1) * rows)
                    joined[k][j] = (
                        own[k][0, cut].astype(jnp.float32)
                        + near[k][0, cut].astype(jnp.float32)
                        + far[k][cut].astype(jnp.float32)
                    ).astype(jnp.bfloat16)
                else:
                    joined[k][j] = jnp.zeros(joined[k].shape[1:], jnp.bfloat16)

    early_streams = [(index, way) for index in range(many) for way in (0, 1)]
    late_streams = [(index, way) for index in range(many, total) for way in (0, 1)]
    for k in range(dense):
        for part in (1, 0):
            to_core(k, part).start()
            own_block(k, part).start()
    begin(early_streams)
    ends = sorted({0, 1, lag, count - 1, hops, lag + count - 1, lag + hops})
    for low, high in zip(ends[:-1], ends[1:]):
        if low == 1:
            send_far()
        if low == lag:
            join()
            begin(late_streams)

        def ticks(tick, carry, low=low):
            for streams, start in ((early_streams, 0), (late_streams, lag)):
                if start <= low < start + count - 1:
                    add_step(streams, tick - start)
                elif start + count - 1 <= low < start + hops:
                    hand_step(streams, tick - start)
            return carry

        lax.fori_loop(low, high, ticks, 0)
    for index, way in early_streams + late_streams:
        store(index, way, hops - 1).wait()


def ring_sum(late, partials):
    many, count = late.shape[:2]
    quarters = [(partial.shape[0] // 4, partial.shape[1]) for partial in partials]
    cuts = [(-(-rows // (8 * count)) * 8, columns) for rows, columns in quarters]
    shapes = [late.shape[2:]] * many + cuts
    total, dense = len(shapes), len(partials)
    halves = [(rows, columns // 2) for rows, columns in shapes]
    size = late.size + sum(partial.size for partial in partials)
    dma = pltpu.SemaphoreType.DMA
    return pl.pallas_call(
        functools.partial(ring_kernel, count, many, 5, shapes),
        out_shape=[jax.ShapeDtypeStruct(late.shape, late.dtype)]
        + [jax.ShapeDtypeStruct((count,) + cut, late.dtype) for cut in cuts],
        in_specs=[pl.BlockSpec(memory_space=pl.ANY)] * (1 + dense),
        out_specs=[pl.BlockSpec(memory_space=pl.ANY)] * (1 + dense),
        scratch_shapes=[pltpu.VMEM((2, SLOTS) + half, jnp.bfloat16) for half in halves]
        + [pltpu.VMEM((2, 2) + half, jnp.bfloat16) for half in halves]
        + [pltpu.VMEM((2,) + quarter, jnp.bfloat16) for quarter in quarters]
        + [pltpu.VMEM((2,) + quarter, jnp.bfloat16) for quarter in quarters]
        + [pltpu.VMEM(quarter, jnp.bfloat16) for quarter in quarters]
        + [pltpu.VMEM((count,) + cut, jnp.bfloat16) for cut in cuts]
        + [
            dma((2 * total, SLOTS)),
            dma((2 * total, SLOTS)),
            dma((2 * total, 2)),
            dma((2 * total, SLOTS)),
            dma((dense, 2)),
            dma((dense, 2)),
            dma((dense, 2)),
            dma((dense,)),
            dma((dense,)),
            pltpu.SemaphoreType.REGULAR((2 * total,)),
        ],
        compiler_params=pltpu.CompilerParams(
            collective_id=0, has_side_effects=True, vmem_limit_bytes=VMEM_BYTES
        ),
        cost_estimate=pl.CostEstimate(flops=2 * size, bytes_accessed=8 * size, transcendentals=0),
        name="ring_sum",
    )(late, *partials)


def finish_kernel(firsts, *refs):
    units, (gate, up, down) = refs[:-3], refs[-3:]
    for index, unit in enumerate(units):
        e = pl.program_id(0)

        @pl.when((e >= firsts[index]) & (e < firsts[index + 1]))
        def _():
            rows = unit.shape[2] // 3
            for k in range(unit.shape[1]):
                gate[0, k * rows : (k + 1) * rows] = unit[0, k, :rows].astype(jnp.float32)
                up[0, k * rows : (k + 1) * rows] = unit[0, k, rows : 2 * rows].astype(jnp.float32)
            turned = jnp.concatenate([unit[0, k, 2 * rows :] for k in range(unit.shape[1])], 0)
            down[0] = turned.astype(jnp.float32).T


def finish(units, width):
    count, rows3, columns = units[0].shape[1:]
    rows = rows3 // 3
    pair = count // 4
    firsts = [0]
    for unit in units:
        firsts.append(firsts[-1] + unit.shape[0])
    experts = firsts[-1]

    def place(index):
        first, end = firsts[index], firsts[index + 1]

        def chunk(e, c):
            inside = jnp.clip(e, first, end - 1)
            return (inside - first, jnp.where(e < first, 0, jnp.where(e >= end, 3, c)), 0, 0)

        return chunk

    return pl.pallas_call(
        functools.partial(finish_kernel, firsts),
        grid=(experts, 4),
        in_specs=[pl.BlockSpec((1, pair, rows3, columns), place(index)) for index in range(len(units))],
        out_specs=[
            pl.BlockSpec((1, pair * rows, columns), lambda e, c: (e, c, 0)),
            pl.BlockSpec((1, pair * rows, columns), lambda e, c: (e, c, 0)),
            pl.BlockSpec((1, columns, pair * rows), lambda e, c: (e, 0, c)),
        ],
        out_shape=[
            jax.ShapeDtypeStruct((experts, width, columns), jnp.float32),
            jax.ShapeDtypeStruct((experts, width, columns), jnp.float32),
            jax.ShapeDtypeStruct((experts, columns, width), jnp.float32),
        ],
        name="finish",
        compiler_params=pltpu.CompilerParams(vmem_limit_bytes=48 * 2**20),
    )(*units)


def swap_core(value):
    return lax.ppermute(value, "ep", [(0, 1), (1, 0), (2, 3), (3, 2)])


def swap_chip(value):
    return lax.ppermute(value, "ep", [(0, 2), (2, 0), (1, 3), (3, 1)])


def add_bf(a, b):
    return (a.astype(jnp.float32) + b.astype(jnp.float32)).astype(jnp.bfloat16)


def per_device(
    tokens,
    norm_attn,
    w_query,
    key_projection,
    value_projection,
    w_out,
    norm_ffn,
    w_router,
    w_gate,
    w_up,
    w_down,
    routes,
    cotangent,
):
    token_count, width = tokens.shape
    experts_all = w_router.shape[1]
    holder = lax.axis_index("ep")
    held = w_gate.shape[0]
    replicas = lax.axis_size("rep")
    cot_near = (cotangent, swap_core(cotangent))
    cot_far = swap_chip(cotangent)
    cosine, sine = rope_tables(token_count)
    normed, queries, keys, values, log_totals, attn, resid, h_two, probs, combine = attention_forward(
        tokens, norm_attn, w_query, key_projection, value_projection, cosine, sine, w_out, norm_ffn, w_router, routes
    )
    h_two, combine, cot_far = lax.optimization_barrier((h_two, combine, cot_far))
    chosen = jnp.max((routes[:, :, None] == jnp.arange(experts_all)[None, None, :]).astype(jnp.float32), 1)

    def own_columns(block):
        return lax.dynamic_slice_in_dim(block, holder * held, held, 1)

    h_near = (h_two, swap_core(h_two))
    gates_near = (own_columns(combine), own_columns(swap_core(combine)))
    h_far, gates_far = swap_chip(h_two), swap_chip(combine)
    near = expert_pass(h_near, cot_near, gates_near, w_gate, w_up, w_down)
    near, h_far, gates_far = lax.optimization_barrier((near, h_far, gates_far))
    h_far = (h_far, swap_core(h_far))
    cot_far = (cot_far, swap_core(cot_far))
    gates_far = (own_columns(gates_far), own_columns(swap_core(gates_far)))
    far = expert_pass(h_far, cot_far, gates_far, w_gate, w_up, w_down)
    ghs, dgs, dus = zip(near[:3], far[:3])
    hs, cots = h_near + h_far, cot_near + cot_far

    def widen(block):
        return lax.dynamic_update_slice_in_dim(
            jnp.zeros((block.shape[0], experts_all), jnp.float32), block, holder * held, 1
        )

    router_near = widen(near[3]) + swap_core(widen(near[4]))
    d_router = chosen * (router_near + swap_chip(widen(far[3]) + swap_core(widen(far[4]))))
    dh_far, other = sum_over_experts([dgs[1], dus[1]], [w_gate, w_up], 1)
    dh_far = swap_chip(add_bf(dh_far, swap_core(other)))
    dh_own, other = sum_over_experts([dgs[0], dus[0]], [w_gate, w_up], 1)
    dh_near = swap_core(other)
    ghs, dh_own = lax.optimization_barrier((ghs, dh_own))
    early = weight_grads(replicas, 0, EARLY, hs, cots, ghs, dgs, dus)
    y_far, other = sum_over_experts([ghs[1]], [w_down], 0)
    y_far = swap_chip(add_bf(y_far, swap_core(other)))
    early, y_far_started, dh_far = lax.optimization_barrier((early, other, dh_far))
    early = [lax.psum_scatter(early[e], "rep", scatter_dimension=0, tiled=True) for e in range(EARLY)]
    d_resid, d_pre, grad_out = attention_back(
        dh_own, dh_near, dh_far, d_router, probs, resid, norm_ffn, cotangent, w_router, w_out, h_two, attn,
        queries, keys, values, log_totals, cosine, sine,
    )
    d_input, grad_qkv = input_back(
        d_pre, normed, tokens, norm_attn, d_resid, w_query, key_projection, value_projection
    )
    ghs, grad_qkv = lax.optimization_barrier((ghs, grad_qkv))
    late = weight_grads(replicas, EARLY, held - EARLY, hs, cots, ghs, dgs, dus)
    y_own, other = sum_over_experts([ghs[0]], [w_down], 0)
    mixed = (
        resid
        + y_own.astype(jnp.float32)
        + swap_core(other).astype(jnp.float32)
        + y_far.astype(jnp.float32)
    ).astype(jnp.bfloat16)
    early, late, mixed = lax.optimization_barrier((early, late, mixed))
    early = jnp.stack([lax.all_gather(part, "rep", axis=0, tiled=True) for part in early])
    late, sum_o, sum_qkv = ring_sum(late, [grad_out, grad_qkv])
    key_width = key_projection.shape[1]
    sum_o, sum_qkv = (
        total.reshape(-1, total.shape[2])[: width // 4].astype(jnp.float32) for total in (sum_o, sum_qkv)
    )
    sum_o, sum_r, sum_nf = (
        sum_o[:, :width], sum_o[:, width : width + experts_all], sum_o[:, width + LANES]
    )
    sum_q, sum_k, sum_v, sum_na = jnp.split(
        sum_qkv[:, : width + 2 * key_width + 1], [width, width + key_width, width + 2 * key_width], 1
    )
    sum_na = sum_na[:, 0]
    full_gate, full_up, full_down = finish([early, late], width)
    return (
        mixed,
        d_input,
        sum_na,
        sum_q,
        sum_k,
        sum_v,
        sum_o,
        sum_nf,
        sum_r,
        full_gate,
        full_up,
        full_down,
    )


def solution(mesh):
    placed = (
        P(("rep", "ep"), None),
        P(),
        P(),
        P(),
        P(),
        P(),
        P(),
        P(),
        P("ep", None, None),
        P("ep", None, None),
        P("ep", None, None),
        P(("rep", "ep"), None),
        P(("rep", "ep"), None),
    )
    return jax.shard_map(
        per_device,
        mesh=mesh,
        in_specs=placed,
        out_specs=(
            P(("rep", "ep"), None),
            P(("rep", "ep"), None),
            P("ep"),
            P("ep", None),
            P("ep", None),
            P("ep", None),
            P("ep", None),
            P("ep"),
            P("ep", None),
            P("ep", None, None),
            P("ep", None, None),
            P("ep", None, None),
        ),
        check_vma=False,
    )
```

time: 1210 us -> 922 us (0.76)
  Pallas kernels: 360 us -> 824 us
  matrix products: 442 us -> 0 us
  waiting for transfers between devices: 187 us -> 11.2 us
  other arithmetic: 80.8 us -> 13.7 us
  local copies, waits for them, and re-layouts: 106 us -> 38.9 us
    pallas_call x2 -> x13, Pallas kernels: 360 us -> 824 us  [the longest x1 488 us: ring_sum(): pl.pallas_call(functools.partial(ring_kernel, count, many, 5, shapes), ou...]
    dot_general x66 -> x0, matrix products: 442 us -> none  [the longest x5 62.9 us: per_device(): jnp.einsum('tf,df->td', du_list[e], w_up[e], preferred_element_type=jnp.f...]
    ppermute x8 -> x6, waiting for transfers between devices: 184 us -> 8.72 us  [swap_chip(): return lax.ppermute(value, 'ep', [(0, 2), (2, 0), (1, 3), (3, 1)])]
    convert_element_type x10 -> x4, other arithmetic: 28.7 us -> 3.9 us  [the longest x1 1.96 us: per_device(): mixed = (resid + y_own.astype(jnp.float32) + swap_core(other).astype(jnp....]
    concatenate x5 -> x0, local copies, waits for them, and re-layouts: 23.3 us -> none  [the longest x2 13.9 us: per_device(): jnp.concatenate([grad_query, grad_key, grad_value, grad_norm_attn[:, None...]
    concatenate x8 -> x1, other arithmetic: 18 us -> 1.25 us  [rope_tables(): jnp.concatenate([cosine] * 4, 1)]
    reshape x5 -> x0, local copies, waits for them, and re-layouts: 15.8 us -> none  [per_device(): down_grad.astype(jnp.bfloat16)]
    unnamed x290 -> x37, local copies, waits for them, and re-layouts: 29.2 us -> 14 us
  transfers between devices with their start and end apart: 28 -> 20, of which waited for: 7 -> 4; matrix products, arithmetic and copies ran while one was open for 28% -> 5% of each run, Pallas kernels for 28% -> 81%
where the time goes in v3:
time: 922 us; the launch traced here: 912 us
  Pallas kernels  824 us (89%)
  local copies, waits for them, and re-layouts  38.9 us (4%)
  between operations  14.7 us (2%)
  other arithmetic  13.7 us (1%)
  waiting for transfers between devices  11.2 us (1%)
  starting transfers between devices  9.62 us (1%)
    pallas_call x1, Pallas kernels, ring_sum(): pl.pallas_call(functools.partial(ring_kernel, count, many, 5, shapes), ou...  488 us
    pallas_call x4, Pallas kernels, sum_over_experts(): pl.pallas_call(functools.partial(sum_kernel, right_dim, len(lefts)), grid...  81 us
    pallas_call x2, Pallas kernels, weight_grads(): pl.pallas_call(weight_kernel, grid=(many, 3), in_specs=[whole(hs[0])] * 8...  68.8 us
    pallas_call x2, Pallas kernels, expert_pass(): pl.pallas_call(functools.partial(expert_kernel, 256), grid=(held,), in_sp...  68.3 us
    pallas_call x1, Pallas kernels, attention_back(): pl.pallas_call(attention_back_kernel, out_shape=[shape((count, width), jn...  40.9 us
    pallas_call x1, Pallas kernels, attention_forward(): pl.pallas_call(attention_kernel, out_shape=[shape((count, width), jnp.bfl...  32.9 us
    pallas_call x1, Pallas kernels, finish(): pl.pallas_call(functools.partial(finish_kernel, firsts), grid=(experts, 4...  25.5 us
    pallas_call x1, Pallas kernels, input_back(): pl.pallas_call(input_kernel, out_shape=[shape((count, width), jnp.float32...  18.6 us
  transfers between devices with their start and end apart: 20, of which 4 were waited for; matrix products, arithmetic and copies ran while one was open for 5% of the time, Pallas kernels for 81%

profile of v3, /device:TPU:0, one launch (start us, length us, event | category | flops | bytes accessed | tf_op | source)
XLA Modules:
  0.0 912.3 jit_solution(6757252692366871750)
XLA Ops:
  7.2 3.0 collective-permute-start
  18.6 32.9 %attention_forward.1 = (bf16[512,1536]{1,0:T(8,128)(2,1)}, bf16[512,1536]{1,0:T(8,128)(2,1)}, bf16[512,512]{1,0:T(8,128)(2,1)}, bf16[512,512]{1,0:T(8,128)(2,1)}...) custom-call(bf16[512,1536]{1,0:T(8,128)(2,1)} %tokens.3, ...), custom_call_target="tpu_custom_call" | custom-call | flops 7247757312 | bytes 18874368 | tf_op jit(solution)/shard_map/attention_forward/pallas_call | solution.py:278
  58.1 34.3 %expert_pass.2 = (bf16[5,1024,512]{2,1,0:T(8,128)(2,1)}, bf16[5,1024,512]{2,1,0:T(8,128)(2,1)}, bf16[5,1024,512]{2,1,0:T(8,128)(2,1)}, f32[512,5]{1,0:T(8,128)}, f32[512,5]{1,0:T(8,128)}) custom-call(bf16[512,1536]{1,0:T(8,128)(2,1)} %get-tuple-element.74.h0.refs_0_.h_two, bf16[512,1536]{1,0:T(8,128)(2,1)} %collective-permute-done.1.h1.refs_1_, ...), custom_call_target="tpu_custom_call" | custom-call | flops 24159191040 | bytes 23592960 | tf_op jit(solution)/shard_map/expert_pass/pallas_call | solution.py:97
  95.6 2.4 collective-permute-done.8
  101.2 34.1 %expert_pass.3 = (bf16[5,1024,512]{2,1,0:T(8,128)(2,1)}, bf16[5,1024,512]{2,1,0:T(8,128)(2,1)}, bf16[5,1024,512]{2,1,0:T(8,128)(2,1)}, f32[512,5]{1,0:T(8,128)}, f32[512,5]{1,0:T(8,128)}) custom-call(bf16[512,1536]{1,0:T(8,128)(2,1)} %copy-done.8, bf16[512,1536]{1,0:T(8,128)(2,1)} %copy-done.10, bf16[512,1536]{1,0:T(8,128)(2,1)} %copy-done.6, ...), custom_call_target="tpu_custom_call" | custom-call | flops 24159191040 | bytes 23592960 | tf_op jit(solution)/shard_map/expert_pass/pallas_call | solution.py:97
  135.3 25.1 %sum_over_experts.6 = (bf16[512,1536]{1,0:T(8,128)(2,1)}, bf16[512,1536]{1,0:T(8,128)(2,1)}) custom-call(bf16[5,1024,512]{2,1,0:T(8,128)(2,1)} %get-tuple-element.91.refs_11_.refs_0_, bf16[5,1024,512]{2,1,0:T(8,128)(2,1)} %get-tuple-element.92.refs_13_.refs_1_, bf16[5,1536,512]{2,1,0:T(8,128)(2,1)} %refs_2_.3, bf16[5,1536,512]{2,1,0:T(8,128)(2,1)} %refs_3_.3), custom_call_target="tpu_custom_call" | custom-call | flops 16106127360 | bytes 26214400 | tf_op jit(solution)/shard_map/sum_over_experts/pallas_call | solution.py:176
  160.6 24.8 %sum_over_experts.4 = (bf16[512,1536]{1,0:T(8,128)(2,1)}, bf16[512,1536]{1,0:T(8,128)(2,1)}) custom-call(bf16[5,1024,512]{2,1,0:T(8,128)(2,1)} %get-tuple-element.86.refs_0_.refs_10_, bf16[5,1024,512]{2,1,0:T(8,128)(2,1)} %get-tuple-element.87.refs_1_.refs_12_, bf16[5,1536,512]{2,1,0:T(8,128)(2,1)} %refs_2_.3, bf16[5,1536,512]{2,1,0:T(8,128)(2,1)} %refs_3_.3), custom_call_target="tpu_custom_call" | custom-call | flops 16106127360 | bytes 26214400 | tf_op jit(solution)/shard_map/sum_over_experts/pallas_call | solution.py:176
  186.1 15.4 %sum_over_experts.5 = (bf16[512,1536]{1,0:T(8,128)(2,1)}, bf16[512,1536]{1,0:T(8,128)(2,1)}) custom-call(bf16[5,1024,512]{2,1,0:T(8,128)(2,1)} %get-tuple-element.116.refs_9_.refs_0_, bf16[5,512,1536]{2,1,0:T(8,128)(2,1)} %refs_1_.3), custom_call_target="tpu_custom_call" | custom-call | flops 8053063680 | bytes 13107200 | tf_op jit(solution)/shard_map/sum_over_experts/pallas_call | solution.py:176
  201.6 18.3 %weight_grads.2 = bf16[1,8,3,192,512]{4,3,2,1,0:T(8,128)(2,1)} custom-call(bf16[512,1536]{1,0:T(8,128)(2,1)} %get-tuple-element.74.h0.refs_0_.h_two, bf16[512,1536]{1,0:T(8,128)(2,1)} %collective-permute-done.1.h1.refs_1_, bf16[512,1536]{1,0:T(8,128)(2,1)} %copy-done.8, bf16[512,1536]{1,0:T(8,128)(2,1)} %copy-done.10, bf16[512,1536]{1,0:T(8,128)(2,1)} %refs_4_.3, ...), custom_call_target="tpu_custom_call" | custom-call | flops 9663676416 | bytes 11010048 | tf_op jit(solution)/shard_map/weight_grads/pallas_call | solution.py:136
  219.8 2.7 collective-permute-done.10.dh_far
  230.3 1.9 dynamic-slice_add_fusion
  234.8 1.9 dynamic-slice_add_fusion.1
  236.7 1.9 add.67
  238.6 4.2 collective-permute-done.14
  246.7 40.9 %attention_back.1 = (f32[512,1536]{1,0:T(8,128)}, bf16[512,2560]{1,0:T(8,128)(2,1)}, bf16[1536,1792]{1,0:T(8,128)(2,1)}) custom-call(bf16[512,1536]{1,0:T(8,128)(2,1)} %get-tuple-element.97.dh_own, bf16[512,1536]{1,0:T(8,128)(2,1)} %collective-permute-done.11.dh_near, bf16[512,1536]{1,0:T(8,128)(2,1)} %copy-done.16, f32[512,20]{1,0:T(8,128)} %add_multiply_fusion.d_router, ...), custom_call_target="tpu_custom_call" | custom-call | flops 12079595520 | bytes 18874368 | tf_op jit(solution)/shard_map/attention_back/pallas_call | solution.py:385
  287.6 18.6 %input_back.1 = (f32[512,1536]{1,0:T(8,128)}, bf16[1536,2816]{1,0:T(8,128)(2,1)}) custom-call(bf16[512,2560]{1,0:T(8,128)(2,1)} %get-tuple-element.111.d_pre, bf16[512,1536]{1,0:T(8,128)(2,1)} %get-tuple-element.112.normed, bf16[512,1536]{1,0:T(8,128)(2,1)} %tokens.3, bf16[1,1536]{1,0:T(2,128)(2,1)} %broadcast_in_dim.4.norm_attn, ...), custom_call_target="tpu_custom_call" | custom-call | flops 9663676416 | bytes 28311552 | tf_op jit(solution)/shard_map/input_back/pallas_call | solution.py:432
  306.2 15.6 %sum_over_experts.7 = (bf16[512,1536]{1,0:T(8,128)(2,1)}, bf16[512,1536]{1,0:T(8,128)(2,1)}) custom-call(bf16[5,1024,512]{2,1,0:T(8,128)(2,1)} %get-tuple-element.115.refs_8_.refs_0_, bf16[5,512,1536]{2,1,0:T(8,128)(2,1)} %refs_1_.3), custom_call_target="tpu_custom_call" | custom-call | flops 8053063680 | bytes 13107200 | tf_op jit(solution)/shard_map/sum_over_experts/pallas_call | solution.py:176
  321.8 50.5 %weight_grads.3 = bf16[4,8,3,192,512]{4,3,2,1,0:T(8,128)(2,1)} custom-call(bf16[512,1536]{1,0:T(8,128)(2,1)} %get-tuple-element.74.h0.refs_0_.h_two, bf16[512,1536]{1,0:T(8,128)(2,1)} %collective-permute-done.1.h1.refs_1_, bf16[512,1536]{1,0:T(8,128)(2,1)} %copy-done.8, bf16[512,1536]{1,0:T(8,128)(2,1)} %copy-done.10, bf16[512,1536]{1,0:T(8,128)(2,1)} %refs_4_.3, ...), custom_call_target="tpu_custom_call" | custom-call | flops 38654705664 | bytes 44040192 | tf_op jit(solution)/shard_map/weight_grads/pallas_call | solution.py:136
  372.4 2.0 add_convert_fusion
  374.4 488.1 %ring_sum.1 = (bf16[4,8,576,512]{3,2,1,0:T(8,128)(2,1)}, bf16[8,48,1792]{2,1,0:T(8,128)(2,1)}, bf16[8,48,2816]{2,1,0:T(8,128)(2,1)}) custom-call(bf16[4,8,576,512]{3,2,1,0:T(8,128)(2,1)} %bitcast.12, bf16[1536,1792]{1,0:T(8,128)(2,1)} %get-tuple-element.123.refs_1_, bf16[1536,2816]{1,0:T(8,128)(2,1)} %get-tuple-element.124.refs_2_), custom_call_target="tpu_custom_call" | custom-call | flops 33030144 | bytes 132120576 | tf_op jit(solution)/shard_map/ring_sum/pallas_call | solution.py:688
  867.7 2.0 copy-done.1
  874.6 2.6 fusion.5
  877.2 2.3 copy-done
  879.5 25.5 %finish.1 = (f32[5,1536,512]{2,1,0:T(8,128)}, f32[5,1536,512]{2,1,0:T(8,128)}, f32[5,512,1536]{2,1,0:T(8,128)}) custom-call(bf16[1,8,576,512]{3,2,1,0:T(8,128)(2,1)S(1)} %bitcast.10, bf16[4,8,576,512]{3,2,1,0:T(8,128)(2,1)} %get-tuple-element.128.refs_1_), custom_call_target="tpu_custom_call" | custom-call | tf_op jit(solution)/shard_map/finish/pallas_call | solution.py:753
  (102 shorter events, 46.5 us)
Async XLA Ops:
  7.2 367.2 %reduce-scatter.2.cloned.1.call-start = ((), (), s32[]{:S(2)}) async-start(), calls=%async_computation.1 | async-start | bytes 5308416 | tf_op jit(solution)/shard_map/reduce_scatter | solution.py:844
  7.2 44.3 %collective-permute-start = (bf16[512,1536]{1,0:T(8,128)(2,1)}, bf16[512,1536]{1,0:T(8,128)(2,1)S(1)}, u32[]{:S(2)}, u32[]{:S(2)}) collective-permute-start(bf16[512,1536]{1,0:T(8,128)(2,1)} %refs_4_.3), channel_id=1, source_target_pairs={{0,2},{2,0},{1,3},{3,1},{4,6},{6,4},{5,7},{7,5},{8,10},{10,8},{9,1... | collective-permute-start | bytes 4718600 | tf_op jit(solution)/shard_map/ppermute | solution.py:777
  10.2 46.7 %collective-permute-start.2 = (bf16[512,1536]{1,0:T(8,128)(2,1)}, bf16[512,1536]{1,0:T(8,128)(2,1)S(1)}, u32[]{:S(2)}, u32[]{:S(2)}) collective-permute-start(bf16[512,1536]{1,0:T(8,128)(2,1)} %refs_4_.3), channel_id=1, source_target_pairs={{0,1},{1,0},{2,3},{3,2},{4,5},{5,4},{6,7},{7,6},{8,9},{9,8},{10,11... | collective-permute-start | bytes 4718600 | tf_op jit(solution)/shard_map/ppermute | solution.py:773
  51.5 40.9 %copy-start.6 = (bf16[512,1536]{1,0:T(8,128)(2,1)}, bf16[512,1536]{1,0:T(8,128)(2,1)S(1)}, u32[]{:S(2)}) copy-start(bf16[512,1536]{1,0:T(8,128)(2,1)S(1)} %collective-permute-done.c0.refs_6_) | copy-start | bytes 4718596
  51.5 5.5 collective-permute-start.1
  52.1 40.3 %collective-permute-start.5 = (f32[512,20]{1,0:T(8,128)}, f32[512,20]{1,0:T(8,128)S(1)}, u32[]{:S(2)}, u32[]{:S(2)}) collective-permute-start(f32[512,20]{1,0:T(8,128)} %get-tuple-element.75), channel_id=1, source_target_pairs={{0,2},{2,0},{1,3},{3,1},{4,6},{6,4},{5,7},{7,5},{8,10},{10,8},{9,1... | collective-permute-start | bytes 122888 | tf_op jit(solution)/shard_map/ppermute | solution.py:777
  52.1 3.8 collective-permute-start.3
  52.2 42.0 %collective-permute-start.4 = (bf16[512,1536]{1,0:T(8,128)(2,1)}, bf16[512,1536]{1,0:T(8,128)(2,1)S(1)}, u32[]{:S(2)}, u32[]{:S(2)}) collective-permute-start(bf16[512,1536]{1,0:T(8,128)(2,1)} %get-tuple-element.74.h0.refs_0_.h_two), channel_id=1, source_target_pairs={{0,2},{2,0},{1,3},{3,1},{4,6},{6,4},{5,7},{7,5},{8,10},{10,8},{9,1... | collective-permute-start | bytes 4718600 | tf_op jit(solution)/shard_map/ppermute | solution.py:777
  55.9 43.0 %collective-permute-start.7 = (bf16[512,1536]{1,0:T(8,128)(2,1)S(1)}, bf16[512,1536]{1,0:T(8,128)(2,1)S(1)}, u32[]{:S(2)}, u32[]{:S(2)}) collective-permute-start(bf16[512,1536]{1,0:T(8,128)(2,1)S(1)} %collective-permute-done.c0.refs_6_), channel_id=1, source_target_pairs={{0,1},{1,0},{2,3},{3,2},{4,5},{5,4},{6,7},{7,6},{8,9},{9,8},{10,11... | collective-permute-start | bytes 4718600 | tf_op jit(solution)/shard_map/ppermute | solution.py:773
  94.3 4.6 collective-permute-start.6
  94.3 3.8 collective-permute-start.8
  160.4 24.9 %copy-start.13 = (bf16[512,1536]{1,0:T(8,128)(2,1)S(1)}, bf16[512,1536]{1,0:T(8,128)(2,1)}, u32[]{:S(2)}) copy-start(bf16[512,1536]{1,0:T(8,128)(2,1)} %get-tuple-element.94) | copy-start | bytes 4718596
  160.4 24.9 %collective-permute-start.9 = (bf16[512,1536]{1,0:T(8,128)(2,1)}, bf16[512,1536]{1,0:T(8,128)(2,1)S(1)}, u32[]{:S(2)}, u32[]{:S(2)}) collective-permute-start(bf16[512,1536]{1,0:T(8,128)(2,1)} %get-tuple-element.95), channel_id=1, source_target_pairs={{0,1},{1,0},{2,3},{3,2},{4,5},{5,4},{6,7},{7,6},{8,9},{9,8},{10,11... | collective-permute-start | bytes 4718600 | tf_op jit(solution)/shard_map/ppermute | solution.py:773
  185.8 36.7 %collective-permute-start.10 = (bf16[512,1536]{1,0:T(8,128)(2,1)S(1)}, bf16[512,1536]{1,0:T(8,128)(2,1)S(1)}, u32[]{:S(2)}, u32[]{:S(2)}) collective-permute-start(bf16[512,1536]{1,0:T(8,128)(2,1)S(1)} %add_convert_fusion.2), channel_id=1, source_target_pairs={{0,2},{2,0},{1,3},{3,1},{4,6},{6,4},{5,7},{7,5},{8,10},{10,8},{9,1... | collective-permute-start | bytes 4718600 | tf_op jit(solution)/shard_map/ppermute | solution.py:777
  223.8 653.4 %all-gather.2.cloned.1.call-start = ((), (), s32[]{:S(2)}) async-start(), calls=%async_computation.2 | async-start | bytes 5308416 | tf_op jit(solution)/shard_map/all_gather | solution.py:862
  223.8 20.8 %collective-permute-start.16 = (bf16[512,1536]{1,0:T(8,128)(2,1)}, bf16[512,1536]{1,0:T(8,128)(2,1)S(1)}, u32[]{:S(2)}, u32[]{:S(2)}) collective-permute-start(bf16[512,1536]{1,0:T(8,128)(2,1)} %get-tuple-element.93), channel_id=1, source_target_pairs={{0,1},{1,0},{2,3},{3,2},{4,5},{5,4},{6,7},{7,6},{8,9},{9,8},{10,11... | collective-permute-start | bytes 4718600 | tf_op jit(solution)/shard_map/ppermute | solution.py:773
  223.9 22.8 %collective-permute-start.11 = (bf16[512,1536]{1,0:T(8,128)(2,1)}, bf16[512,1536]{1,0:T(8,128)(2,1)}, u32[]{:S(2)}, u32[]{:S(2)}) collective-permute-start(bf16[512,1536]{1,0:T(8,128)(2,1)} %get-tuple-element.98), channel_id=1, source_target_pairs={{0,1},{1,0},{2,3},{3,2},{4,5},{5,4},{6,7},{7,6},{8,9},{9,8},{10,11... | collective-permute-start | bytes 4718600 | tf_op jit(solution)/shard_map/ppermute | solution.py:773
  226.8 3.5 collective-permute-start.13
  229.9 4.9 collective-permute-start.12
  234.0 8.8 collective-permute-start.14
  246.1 126.2 %collective-permute-start.17 = (bf16[512,1536]{1,0:T(8,128)(2,1)}, bf16[512,1536]{1,0:T(8,128)(2,1)S(1)}, u32[]{:S(2)}, u32[]{:S(2)}) collective-permute-start(bf16[512,1536]{1,0:T(8,128)(2,1)} %add_convert_fusion.1), channel_id=1, source_target_pairs={{0,2},{2,0},{1,3},{3,1},{4,6},{6,4},{5,7},{7,5},{8,10},{10,8},{9,1... | collective-permute-start | bytes 4718600 | tf_op jit(solution)/shard_map/ppermute | solution.py:777
  321.8 50.6 %copy-start.4 = (f32[512,1536]{1,0:T(8,128)S(1)}, f32[512,1536]{1,0:T(8,128)}, u32[]{:S(2)}) copy-start(f32[512,1536]{1,0:T(8,128)} %get-tuple-element.105.resid) | copy-start | bytes 9437188
  321.8 50.6 %copy-start.11 = (bf16[512,1536]{1,0:T(8,128)(2,1)S(1)}, bf16[512,1536]{1,0:T(8,128)(2,1)}, u32[]{:S(2)}) copy-start(bf16[512,1536]{1,0:T(8,128)(2,1)} %get-tuple-element.117) | copy-start | bytes 4718596
  321.8 50.5 %collective-permute-start.15 = (bf16[512,1536]{1,0:T(8,128)(2,1)}, bf16[512,1536]{1,0:T(8,128)(2,1)S(1)}, u32[]{:S(2)}, u32[]{:S(2)}) collective-permute-start(bf16[512,1536]{1,0:T(8,128)(2,1)} %get-tuple-element.118), channel_id=1, source_target_pairs={{0,1},{1,0},{2,3},{3,2},{4,5},{5,4},{6,7},{7,6},{8,9},{9,8},{10,11... | collective-permute-start | bytes 4718600 | tf_op jit(solution)/shard_map/ppermute | solution.py:773
  (14 other events, 47.4 us)
Sparse Core Ops, SparseCore 0:
  223.9 95.5 reduce-scatter.1
  374.5 132.5 all-gather.1

commit v4 on v3

--- a/solution.py
+++ b/solution.py
@@ -55,6 +55,7 @@
 def expert_kernel(tile, h0, h1, c0, c1, gates0, gates1, w_gate, w_up, w_down, gh, dg, du, d_router0, d_router1):
     e = pl.program_id(0)
     tokens, lanes = gates0.shape
+    expert = lax.axis_index("ep") * pl.num_programs(0) + e
     lane = lax.broadcasted_iota(jnp.int32, (tile, lanes), 1)
 
     @pl.when(e == 0)
@@ -73,12 +74,12 @@
             gate_pre = contract(entries, w_gate[0], 1, 0)
             up_pre = contract(entries, w_up[0], 1, 0)
             back = contract(rows_c[rows, :], w_down[0], 1, 1)
-            column = jnp.sum(jnp.where(lane == e, gates[rows, :], 0.0), 1, keepdims=True)
+            column = jnp.sum(jnp.where(lane == expert, gates[rows, :], 0.0), 1, keepdims=True)
             sigma = jax.nn.sigmoid(gate_pre)
             swish = gate_pre * sigma
             hidden = (swish * up_pre).astype(jnp.bfloat16).astype(jnp.float32)
             d_router[rows, :] = jnp.where(
-                lane == e, jnp.sum(hidden * back, 1, keepdims=True), d_router[rows, :]
+                lane == expert, jnp.sum(hidden * back, 1, keepdims=True), d_router[rows, :]
             )
             d_hidden = column * back
             dg[0, out, :] = (
@@ -211,6 +212,15 @@
         ],
         0,
     )
+
+
+def chosen_of(routes, shape):
+    expert = lax.broadcasted_iota(jnp.int32, shape, 1)
+    picks = routes[...].T
+    chosen = picks[:, :1] == expert
+    for k in range(1, picks.shape[1]):
+        chosen = chosen | (picks[:, k : k + 1] == expert)
+    return chosen
 
 
 def attention_kernel(
@@ -253,17 +263,11 @@
     inverse = lax.rsqrt(jnp.mean(total * total, -1, keepdims=True) + epsilon)
     second = (total * inverse * norm_ffn[...].astype(jnp.float32)).astype(jnp.bfloat16)
     h_two[...] = second
-    logits = contract(second, w_router[...], 1, 0)
-    lane = lax.broadcasted_iota(jnp.int32, logits.shape, 1)
-    experts = probs.shape[1]
-    logits = jnp.where(lane < experts, logits, masked_value)
+    logits = contract(second, w_router[...], 1, 1)
     shifted = jnp.exp(logits - jnp.max(logits, -1, keepdims=True))
     soft = shifted / jnp.sum(shifted, -1, keepdims=True)
-    chosen = jnp.zeros(logits.shape, jnp.bool_)
-    for k in range(routes.shape[1]):
-        chosen = chosen | (routes[:, k : k + 1] == lane)
-    probs[...] = soft[:, :experts]
-    combine[...] = jnp.where(chosen, soft, 0.0)[:, :experts]
+    probs[...] = soft
+    combine[...] = jnp.where(chosen_of(routes, logits.shape), soft, 0.0)
 
 
 LANES = 128
@@ -272,7 +276,6 @@
 def attention_forward(tokens, norm_attn, w_query, w_key, w_value, cosine, sine, w_out, norm_ffn, w_router, routes):
     count, width = tokens.shape
     experts = w_router.shape[1]
-    wide_router = jnp.pad(w_router, ((0, 0), (0, LANES - experts)))
     key_width = w_key.shape[1]
     shape = jax.ShapeDtypeStruct
     return pl.pallas_call(
@@ -295,7 +298,7 @@
         ),
         name="attention_forward",
     )(
-        tokens, norm_attn[None], w_query, w_key, w_value, cosine, sine, w_out, norm_ffn[None], wide_router, routes
+        tokens, norm_attn[None], w_query, w_key, w_value, cosine, sine, w_out, norm_ffn[None], w_router.T, routes.T
     )
 
 
@@ -305,21 +308,22 @@
 
 
 def attention_back_kernel(
-    dh_own, dh_near, dh_far, d_router, probs, resid, norm_ffn, cotangent, w_router, w_out, h_two, attn,
+    dh_own, dh_near, dh_far, router_own, router_near, router_far, routes, probs, resid, norm_ffn, cotangent, w_router, w_out, h_two, attn,
     queries, keys, values, log_totals, cosine, sine,
     d_resid, d_pre, grad_out, d_branch, d_attn, d_queries, d_keys, d_values,
 ):
     count, width = resid.shape
     experts = probs.shape[1]
     soft = probs[...]
-    to_router = d_router[...]
+    to_router = jnp.where(
+        chosen_of(routes, soft.shape), router_own[...] + router_near[...] + router_far[...], 0.0
+    )
     d_logits = (soft * (to_router - jnp.sum(soft * to_router, -1, keepdims=True))).astype(jnp.bfloat16)
-    d_logits = jnp.concatenate([d_logits, jnp.zeros((count, LANES - experts), jnp.bfloat16)], 1)
     d_normed = (
         dh_own[...].astype(jnp.float32)
         + dh_near[...].astype(jnp.float32)
         + dh_far[...].astype(jnp.float32)
-        + contract(d_logits, w_router[...], 1, 1)
+        + contract(d_logits, w_router[...], 1, 0)
     )
     total = resid[...]
     inverse = lax.rsqrt(jnp.mean(total * total, -1, keepdims=True) + epsilon)
@@ -331,6 +335,7 @@
     d_resid[...] = back
     d_branch[...] = back.astype(jnp.bfloat16)
     grad_out[:, :width] = contract(attn[...], d_branch[...], 0, 0).astype(jnp.bfloat16)
+    d_logits = jnp.concatenate([d_logits, jnp.zeros((count, LANES - experts), jnp.bfloat16)], 1)
     grad_out[:, width : width + LANES] = contract(h_two[...], d_logits, 0, 0).astype(jnp.bfloat16)
     grad_out[:, width + LANES :] = as_lane(jnp.sum(d_normed * normal, 0, keepdims=True))
     d_attn[...] = contract(d_branch[...], w_out[...], 1, 1).astype(jnp.bfloat16)
@@ -376,11 +381,10 @@
     d_pre[:, width + key_width :] = d_values[...].astype(jnp.bfloat16)
 
 
-def attention_back(dh_own, dh_near, dh_far, d_router, probs, resid, norm_ffn, cotangent, w_router, w_out, h_two, attn,
+def attention_back(dh_own, dh_near, dh_far, router_own, router_near, router_far, routes, probs, resid, norm_ffn, cotangent, w_router, w_out, h_two, attn,
                    queries, keys, values, log_totals, cosine, sine):
     count, width = resid.shape
     key_width = keys.shape[1]
-    wide_router = jnp.pad(w_router, ((0, 0), (0, LANES - w_router.shape[1])))
     shape = jax.ShapeDtypeStruct
     return pl.pallas_call(
         attention_back_kernel,
@@ -402,8 +406,8 @@
         ),
         name="attention_back",
     )(
-        dh_own, dh_near, dh_far, d_router, probs, resid, norm_ffn[None], cotangent, wide_router, w_out, h_two, attn,
-        queries, keys, values, log_totals, cosine, sine,
+        dh_own, dh_near, dh_far, router_own, router_near, router_far, routes.T, probs, resid, norm_ffn[None], cotangent,
+        w_router.T, w_out, h_two, attn, queries, keys, values, log_totals, cosine, sine,
     )
 
 
@@ -718,7 +722,20 @@
 
 
 def finish_kernel(firsts, *refs):
-    units, (gate, up, down) = refs[:-3], refs[-3:]
+    units, (dense_o, dense_qkv) = refs[: len(firsts) - 1], refs[len(firsts) - 1 : len(firsts) + 1]
+    gate, up, down, out, query, key, value, extra_o, extra_qkv = refs[len(firsts) + 1 :]
+
+    @pl.when((pl.program_id(0) == 0) & (pl.program_id(1) == 0))
+    def _():
+        for dense, parts in ((dense_o, (out, extra_o)), (dense_qkv, (query, key, value, extra_qkv))):
+            start = 0
+            for part in parts:
+                columns = part.shape[1]
+                rows = dense.shape[1]
+                for j in range(part.shape[0] // rows):
+                    part[j * rows : (j + 1) * rows] = dense[j, :, start : start + columns].astype(jnp.float32)
+                start += columns
+
     for index, unit in enumerate(units):
         e = pl.program_id(0)
 
@@ -732,10 +749,14 @@
             down[0] = turned.astype(jnp.float32).T
 
 
-def finish(units, width):
+def finish(units, dense, width, key_width):
     count, rows3, columns = units[0].shape[1:]
     rows = rows3 // 3
     pair = count // 4
+    small = [
+        jax.ShapeDtypeStruct((width // 4, part), jnp.float32)
+        for part in (width, width, key_width, key_width, 2 * LANES, 2 * LANES)
+    ]
     firsts = [0]
     for unit in units:
         firsts.append(firsts[-1] + unit.shape[0])
@@ -753,20 +774,23 @@
     return pl.pallas_call(
         functools.partial(finish_kernel, firsts),
         grid=(experts, 4),
-        in_specs=[pl.BlockSpec((1, pair, rows3, columns), place(index)) for index in range(len(units))],
+        in_specs=[pl.BlockSpec((1, pair, rows3, columns), place(index)) for index in range(len(units))]
+        + [whole(part) for part in dense],
         out_specs=[
             pl.BlockSpec((1, pair * rows, columns), lambda e, c: (e, c, 0)),
             pl.BlockSpec((1, pair * rows, columns), lambda e, c: (e, c, 0)),
             pl.BlockSpec((1, columns, pair * rows), lambda e, c: (e, 0, c)),
-        ],
+        ]
+        + [whole(part) for part in small],
         out_shape=[
             jax.ShapeDtypeStruct((experts, width, columns), jnp.float32),
             jax.ShapeDtypeStruct((experts, width, columns), jnp.float32),
             jax.ShapeDtypeStruct((experts, columns, width), jnp.float32),
-        ],
+        ]
+        + small,
         name="finish",
-        compiler_params=pltpu.CompilerParams(vmem_limit_bytes=48 * 2**20),
-    )(*units)
+        compiler_params=pltpu.CompilerParams(vmem_limit_bytes=VMEM_BYTES),
+    )(*units, *dense)
 
 
 def swap_core(value):
@@ -798,7 +822,6 @@
 ):
     token_count, width = tokens.shape
     experts_all = w_router.shape[1]
-    holder = lax.axis_index("ep")
     held = w_gate.shape[0]
     replicas = lax.axis_size("rep")
     cot_near = (cotangent, swap_core(cotangent))
@@ -808,44 +831,37 @@
         tokens, norm_attn, w_query, key_projection, value_projection, cosine, sine, w_out, norm_ffn, w_router, routes
     )
     h_two, combine, cot_far = lax.optimization_barrier((h_two, combine, cot_far))
-    chosen = jnp.max((routes[:, :, None] == jnp.arange(experts_all)[None, None, :]).astype(jnp.float32), 1)
-
-    def own_columns(block):
-        return lax.dynamic_slice_in_dim(block, holder * held, held, 1)
-
     h_near = (h_two, swap_core(h_two))
-    gates_near = (own_columns(combine), own_columns(swap_core(combine)))
+    gates_near = (combine, swap_core(combine))
     h_far, gates_far = swap_chip(h_two), swap_chip(combine)
     near = expert_pass(h_near, cot_near, gates_near, w_gate, w_up, w_down)
     near, h_far, gates_far = lax.optimization_barrier((near, h_far, gates_far))
     h_far = (h_far, swap_core(h_far))
     cot_far = (cot_far, swap_core(cot_far))
-    gates_far = (own_columns(gates_far), own_columns(swap_core(gates_far)))
+    gates_far = (gates_far, swap_core(gates_far))
     far = expert_pass(h_far, cot_far, gates_far, w_gate, w_up, w_down)
     ghs, dgs, dus = zip(near[:3], far[:3])
     hs, cots = h_near + h_far, cot_near + cot_far
 
-    def widen(block):
-        return lax.dynamic_update_slice_in_dim(
-            jnp.zeros((block.shape[0], experts_all), jnp.float32), block, holder * held, 1
-        )
-
-    router_near = widen(near[3]) + swap_core(widen(near[4]))
-    d_router = chosen * (router_near + swap_chip(widen(far[3]) + swap_core(widen(far[4]))))
+    router_own, router_near = near[3], swap_core(near[4])
+    router_far = swap_chip(far[3] + swap_core(far[4]))
+    early = weight_grads(replicas, 0, EARLY, hs, cots, ghs, dgs, dus)
+    dgs, early = lax.optimization_barrier((dgs, early))
+    early = [lax.psum_scatter(early[e], "rep", scatter_dimension=0, tiled=True) for e in range(EARLY)]
     dh_far, other = sum_over_experts([dgs[1], dus[1]], [w_gate, w_up], 1)
     dh_far = swap_chip(add_bf(dh_far, swap_core(other)))
     dh_own, other = sum_over_experts([dgs[0], dus[0]], [w_gate, w_up], 1)
     dh_near = swap_core(other)
     ghs, dh_own = lax.optimization_barrier((ghs, dh_own))
-    early = weight_grads(replicas, 0, EARLY, hs, cots, ghs, dgs, dus)
     y_far, other = sum_over_experts([ghs[1]], [w_down], 0)
+    dh_far, other = lax.optimization_barrier((dh_far, other))
     y_far = swap_chip(add_bf(y_far, swap_core(other)))
-    early, y_far_started, dh_far = lax.optimization_barrier((early, other, dh_far))
-    early = [lax.psum_scatter(early[e], "rep", scatter_dimension=0, tiled=True) for e in range(EARLY)]
     d_resid, d_pre, grad_out = attention_back(
-        dh_own, dh_near, dh_far, d_router, probs, resid, norm_ffn, cotangent, w_router, w_out, h_two, attn,
+        dh_own, dh_near, dh_far, router_own, router_near, router_far, routes, probs, resid, norm_ffn, cotangent, w_router, w_out, h_two, attn,
         queries, keys, values, log_totals, cosine, sine,
     )
+    early, d_pre = lax.optimization_barrier((early, d_pre))
+    early = jnp.stack([lax.all_gather(part, "rep", axis=0, tiled=True) for part in early])
     d_input, grad_qkv = input_back(
         d_pre, normed, tokens, norm_attn, d_resid, w_query, key_projection, value_projection
     )
@@ -858,21 +874,12 @@
         + swap_core(other).astype(jnp.float32)
         + y_far.astype(jnp.float32)
     ).astype(jnp.bfloat16)
-    early, late, mixed = lax.optimization_barrier((early, late, mixed))
-    early = jnp.stack([lax.all_gather(part, "rep", axis=0, tiled=True) for part in early])
+    late, mixed = lax.optimization_barrier((late, mixed))
     late, sum_o, sum_qkv = ring_sum(late, [grad_out, grad_qkv])
-    key_width = key_projection.shape[1]
-    sum_o, sum_qkv = (
-        total.reshape(-1, total.shape[2])[: width // 4].astype(jnp.float32) for total in (sum_o, sum_qkv)
-    )
-    sum_o, sum_r, sum_nf = (
-        sum_o[:, :width], sum_o[:, width : width + experts_all], sum_o[:, width + LANES]
-    )
-    sum_q, sum_k, sum_v, sum_na = jnp.split(
-        sum_qkv[:, : width + 2 * key_width + 1], [width, width + key_width, width + 2 * key_width], 1
-    )
-    sum_na = sum_na[:, 0]
-    full_gate, full_up, full_down = finish([early, late], width)
+    full_gate, full_up, full_down, sum_o, sum_q, sum_k, sum_v, extra_o, extra_qkv = finish(
+        [early, late], [sum_o, sum_qkv], width, key_projection.shape[1]
+    )
+    sum_r, sum_nf, sum_na = extra_o[:, :experts_all], extra_o[:, LANES], extra_qkv[:, 0]
     return (
         mixed,
         d_input,

time: 922 us -> 848 us (0.920)
  Pallas kernels: 824 us -> 776 us
  local copies, waits for them, and re-layouts: 38.9 us -> 12.3 us
    pallas_call x1, Pallas kernels: 488 us -> 431 us  [ring_sum(): pl.pallas_call(functools.partial(ring_kernel, count, many, 5, shapes), ou...]
    ppermute x12, waiting for transfers between devices: 2.46 us -> 14.4 us  [swap_core(): return lax.ppermute(value, 'ep', [(0, 1), (1, 0), (2, 3), (3, 2)])]
  transfers between devices with their start and end apart: 20 -> 20, of which waited for: 4 -> 6; matrix products, arithmetic and copies ran while one was open for 5% -> 1% of each run, Pallas kernels for 81% -> 83%
where the time goes in v4:
time: 848 us; the launch traced here: 839 us
  Pallas kernels  776 us (92%)
  waiting for transfers between devices  18 us (2%)
  between operations  14.8 us (2%)
  local copies, waits for them, and re-layouts  12.3 us (1%)
  starting transfers between devices  9.61 us (1%)
    pallas_call x1, Pallas kernels, ring_sum(): pl.pallas_call(functools.partial(ring_kernel, count, many, 5, shapes), ou...  431 us
    pallas_call x4, Pallas kernels, sum_over_experts(): pl.pallas_call(functools.partial(sum_kernel, right_dim, len(lefts)), grid...  80.7 us
    pallas_call x2, Pallas kernels, weight_grads(): pl.pallas_call(weight_kernel, grid=(many, 3), in_specs=[whole(hs[0])] * 8...  69.1 us
    pallas_call x2, Pallas kernels, expert_pass(): pl.pallas_call(functools.partial(expert_kernel, 256), grid=(held,), in_sp...  68.4 us
    pallas_call x1, Pallas kernels, attention_back(): pl.pallas_call(attention_back_kernel, out_shape=[shape((count, width), jn...  43.1 us
    pallas_call x1, Pallas kernels, attention_forward(): pl.pallas_call(attention_kernel, out_shape=[shape((count, width), jnp.bfl...  32.8 us
    pallas_call x1, Pallas kernels, finish(): pl.pallas_call(functools.partial(finish_kernel, firsts), grid=(experts, 4...  31.3 us
    pallas_call x1, Pallas kernels, input_back(): pl.pallas_call(input_kernel, out_shape=[shape((count, width), jnp.float32...  19.3 us
  transfers between devices with their start and end apart: 20, of which 6 were waited for; matrix products, arithmetic and copies ran while one was open for 1% of the time, Pallas kernels for 83%

profile of v4, /device:TPU:0, one launch (start us, length us, event | category | flops | bytes accessed | tf_op | source)
XLA Modules:
  0.0 838.7 jit_solution(14249512029640842255)
XLA Ops:
  7.2 3.0 collective-permute-start
  15.1 32.8 %attention_forward.1 = (bf16[512,1536]{1,0:T(8,128)(2,1)}, bf16[512,1536]{1,0:T(8,128)(2,1)}, bf16[512,512]{1,0:T(8,128)(2,1)}, bf16[512,512]{1,0:T(8,128)(2,1)}...) custom-call(bf16[512,1536]{1,0:T(8,128)(2,1)} %tokens.3, ...), custom_call_target="tpu_custom_call" | custom-call | flops 7247757312 | bytes 18874368 | tf_op jit(solution)/shard_map/attention_forward/pallas_call | solution.py:281
  48.7 2.0 collective-permute-start.5
  53.3 34.3 %expert_pass.2 = (bf16[5,1024,512]{2,1,0:T(8,128)(2,1)}, bf16[5,1024,512]{2,1,0:T(8,128)(2,1)}, bf16[5,1024,512]{2,1,0:T(8,128)(2,1)}, f32[512,20]{1,0:T(8,128)}, f32[512,20]{1,0:T(8,128)}) custom-call(bf16[512,1536]{1,0:T(8,128)(2,1)} %get-tuple-element.84.h0.refs_0_.h_two, bf16[512,1536]{1,0:T(8,128)(2,1)} %copy-done.3, bf16[512,1536]{1,0:T(8,128)(2,1)} %refs_4_.3, ...), custom_call_target="tpu_custom_call" | custom-call | flops 24159191040 | bytes 23592960 | tf_op jit(solution)/shard_map/expert_pass/pallas_call | solution.py:98
  87.6 3.6 collective-permute-done.5.gates0
  91.8 3.3 collective-permute-done.8.gates1
  96.9 34.1 %expert_pass.3 = (bf16[5,1024,512]{2,1,0:T(8,128)(2,1)}, bf16[5,1024,512]{2,1,0:T(8,128)(2,1)}, bf16[5,1024,512]{2,1,0:T(8,128)(2,1)}, f32[512,20]{1,0:T(8,128)}, f32[512,20]{1,0:T(8,128)}) custom-call(bf16[512,1536]{1,0:T(8,128)(2,1)} %copy-done.4, bf16[512,1536]{1,0:T(8,128)(2,1)} %copy-done.6, bf16[512,1536]{1,0:T(8,128)(2,1)} %copy-done.1, ...), custom_call_target="tpu_custom_call" | custom-call | flops 24159191040 | bytes 23592960 | tf_op jit(solution)/shard_map/expert_pass/pallas_call | solution.py:98
  131.0 18.5 %weight_grads.2 = bf16[1,8,3,192,512]{4,3,2,1,0:T(8,128)(2,1)} custom-call(bf16[512,1536]{1,0:T(8,128)(2,1)} %get-tuple-element.84.h0.refs_0_.h_two, bf16[512,1536]{1,0:T(8,128)(2,1)} %copy-done.3, bf16[512,1536]{1,0:T(8,128)(2,1)} %copy-done.4, bf16[512,1536]{1,0:T(8,128)(2,1)} %copy-done.6, bf16[512,1536]{1,0:T(8,128)(2,1)} %refs_4_.3, ...), custom_call_target="tpu_custom_call" | custom-call | flops 9663676416 | bytes 11010048 | tf_op jit(solution)/shard_map/weight_grads/pallas_call | solution.py:137
  149.6 24.9 %sum_over_experts.5 = (bf16[512,1536]{1,0:T(8,128)(2,1)}, bf16[512,1536]{1,0:T(8,128)(2,1)}) custom-call(bf16[5,1024,512]{2,1,0:T(8,128)(2,1)} %get-tuple-element.107.refs_11_.refs_0_, bf16[5,1024,512]{2,1,0:T(8,128)(2,1)} %get-tuple-element.99.refs_13_.refs_1_, bf16[5,1536,512]{2,1,0:T(8,128)(2,1)} %refs_2_.3, bf16[5,1536,512]{2,1,0:T(8,128)(2,1)} %refs_3_.3), custom_call_target="tpu_custom_call" | custom-call | flops 16106127360 | bytes 26214400 | tf_op jit(solution)/shard_map/sum_over_experts/pallas_call | solution.py:177
  174.6 3.5 collective-permute-done.10
  178.1 1.9 add_convert_fusion.2
  180.3 24.7 %sum_over_experts.4 = (bf16[512,1536]{1,0:T(8,128)(2,1)}, bf16[512,1536]{1,0:T(8,128)(2,1)}) custom-call(bf16[5,1024,512]{2,1,0:T(8,128)(2,1)} %get-tuple-element.100.refs_10_.refs_0_, bf16[5,1024,512]{2,1,0:T(8,128)(2,1)} %get-tuple-element.98.refs_12_.refs_1_, bf16[5,1536,512]{2,1,0:T(8,128)(2,1)} %refs_2_.3, bf16[5,1536,512]{2,1,0:T(8,128)(2,1)} %refs_3_.3), custom_call_target="tpu_custom_call" | custom-call | flops 16106127360 | bytes 26214400 | tf_op jit(solution)/shard_map/sum_over_experts/pallas_call | solution.py:177
  205.6 2.8 collective-permute-done.13
  208.5 1.9 collective-permute-start.14
  210.4 15.6 %sum_over_experts.6 = (bf16[512,1536]{1,0:T(8,128)(2,1)}, bf16[512,1536]{1,0:T(8,128)(2,1)}) custom-call(bf16[5,1024,512]{2,1,0:T(8,128)(2,1)} %get-tuple-element.129.refs_9_.refs_0_, bf16[5,512,1536]{2,1,0:T(8,128)(2,1)} %refs_1_.3), custom_call_target="tpu_custom_call" | custom-call | flops 8053063680 | bytes 13107200 | tf_op jit(solution)/shard_map/sum_over_experts/pallas_call | solution.py:177
  227.8 43.1 %attention_back.1 = (f32[512,1536]{1,0:T(8,128)}, bf16[512,2560]{1,0:T(8,128)(2,1)}, bf16[1536,1792]{1,0:T(8,128)(2,1)}) custom-call(bf16[512,1536]{1,0:T(8,128)(2,1)} %get-tuple-element.105.dh_own, bf16[512,1536]{1,0:T(8,128)(2,1)} %copy-done.11, bf16[512,1536]{1,0:T(8,128)(2,1)} %copy-done.10, f32[512,20]{1,0:T(8,128)} %get-tuple-element.112.router_own, ...), custom_call_target="tpu_custom_call" | custom-call | flops 12079595520 | bytes 18874368 | tf_op jit(solution)/shard_map/attention_back/pallas_call | solution.py:389
  271.2 3.3 collective-permute-done.16
  276.2 19.3 %input_back.1 = (f32[512,1536]{1,0:T(8,128)}, bf16[1536,2816]{1,0:T(8,128)(2,1)}) custom-call(bf16[512,2560]{1,0:T(8,128)(2,1)} %get-tuple-element.124.d_pre, bf16[512,1536]{1,0:T(8,128)(2,1)} %get-tuple-element.125.normed, bf16[512,1536]{1,0:T(8,128)(2,1)} %tokens.3, bf16[1,1536]{1,0:T(2,128)(2,1)} %broadcast_in_dim.4.norm_attn, ...), custom_call_target="tpu_custom_call" | custom-call | flops 9663676416 | bytes 28311552 | tf_op jit(solution)/shard_map/input_back/pallas_call | solution.py:436
  295.5 15.5 %sum_over_experts.7 = (bf16[512,1536]{1,0:T(8,128)(2,1)}, bf16[512,1536]{1,0:T(8,128)(2,1)}) custom-call(bf16[5,1024,512]{2,1,0:T(8,128)(2,1)} %get-tuple-element.128.refs_8_.refs_0_, bf16[5,512,1536]{2,1,0:T(8,128)(2,1)} %refs_1_.3), custom_call_target="tpu_custom_call" | custom-call | flops 8053063680 | bytes 13107200 | tf_op jit(solution)/shard_map/sum_over_experts/pallas_call | solution.py:177
  311.0 50.6 %weight_grads.3 = bf16[4,8,3,192,512]{4,3,2,1,0:T(8,128)(2,1)} custom-call(bf16[512,1536]{1,0:T(8,128)(2,1)} %get-tuple-element.84.h0.refs_0_.h_two, bf16[512,1536]{1,0:T(8,128)(2,1)} %copy-done.3, bf16[512,1536]{1,0:T(8,128)(2,1)} %copy-done.4, bf16[512,1536]{1,0:T(8,128)(2,1)} %copy-done.6, bf16[512,1536]{1,0:T(8,128)(2,1)} %refs_4_.3, ...), custom_call_target="tpu_custom_call" | custom-call | flops 38654705664 | bytes 44040192 | tf_op jit(solution)/shard_map/weight_grads/pallas_call | solution.py:137
  361.6 2.0 add_convert_fusion
  363.6 431.5 %ring_sum.1 = (bf16[4,8,576,512]{3,2,1,0:T(8,128)(2,1)}, bf16[8,48,1792]{2,1,0:T(8,128)(2,1)}, bf16[8,48,2816]{2,1,0:T(8,128)(2,1)}) custom-call(bf16[4,8,576,512]{3,2,1,0:T(8,128)(2,1)} %bitcast.7, bf16[1536,1792]{1,0:T(8,128)(2,1)} %get-tuple-element.138.refs_1_, bf16[1536,2816]{1,0:T(8,128)(2,1)} %get-tuple-element.139.refs_2_), custom_call_target="tpu_custom_call" | custom-call | flops 33030144 | bytes 132120576 | tf_op jit(solution)/shard_map/ring_sum/pallas_call | solution.py:692
  795.1 31.3 %finish.1 = (f32[5,1536,512]{2,1,0:T(8,128)}, f32[5,1536,512]{2,1,0:T(8,128)}, f32[5,512,1536]{2,1,0:T(8,128)}, f32[384,1536]{1,0:T(8,128)}, f32[384,1536]{1,0:T...) custom-call(bf16[1,8,576,512]{3,2,1,0:T(8,128)(2,1)} %bitcast.8, ...), custom_call_target="tpu_custom_call" | custom-call | tf_op jit(solution)/shard_map/finish/pallas_call | solution.py:774
  826.4 1.7 slice_reduce_fusion
  (83 shorter events, 18.9 us)
Async XLA Ops:
  7.2 263.8 %reduce-scatter.2.cloned.1.call-start = ((), (), s32[]{:S(2)}) async-start(), calls=%async_computation.1 | async-start | bytes 5308416 | tf_op jit(solution)/shard_map/reduce_scatter | solution.py:850
  7.2 40.7 %collective-permute-start = (bf16[512,1536]{1,0:T(8,128)(2,1)}, bf16[512,1536]{1,0:T(8,128)(2,1)S(1)}, u32[]{:S(2)}, u32[]{:S(2)}) collective-permute-start(bf16[512,1536]{1,0:T(8,128)(2,1)} %refs_4_.3), channel_id=1, source_target_pairs={{0,2},{2,0},{1,3},{3,1},{4,6},{6,4},{5,7},{7,5},{8,10},{10,8},{9,1... | collective-permute-start | bytes 4718600 | tf_op jit(solution)/shard_map/ppermute | solution.py:801
  10.2 40.4 %collective-permute-start.2 = (bf16[512,1536]{1,0:T(8,128)(2,1)}, bf16[512,1536]{1,0:T(8,128)(2,1)S(1)}, u32[]{:S(2)}, u32[]{:S(2)}) collective-permute-start(bf16[512,1536]{1,0:T(8,128)(2,1)} %refs_4_.3), channel_id=1, source_target_pairs={{0,1},{1,0},{2,3},{3,2},{4,5},{5,4},{6,7},{7,6},{8,9},{9,8},{10,11... | collective-permute-start | bytes 4718600 | tf_op jit(solution)/shard_map/ppermute | solution.py:797
  48.0 4.2 collective-permute-start.1
  48.5 3.6 collective-permute-start.3
  48.6 42.6 %collective-permute-start.4 = (bf16[512,1536]{1,0:T(8,128)(2,1)}, bf16[512,1536]{1,0:T(8,128)(2,1)S(1)}, u32[]{:S(2)}, u32[]{:S(2)}) collective-permute-start(bf16[512,1536]{1,0:T(8,128)(2,1)} %get-tuple-element.84.h0.refs_0_.h_two), channel_id=1, source_target_pairs={{0,2},{2,0},{1,3},{3,1},{4,6},{6,4},{5,7},{7,5},{8,10},{10,8},{9,1... | collective-permute-start | bytes 4718600 | tf_op jit(solution)/shard_map/ppermute | solution.py:801
  48.7 42.5 %collective-permute-start.5 = (f32[512,20]{1,0:T(8,128)}, f32[512,20]{1,0:T(8,128)S(1)}, u32[]{:S(2)}, u32[]{:S(2)}) collective-permute-start(f32[512,20]{1,0:T(8,128)} %get-tuple-element.85.gates0), channel_id=1, source_target_pairs={{0,2},{2,0},{1,3},{3,1},{4,6},{6,4},{5,7},{7,5},{8,10},{10,8},{9,1... | collective-permute-start | bytes 122888 | tf_op jit(solution)/shard_map/ppermute | solution.py:801
  50.7 41.1 %collective-permute-start.7 = (bf16[512,1536]{1,0:T(8,128)(2,1)S(1)}, bf16[512,1536]{1,0:T(8,128)(2,1)S(1)}, u32[]{:S(2)}, u32[]{:S(2)}) collective-permute-start(bf16[512,1536]{1,0:T(8,128)(2,1)S(1)} %collective-permute-done.c0.refs_6_), channel_id=1, source_target_pairs={{0,1},{1,0},{2,3},{3,2},{4,5},{5,4},{6,7},{7,6},{8,9},{9,8},{10,11... | collective-permute-start | bytes 4718600 | tf_op jit(solution)/shard_map/ppermute | solution.py:797
  91.2 3.9 collective-permute-start.6
  91.3 3.8 collective-permute-start.8
  149.5 645.6 %all-gather.2.cloned.1.call-start = ((), (), s32[]{:S(2)}) async-start(), calls=%async_computation.2 | async-start | bytes 5308416 | tf_op jit(solution)/shard_map/all_gather | solution.py:864
  174.5 3.6 collective-permute-start.10
  180.0 46.0 %collective-permute-start.11 = (bf16[512,1536]{1,0:T(8,128)(2,1)S(1)}, bf16[512,1536]{1,0:T(8,128)(2,1)S(1)}, u32[]{:S(2)}, u32[]{:S(2)}) collective-permute-start(bf16[512,1536]{1,0:T(8,128)(2,1)S(1)} %add_convert_fusion.2), channel_id=1, source_target_pairs={{0,2},{2,0},{1,3},{3,1},{4,6},{6,4},{5,7},{7,5},{8,10},{10,8},{9,1... | collective-permute-start | bytes 4718600 | tf_op jit(solution)/shard_map/ppermute | solution.py:801
  205.0 21.0 %collective-permute-start.9 = (bf16[512,1536]{1,0:T(8,128)(2,1)}, bf16[512,1536]{1,0:T(8,128)(2,1)S(1)}, u32[]{:S(2)}, u32[]{:S(2)}) collective-permute-start(bf16[512,1536]{1,0:T(8,128)(2,1)} %get-tuple-element.106), channel_id=1, source_target_pairs={{0,1},{1,0},{2,3},{3,2},{4,5},{5,4},{6,7},{7,6},{8,9},{9,8},{10,11... | collective-permute-start | bytes 4718600 | tf_op jit(solution)/shard_map/ppermute | solution.py:797
  205.1 3.4 collective-permute-start.13
  205.6 20.5 %collective-permute-start.12 = (f32[512,20]{1,0:T(8,128)S(1)}, f32[512,20]{1,0:T(8,128)S(1)}, u32[]{:S(2)}, u32[]{:S(2)}) collective-permute-start(f32[512,20]{1,0:T(8,128)S(1)} %copy-done.13), channel_id=1, source_target_pairs={{0,1},{1,0},{2,3},{3,2},{4,5},{5,4},{6,7},{7,6},{8,9},{9,8},{10,11... | collective-permute-start | bytes 122888 | tf_op jit(solution)/shard_map/ppermute | solution.py:797
  208.5 17.6 %collective-permute-start.14 = (f32[512,20]{1,0:T(8,128)S(1)}, f32[512,20]{1,0:T(8,128)S(1)}, u32[]{:S(2)}, u32[]{:S(2)}) collective-permute-start(f32[512,20]{1,0:T(8,128)S(1)} %add.46), channel_id=1, source_target_pairs={{0,2},{2,0},{1,3},{3,1},{4,6},{6,4},{5,7},{7,5},{8,10},{10,8},{9,1... | collective-permute-start | bytes 122888 | tf_op jit(solution)/shard_map/ppermute | solution.py:801
  227.8 43.2 %copy-start.12 = (bf16[512,1536]{1,0:T(8,128)(2,1)S(1)}, bf16[512,1536]{1,0:T(8,128)(2,1)}, u32[]{:S(2)}) copy-start(bf16[512,1536]{1,0:T(8,128)(2,1)} %get-tuple-element.133) | copy-start | bytes 4718596
  227.8 46.6 %copy-start.8 = (bf16[512,1536]{1,0:T(8,128)(2,1)S(1)}, bf16[512,1536]{1,0:T(8,128)(2,1)}, u32[]{:S(2)}) copy-start(bf16[512,1536]{1,0:T(8,128)(2,1)} %get-tuple-element.132) | copy-start | bytes 4718596
  271.0 3.5 collective-permute-start.16
  276.0 85.6 %collective-permute-start.17 = (bf16[512,1536]{1,0:T(8,128)(2,1)}, bf16[512,1536]{1,0:T(8,128)(2,1)S(1)}, u32[]{:S(2)}, u32[]{:S(2)}) collective-permute-start(bf16[512,1536]{1,0:T(8,128)(2,1)} %add_convert_fusion.1), channel_id=1, source_target_pairs={{0,2},{2,0},{1,3},{3,1},{4,6},{6,4},{5,7},{7,5},{8,10},{10,8},{9,1... | collective-permute-start | bytes 4718600 | tf_op jit(solution)/shard_map/ppermute | solution.py:801
  311.0 50.6 %copy-start.7 = (bf16[512,1536]{1,0:T(8,128)(2,1)S(1)}, bf16[512,1536]{1,0:T(8,128)(2,1)}, u32[]{:S(2)}) copy-start(bf16[512,1536]{1,0:T(8,128)(2,1)} %get-tuple-element.130) | copy-start | bytes 4718596
  311.0 50.6 %collective-permute-start.15 = (bf16[512,1536]{1,0:T(8,128)(2,1)}, bf16[512,1536]{1,0:T(8,128)(2,1)S(1)}, u32[]{:S(2)}, u32[]{:S(2)}) collective-permute-start(bf16[512,1536]{1,0:T(8,128)(2,1)} %get-tuple-element.131), channel_id=1, source_target_pairs={{0,1},{1,0},{2,3},{3,2},{4,5},{5,4},{6,7},{7,6},{8,9},{9,8},{10,11... | collective-permute-start | bytes 4718600 | tf_op jit(solution)/shard_map/ppermute | solution.py:797
  311.0 50.6 %copy-start = (f32[512,1536]{1,0:T(8,128)S(1)}, f32[512,1536]{1,0:T(8,128)}, u32[]{:S(2)}) copy-start(f32[512,1536]{1,0:T(8,128)} %get-tuple-element.117.resid) | copy-start | bytes 9437188
  (15 other events, 139.4 us)
Sparse Core Ops, SparseCore 0:
  149.6 95.5 reduce-scatter.1
  271.1 80.2 all-gather.1

commit v5 on v4

--- a/solution.py
+++ b/solution.py
@@ -14,7 +14,7 @@
 TOPK = 8
 SEQUENCE_TOKENS = 512
 BLOCK = 256
-EARLY = 1
+EARLY = 2
 
 
 epsilon = 1e-06
@@ -455,34 +455,34 @@
     return (1 - back) * 2 * place + back * (2 * (count - 1 - place) + 1)
 
 
-def ring_kernel(count, many, lag, shapes, *refs):
-    dense = len(shapes) - many
-    inputs, outputs, rest = refs[: 1 + dense], refs[1 + dense : 2 + 2 * dense], refs[2 + 2 * dense :]
-    total = len(shapes)
-    held, terms, rest = rest[:total], rest[total : 2 * total], rest[2 * total :]
-    own, near, far, joined, rest = (
-        rest[:dense], rest[dense : 2 * dense], rest[2 * dense : 3 * dense], rest[3 * dense : 4 * dense], rest[4 * dense :]
-    )
-    arrived, sent, loaded, stored, near_sent, near_arrived, own_loaded, far_sent, far_arrived, credit = rest
-    sources = [inputs[0].at[k] for k in range(many)] + list(joined)
-    sums = [outputs[0].at[k] for k in range(many)] + list(outputs[1:])
+def ring_place(count):
     here = lax.axis_index("rep")
     odd = here % 2
     rank = here // 2 + odd * (count - 1 - 2 * (here // 2))
     after = ring_device((rank + 1) % count, count)
     before = ring_device((rank + count - 1) % count, count)
-    hops = 2 * (count - 1)
+    return rank, after, before
+
+
+def group_places():
     holder = lax.axis_index("ep")
     core = holder + 1 - 2 * (holder % 2)
-    chip = (holder + 2) % 4
-    far_core = (core + 2) % 4
-
+    return holder, core, (holder + 2) % 4, (core + 2) % 4
+
+
+def greet(after, before, core, chip):
     barrier = pltpu.get_barrier_semaphore()
     for neighbour in (before, after):
         pl.semaphore_signal(barrier, inc=1, device_id={"rep": neighbour})
     for neighbour in (core, chip):
         pl.semaphore_signal(barrier, inc=1, device_id={"ep": neighbour})
     pl.semaphore_wait(barrier, 4)
+
+
+def ring_tools(count, shapes, sources, sums, held, terms, semaphores):
+    arrived, sent, loaded, stored, credit = semaphores
+    rank, after, before = ring_place(count)
+    hops = 2 * (count - 1)
 
     def columns(index, way):
         half = shapes[index][1] // 2
@@ -590,6 +590,34 @@
                 pass_on(index, way, hop)
 
             store(index, way, hop).start()
+
+    def end(streams):
+        for index, way in streams:
+            store(index, way, hops - 1).wait()
+
+    return begin, add_step, hand_step, end
+
+
+def both_ways(indices):
+    return [(index, way) for index in indices for way in (0, 1)]
+
+
+def ring_kernel(count, many, lag, shapes, *refs):
+    dense = len(shapes) - many
+    inputs, outputs, rest = refs[: 1 + dense], refs[1 + dense : 2 + 2 * dense], refs[2 + 2 * dense :]
+    total = len(shapes)
+    held, terms, rest = rest[:total], rest[total : 2 * total], rest[2 * total :]
+    own, near, far, joined, rest = (
+        rest[:dense], rest[dense : 2 * dense], rest[2 * dense : 3 * dense], rest[3 * dense : 4 * dense], rest[4 * dense :]
+    )
+    near_sent, near_arrived, own_loaded, far_sent, far_arrived = rest[:5]
+    sources = [inputs[0].at[k] for k in range(many)] + list(joined)
+    sums = [outputs[0].at[k] for k in range(many)] + list(outputs[1:])
+    _, after, before = ring_place(count)
+    holder, core, chip, far_core = group_places()
+    hops = 2 * (count - 1)
+    greet(after, before, core, chip)
+    begin, add_step, hand_step, end = ring_tools(count, shapes, sources, sums, held, terms, rest[5:])
 
     def block(k, index):
         rows = own[k].shape[1]
@@ -652,8 +680,7 @@
                 else:
                     joined[k][j] = jnp.zeros(joined[k].shape[1:], jnp.bfloat16)
 
-    early_streams = [(index, way) for index in range(many) for way in (0, 1)]
-    late_streams = [(index, way) for index in range(many, total) for way in (0, 1)]
+    early_streams, late_streams = both_ways(range(many)), both_ways(range(many, total))
     for k in range(dense):
         for part in (1, 0):
             to_core(k, part).start()
@@ -676,8 +703,7 @@
             return carry
 
         lax.fori_loop(low, high, ticks, 0)
-    for index, way in early_streams + late_streams:
-        store(index, way, hops - 1).wait()
+    end(early_streams + late_streams)
 
 
 def ring_sum(late, partials):
@@ -702,15 +728,15 @@
         + [pltpu.VMEM(quarter, jnp.bfloat16) for quarter in quarters]
         + [pltpu.VMEM((count,) + cut, jnp.bfloat16) for cut in cuts]
         + [
-            dma((2 * total, SLOTS)),
-            dma((2 * total, SLOTS)),
-            dma((2 * total, 2)),
-            dma((2 * total, SLOTS)),
             dma((dense, 2)),
             dma((dense, 2)),
             dma((dense, 2)),
             dma((dense,)),
             dma((dense,)),
+            dma((2 * total, SLOTS)),
+            dma((2 * total, SLOTS)),
+            dma((2 * total, 2)),
+            dma((2 * total, SLOTS)),
             pltpu.SemaphoreType.REGULAR((2 * total,)),
         ],
         compiler_params=pltpu.CompilerParams(
@@ -719,6 +745,296 @@
         cost_estimate=pl.CostEstimate(flops=2 * size, bytes_accessed=8 * size, transcendentals=0),
         name="ring_sum",
     )(late, *partials)
+
+
+def overlap_kernel(count, first, shapes, *refs):
+    unit, near, far, (w_gate, w_up, w_down), hs, cots = (
+        refs[0], refs[1:4], refs[4:7], refs[7:10], refs[10:14], refs[14:18]
+    )
+    unit_sum, grads, outs, refs = refs[18], refs[19], refs[20:26], refs[26:]
+    many = len(shapes)
+    held_slots, terms, refs = refs[:many], refs[many : 2 * many], refs[2 * many :]
+    (
+        left_a, left_b, right_a, right_b, right_c, total, total_w, stage, stage_w, from_core, from_chip,
+        ready, core_sent, core_arrived, chip_sent, chip_arrived, out_done, grads_done,
+    ) = refs[:18]
+    held = w_gate.shape[0]
+    tokens = hs[0].shape[0]
+    _, after, before = ring_place(count)
+    holder, core, chip, _ = group_places()
+    hops = 2 * (count - 1)
+    greet(after, before, core, chip)
+    streams = both_ways(range(many))
+    begin, add_step, hand_step, end = ring_tools(
+        count,
+        shapes,
+        [unit.at[k] for k in range(many)],
+        [unit_sum.at[k] for k in range(many)],
+        held_slots,
+        terms,
+        refs[18:],
+    )
+
+    def tick(hop):
+        pl.when(hop < count - 1)(lambda: add_step(streams, hop))
+        pl.when((hop >= count - 1) & (hop < hops))(lambda: hand_step(streams, hop))
+
+    def copies(bank, *pairs):
+        return [pltpu.make_async_copy(source, target, ready.at[bank, k]) for source, target, k in pairs]
+
+    def load_dh(side, e, bank):
+        return copies(
+            bank,
+            (side[1].at[e], left_a.at[bank], 0),
+            (side[2].at[e], left_b.at[bank], 1),
+            (w_gate.at[e], right_a.at[bank], 2),
+            (w_up.at[e], right_b.at[bank], 3),
+        )
+
+    def load_y(side, e, bank):
+        return copies(bank, (side[0].at[e], left_a.at[bank], 0), (w_down.at[e], right_c.at[bank], 4))
+
+    def load_w(e, kind, part, bank):
+        side = (near, far)[part // 2]
+        rows = pl.ds((part % 2) * tokens, tokens)
+        right = side[(1, 2, 0)[kind]].at[e, rows, :]
+        left = (hs, hs, cots)[kind][part]
+        return copies(bank, (right, left_a.at[bank, pl.ds(0, tokens), :], 0), (left, right_c.at[bank], 4))
+
+    def begin_all(made):
+        for copy in made:
+            copy.start()
+
+    def await_all(made):
+        for copy in made:
+            copy.wait()
+
+    def to_core(k):
+        return pltpu.make_async_remote_copy(
+            src_ref=stage.at[k % 2, 1],
+            dst_ref=from_core.at[k],
+            send_sem=core_sent.at[k],
+            recv_sem=core_arrived.at[k],
+            device_id={"ep": core},
+        )
+
+    def to_chip(k):
+        return pltpu.make_async_remote_copy(
+            src_ref=stage.at[0, 0],
+            dst_ref=from_chip.at[k // 2],
+            send_sem=chip_sent.at[k // 2],
+            recv_sem=chip_arrived.at[k // 2],
+            device_id={"ep": chip},
+        )
+
+    def send_chip(k):
+        to_core(k).wait_recv()
+        stage[0, 0] = (stage[0, 0].astype(jnp.float32) + from_core[k].astype(jnp.float32)).astype(jnp.bfloat16)
+        to_chip(k).start()
+
+    def own_out(k):
+        return pltpu.make_async_copy(stage.at[1, 0], outs[3 * (k // 2)], out_done.at[3 * (k // 2)])
+
+    def near_out(k):
+        return pltpu.make_async_copy(from_core.at[k], outs[3 * (k // 2) + 1], out_done.at[3 * (k // 2) + 1])
+
+    def far_out(k):
+        return pltpu.make_async_copy(from_chip.at[k // 2], outs[3 * (k // 2) + 2], out_done.at[3 * (k // 2) + 2])
+
+    plans = [(load_dh, far), (load_dh, near), (load_y, far), (load_y, near)]
+    begin_all(load_dh(far, 0, 0))
+    begin(streams)
+    hop = 0
+    for k, (loader, side) in enumerate(plans):
+        base = k * held
+
+        def next_first(bank, k=k):
+            if k + 1 < len(plans):
+                begin_all(plans[k + 1][0](plans[k + 1][1], 0, bank))
+            else:
+                begin_all(load_w(first, 0, 0, bank))
+
+        every = 2 if loader is load_dh else 3
+
+        def piece(e, carry, k=k, loader=loader, side=side, base=base, hop=hop, every=every, next_first=next_first):
+            bank = (base + e) % 2
+            await_all(loader(side, e, bank))
+
+            @pl.when(e + 1 < held)
+            def _():
+                begin_all(loader(side, e + 1, 1 - bank))
+
+            @pl.when(e + 1 == held)
+            def _():
+                next_first(1 - bank)
+
+            if loader is load_dh:
+                term = contract(left_a[bank], right_a[bank], 1, 1) + contract(left_b[bank], right_b[bank], 1, 1)
+            else:
+                term = contract(left_a[bank], right_c[bank], 1, 0)
+
+            @pl.when(e == 0)
+            def _():
+                total[...] = term
+
+            @pl.when(e > 0)
+            def _():
+                total[...] += term
+
+            @pl.when((e + 1) % every == 0)
+            def _():
+                tick(hop + e // every)
+
+            if k % 2 == 1:
+
+                @pl.when(e == 1)
+                def _():
+                    send_chip(k - 1)
+
+            return carry
+
+        lax.fori_loop(0, held, piece, 0)
+        hop += held // every
+        if k >= 2:
+            to_core(k - 2).wait_send()
+            if k == 2:
+                to_chip(0).wait_send()
+            else:
+                own_out(1).wait()
+        for half in (0, 1):
+            stage[k % 2, half] = total[half * tokens : (half + 1) * tokens].astype(jnp.bfloat16)
+        to_core(k).start()
+        if k % 2 == 1:
+            own_out(k).start()
+        tick(hop)
+        hop += 1
+
+    kinds = 3
+    base = len(plans) * held
+
+    def grads_out(e, kind):
+        slot = (kinds * e + kind) % 2
+        return pltpu.make_async_copy(stage_w.at[slot], grads.at[e, :, kind], grads_done.at[slot])
+
+    def expert(e, carry):
+        for kind in range(kinds):
+            for part in range(4):
+                bank = (base + 4 * kind + part) % 2
+                await_all(load_w(e + first, kind, part, bank))
+                if part < 3:
+                    begin_all(load_w(e + first, kind, part + 1, 1 - bank))
+                elif kind < kinds - 1:
+                    begin_all(load_w(e + first, kind + 1, 0, 1 - bank))
+                else:
+
+                    @pl.when(e + first + 1 < held)
+                    def _():
+                        begin_all(load_w(e + first + 1, 0, 0, 1 - bank))
+
+                term = contract(right_c[bank], left_a[bank, :tokens], 0, 0)
+                if part == 0:
+                    total_w[...] = term
+                else:
+                    total_w[...] += term
+
+            @pl.when(kinds * e + kind >= 2)
+            def _():
+                grads_out(e, kind).wait()
+
+            slot = (kinds * e + kind) % 2
+            rows = stage_w.shape[2]
+            for j in range(count):
+                stage_w[slot, j] = total_w[j * rows : (j + 1) * rows].astype(jnp.bfloat16)
+            grads_out(e, kind).start()
+            if kind != 1:
+                tick(hop + 2 * e + kind // 2)
+        return carry
+
+    late = held - first
+    lax.fori_loop(0, late, expert, 0)
+    hop += 2 * late
+
+    def drain(step, carry):
+        tick(step)
+        return carry
+
+    lax.fori_loop(hop, max(hop, hops), drain, 0)
+    end(streams)
+    for k in (1, 3):
+        to_core(k).wait_recv()
+        near_out(k).start()
+    for k in (0, 2):
+        to_chip(k).wait_recv()
+        far_out(k).start()
+    for kind in (kinds - 2, kinds - 1):
+        grads_out(late - 1, kind).wait()
+    own_out(3).wait()
+    to_chip(2).wait_send()
+    for k in (2, 3):
+        to_core(k).wait_send()
+    for k in (1, 3):
+        near_out(k).wait()
+    for k in (0, 2):
+        far_out(k).wait()
+
+
+def overlap(unit, near, far, w_gate, w_up, w_down, hs, cots, first):
+    many, count, rows3, columns = unit.shape
+    tokens, width = hs[0].shape
+    held = w_gate.shape[0]
+    shape, half = (rows3, columns), (rows3, columns // 2)
+    block = jax.ShapeDtypeStruct((tokens, width), jnp.bfloat16)
+    dma = pltpu.SemaphoreType.DMA
+
+    def buffers(*shape):
+        return pltpu.VMEM(shape, jnp.bfloat16)
+
+    flops = 2 * tokens * width * columns * (4 * 3 * held + 12 * (held - first))
+    inputs = [unit, *near, *far, w_gate, w_up, w_down, *hs, *cots]
+    unit_sum, grads, *blocks = pl.pallas_call(
+        functools.partial(overlap_kernel, count, first, [shape] * many),
+        out_shape=[
+            jax.ShapeDtypeStruct(unit.shape, unit.dtype),
+            jax.ShapeDtypeStruct((held - first, count, 3, rows3 // 3, columns), jnp.bfloat16),
+        ]
+        + [block] * 6,
+        in_specs=[pl.BlockSpec(memory_space=pl.ANY)] * len(inputs),
+        out_specs=[pl.BlockSpec(memory_space=pl.ANY)] * 8,
+        scratch_shapes=[
+            *[buffers(2, SLOTS, *half)] * many,
+            *[buffers(2, 2, *half)] * many,
+            buffers(2, 2 * tokens, columns),
+            buffers(2, 2 * tokens, columns),
+            buffers(2, width, columns),
+            buffers(2, width, columns),
+            buffers(2, columns, width),
+            pltpu.VMEM((2 * tokens, width), jnp.float32),
+            pltpu.VMEM((width, columns), jnp.float32),
+            buffers(2, 2, tokens, width),
+            buffers(2, count, rows3 // 3, columns),
+            buffers(4, tokens, width),
+            buffers(2, tokens, width),
+            dma((2, 5)),
+            dma((4,)),
+            dma((4,)),
+            dma((2,)),
+            dma((2,)),
+            dma((6,)),
+            dma((2,)),
+            dma((2 * many, SLOTS)),
+            dma((2 * many, SLOTS)),
+            dma((2 * many, 2)),
+            dma((2 * many, SLOTS)),
+            pltpu.SemaphoreType.REGULAR((2 * many,)),
+        ],
+        compiler_params=pltpu.CompilerParams(
+            collective_id=1, has_side_effects=True, vmem_limit_bytes=VMEM_BYTES
+        ),
+        cost_estimate=pl.CostEstimate(flops=flops, bytes_accessed=8 * unit.size, transcendentals=0),
+        name="overlap",
+    )(*inputs)
+    grads = grads.reshape(held - first, count, rows3, columns)
+    return unit_sum, grads, blocks[:3], blocks[3:]
 
 
 def finish_kernel(firsts, *refs):
@@ -846,35 +1162,19 @@
     router_own, router_near = near[3], swap_core(near[4])
     router_far = swap_chip(far[3] + swap_core(far[4]))
     early = weight_grads(replicas, 0, EARLY, hs, cots, ghs, dgs, dus)
-    dgs, early = lax.optimization_barrier((dgs, early))
-    early = [lax.psum_scatter(early[e], "rep", scatter_dimension=0, tiled=True) for e in range(EARLY)]
-    dh_far, other = sum_over_experts([dgs[1], dus[1]], [w_gate, w_up], 1)
-    dh_far = swap_chip(add_bf(dh_far, swap_core(other)))
-    dh_own, other = sum_over_experts([dgs[0], dus[0]], [w_gate, w_up], 1)
-    dh_near = swap_core(other)
-    ghs, dh_own = lax.optimization_barrier((ghs, dh_own))
-    y_far, other = sum_over_experts([ghs[1]], [w_down], 0)
-    dh_far, other = lax.optimization_barrier((dh_far, other))
-    y_far = swap_chip(add_bf(y_far, swap_core(other)))
+    early, late, (dh_own, dh_near, dh_far), (y_own, y_near, y_far) = overlap(
+        early, near[:3], far[:3], w_gate, w_up, w_down, hs, cots, EARLY
+    )
     d_resid, d_pre, grad_out = attention_back(
         dh_own, dh_near, dh_far, router_own, router_near, router_far, routes, probs, resid, norm_ffn, cotangent, w_router, w_out, h_two, attn,
         queries, keys, values, log_totals, cosine, sine,
     )
-    early, d_pre = lax.optimization_barrier((early, d_pre))
-    early = jnp.stack([lax.all_gather(part, "rep", axis=0, tiled=True) for part in early])
     d_input, grad_qkv = input_back(
         d_pre, normed, tokens, norm_attn, d_resid, w_query, key_projection, value_projection
     )
-    ghs, grad_qkv = lax.optimization_barrier((ghs, grad_qkv))
-    late = weight_grads(replicas, EARLY, held - EARLY, hs, cots, ghs, dgs, dus)
-    y_own, other = sum_over_experts([ghs[0]], [w_down], 0)
     mixed = (
-        resid
-        + y_own.astype(jnp.float32)
-        + swap_core(other).astype(jnp.float32)
-        + y_far.astype(jnp.float32)
+        resid + y_own.astype(jnp.float32) + y_near.astype(jnp.float32) + y_far.astype(jnp.float32)
     ).astype(jnp.bfloat16)
-    late, mixed = lax.optimization_barrier((late, mixed))
     late, sum_o, sum_qkv = ring_sum(late, [grad_out, grad_qkv])
     full_gate, full_up, full_down, sum_o, sum_q, sum_k, sum_v, extra_o, extra_qkv = finish(
         [early, late], [sum_o, sum_qkv], width, key_projection.shape[1]

time: 848 us -> 820 us (0.967)
  between operations: 14.8 us -> 0.98 us
    pallas_call x4 -> x1, Pallas kernels: 80.7 us -> 210 us  [overlap(): pl.pallas_call(functools.partial(overlap_kernel, count, first, [shape] *...]
    pallas_call x1, Pallas kernels: 431 us -> 341 us  [ring_sum(): pl.pallas_call(functools.partial(ring_kernel, count, many, 5, shapes), ou...]
    pallas_call x2 -> x1, Pallas kernels: 69.1 us -> 29.2 us  [weight_grads(): pl.pallas_call(weight_kernel, grid=(many, 3), in_specs=[whole(hs[0])] * 8...]
    ppermute x12 -> x8, waiting for transfers between devices: 14.4 us -> 5.54 us  [swap_core(): return lax.ppermute(value, 'ep', [(0, 1), (1, 0), (2, 3), (3, 2)])]
  transfers between devices with their start and end apart: 20 -> 12, of which waited for: 6 -> 4; matrix products, arithmetic and copies ran while one was open for 1% -> 1% of each run, Pallas kernels for 83% -> 42%
where the time goes in v5:
time: 820 us; the launch traced here: 810 us
  Pallas kernels  774 us (94%)
  local copies, waits for them, and re-layouts  12 us (1%)
  waiting for transfers between devices  9.54 us (1%)
    pallas_call x1, Pallas kernels, ring_sum(): pl.pallas_call(functools.partial(ring_kernel, count, many, 5, shapes), ou...  341 us
    pallas_call x1, Pallas kernels, overlap(): pl.pallas_call(functools.partial(overlap_kernel, count, first, [shape] *...  210 us
    pallas_call x2, Pallas kernels, expert_pass(): pl.pallas_call(functools.partial(expert_kernel, 256), grid=(held,), in_sp...  68.3 us
    pallas_call x1, Pallas kernels, attention_back(): pl.pallas_call(attention_back_kernel, out_shape=[shape((count, width), jn...  42.9 us
    pallas_call x1, Pallas kernels, attention_forward(): pl.pallas_call(attention_kernel, out_shape=[shape((count, width), jnp.bfl...  32.8 us
    pallas_call x1, Pallas kernels, finish(): pl.pallas_call(functools.partial(finish_kernel, firsts), grid=(experts, 4...  31 us
    pallas_call x1, Pallas kernels, weight_grads(): pl.pallas_call(weight_kernel, grid=(many, 3), in_specs=[whole(hs[0])] * 8...  29.2 us
    pallas_call x1, Pallas kernels, input_back(): pl.pallas_call(input_kernel, out_shape=[shape((count, width), jnp.float32...  18.7 us
  transfers between devices with their start and end apart: 12, of which 4 were waited for; matrix products, arithmetic and copies ran while one was open for 1% of the time, Pallas kernels for 42%

profile of v5, /device:TPU:0, one launch (start us, length us, event | category | flops | bytes accessed | tf_op | source)
XLA Modules:
  0.0 809.8 jit_solution(16093432115867916623)
XLA Ops:
  0.6 3.0 collective-permute-start
  3.6 1.3 broadcast_in_dim.4.norm_attn
  4.9 1.3 broadcast_in_dim.5.norm_ffn
  6.2 1.0 fusion
  7.2 1.3 pad_maximum_fusion
  8.5 32.8 %attention_forward.1 = (bf16[512,1536]{1,0:T(8,128)(2,1)}, bf16[512,1536]{1,0:T(8,128)(2,1)}, bf16[512,512]{1,0:T(8,128)(2,1)}, bf16[512,512]{1,0:T(8,128)(2,1)}...) custom-call(bf16[512,1536]{1,0:T(8,128)(2,1)} %tokens.3, ...), custom_call_target="tpu_custom_call" | custom-call | flops 7247757312 | bytes 18874368 | tf_op jit(solution)/shard_map/attention_forward/pallas_call | solution.py:281
  42.1 1.9 collective-permute-start.4
  44.0 1.9 collective-permute-done.3.gates1
  46.6 1.1 copy-done.4
  47.8 34.3 %expert_pass.2 = (bf16[5,1024,512]{2,1,0:T(8,128)(2,1)}, bf16[5,1024,512]{2,1,0:T(8,128)(2,1)}, bf16[5,1024,512]{2,1,0:T(8,128)(2,1)}, f32[512,20]{1,0:T(8,128)}, f32[512,20]{1,0:T(8,128)}) custom-call(bf16[512,1536]{1,0:T(8,128)(2,1)} %get-tuple-element.70.h0.refs_0_.refs_10_.h_two, bf16[512,1536]{1,0:T(8,128)(2,1)} %copy-done.4, ...), custom_call_target="tpu_custom_call" | custom-call | flops 24159191040 | bytes 23592960 | tf_op jit(solution)/shard_map/expert_pass/pallas_call | solution.py:98
  82.1 2.5 collective-permute-done.4.h0.refs_2_.refs_12_
  85.1 3.6 collective-permute-done.8.gates1
  89.4 1.2 copy-done.6
  90.6 34.1 %expert_pass.3 = (bf16[5,1024,512]{2,1,0:T(8,128)(2,1)}, bf16[5,1024,512]{2,1,0:T(8,128)(2,1)}, bf16[5,1024,512]{2,1,0:T(8,128)(2,1)}, f32[512,20]{1,0:T(8,128)}, f32[512,20]{1,0:T(8,128)}) custom-call(bf16[512,1536]{1,0:T(8,128)(2,1)} %copy-done.5, bf16[512,1536]{1,0:T(8,128)(2,1)} %copy-done.6, bf16[512,1536]{1,0:T(8,128)(2,1)} %copy-done.2, ...), custom_call_target="tpu_custom_call" | custom-call | flops 24159191040 | bytes 23592960 | tf_op jit(solution)/shard_map/expert_pass/pallas_call | solution.py:98
  124.9 29.2 %weight_grads.1 = bf16[2,8,3,192,512]{4,3,2,1,0:T(8,128)(2,1)} custom-call(bf16[512,1536]{1,0:T(8,128)(2,1)} %get-tuple-element.70.h0.refs_0_.refs_10_.h_two, bf16[512,1536]{1,0:T(8,128)(2,1)} %copy-done.4, bf16[512,1536]{1,0:T(8,128)(2,1)} %copy-done.5, bf16[512,1536]{1,0:T(8,128)(2,1)} %copy-done.6, bf16[512,1536]{1,0:T(8,128)(2,1)} %cotangent.1, ...), custom_call_target="tpu_custom_call" | custom-call | flops 19327352832 | bytes 22020096 | tf_op jit(solution)/shard_map/weight_grads/pallas_call | solution.py:137
  154.2 210.1 %overlap.1 = (bf16[2,8,576,512]{3,2,1,0:T(8,128)(2,1)}, bf16[3,8,3,192,512]{4,3,2,1,0:T(8,128)(2,1)}, bf16[512,1536]{1,0:T(8,128)(2,1)}, bf16[512,1536]{1,0:T(8,...) custom-call(bf16[2,8,576,512]{3,2,1,0:T(8,128)(2,1)} %bitcast.9, ...), custom_call_target="tpu_custom_call" | custom-call | flops 77309411328 | bytes 37748736 | tf_op jit(solution)/shard_map/overlap/pallas_call | solution.py:994
  364.9 4.3 add_convert_fusion
  369.2 1.5 collective-permute-done.11.router_far
  371.4 42.9 %attention_back.1 = (f32[512,1536]{1,0:T(8,128)}, bf16[512,2560]{1,0:T(8,128)(2,1)}, bf16[1536,1792]{1,0:T(8,128)(2,1)}) custom-call(bf16[512,1536]{1,0:T(8,128)(2,1)} %get-tuple-element.89.dh_own, bf16[512,1536]{1,0:T(8,128)(2,1)} %get-tuple-element.90.dh_near, bf16[512,1536]{1,0:T(8,128)(2,1)} %get-tuple-element.91.dh_far, ...), custom_call_target="tpu_custom_call" | custom-call | flops 12079595520 | bytes 18874368 | tf_op jit(solution)/shard_map/attention_back/pallas_call | solution.py:389
  414.4 18.7 %input_back.1 = (f32[512,1536]{1,0:T(8,128)}, bf16[1536,2816]{1,0:T(8,128)(2,1)}) custom-call(bf16[512,2560]{1,0:T(8,128)(2,1)} %get-tuple-element.102.d_pre, bf16[512,1536]{1,0:T(8,128)(2,1)} %get-tuple-element.103.normed, bf16[512,1536]{1,0:T(8,128)(2,1)} %tokens.3, bf16[1,1536]{1,0:T(2,128)(2,1)} %broadcast_in_dim.4.norm_attn, ...), custom_call_target="tpu_custom_call" | custom-call | flops 9663676416 | bytes 28311552 | tf_op jit(solution)/shard_map/input_back/pallas_call | solution.py:436
  433.0 340.6 %ring_sum.1 = (bf16[3,8,576,512]{3,2,1,0:T(8,128)(2,1)}, bf16[8,48,1792]{2,1,0:T(8,128)(2,1)}, bf16[8,48,2816]{2,1,0:T(8,128)(2,1)}) custom-call(bf16[3,8,576,512]{3,2,1,0:T(8,128)(2,1)} %bitcast.4, bf16[1536,1792]{1,0:T(8,128)(2,1)} %get-tuple-element.108.refs_1_, bf16[1536,2816]{1,0:T(8,128)(2,1)} %get-tuple-element.109.refs_2_), custom_call_target="tpu_custom_call" | custom-call | flops 28311552 | bytes 113246208 | tf_op jit(solution)/shard_map/ring_sum/pallas_call | solution.py:718
  773.6 31.0 %finish.1 = (f32[5,1536,512]{2,1,0:T(8,128)}, f32[5,1536,512]{2,1,0:T(8,128)}, f32[5,512,1536]{2,1,0:T(8,128)}, f32[384,1536]{1,0:T(8,128)}, f32[384,1536]{1,0:T...) custom-call(bf16[2,8,576,512]{3,2,1,0:T(8,128)(2,1)} %get-tuple-element.106.refs_0_,, ...), custom_call_target="tpu_custom_call" | custom-call | tf_op jit(solution)/shard_map/finish/pallas_call | solution.py:1090
  804.6 1.7 slice_reduce_fusion
  807.2 1.7 slice_reduce_fusion.1
  (45 shorter events, 5.9 us)
Async XLA Ops:
  0.6 40.7 %collective-permute-start = (bf16[512,1536]{1,0:T(8,128)(2,1)}, bf16[512,1536]{1,0:T(8,128)(2,1)S(1)}, u32[]{:S(2)}, u32[]{:S(2)}) collective-permute-start(bf16[512,1536]{1,0:T(8,128)(2,1)} %cotangent.1), channel_id=1, source_target_pairs={{0,2},{2,0},{1,3},{3,1},{4,6},{6,4},{5,7},{7,5},{8,10},{10,8},{9,1... | collective-permute-start | bytes 4718600 | tf_op jit(solution)/shard_map/ppermute | solution.py:1117
  3.6 40.4 %collective-permute-start.2 = (bf16[512,1536]{1,0:T(8,128)(2,1)}, bf16[512,1536]{1,0:T(8,128)(2,1)S(1)}, u32[]{:S(2)}, u32[]{:S(2)}) collective-permute-start(bf16[512,1536]{1,0:T(8,128)(2,1)} %cotangent.1), channel_id=1, source_target_pairs={{0,1},{1,0},{2,3},{3,2},{4,5},{5,4},{6,7},{7,6},{8,9},{9,8},{10,11... | collective-permute-start | bytes 4718600 | tf_op jit(solution)/shard_map/ppermute | solution.py:1113
  41.3 40.7 %copy-start.2 = (bf16[512,1536]{1,0:T(8,128)(2,1)}, bf16[512,1536]{1,0:T(8,128)(2,1)S(1)}, u32[]{:S(2)}) copy-start(bf16[512,1536]{1,0:T(8,128)(2,1)S(1)} %collective-permute-done.c0.refs_6_.refs_16_) | copy-start | bytes 4718596
  41.3 4.6 collective-permute-start.1
  41.9 4.0 collective-permute-start.3
  42.0 40.1 %collective-permute-start.5 = (f32[512,20]{1,0:T(8,128)}, f32[512,20]{1,0:T(8,128)S(1)}, u32[]{:S(2)}, u32[]{:S(2)}) collective-permute-start(f32[512,20]{1,0:T(8,128)} %get-tuple-element.71.gates0), channel_id=1, source_target_pairs={{0,2},{2,0},{1,3},{3,1},{4,6},{6,4},{5,7},{7,5},{8,10},{10,8},{9,1... | collective-permute-start | bytes 122888 | tf_op jit(solution)/shard_map/ppermute | solution.py:1117
  42.1 42.5 %collective-permute-start.4 = (bf16[512,1536]{1,0:T(8,128)(2,1)}, bf16[512,1536]{1,0:T(8,128)(2,1)S(1)}, u32[]{:S(2)}, u32[]{:S(2)}) collective-permute-start(bf16[512,1536]{1,0:T(8,128)(2,1)} %get-tuple-element.70.h0.refs_0_.refs_10_.h_two), channel_id=1, source_target_pairs={{0,2},{2,0},{1,3},{3,1},{4,6},{6,4},{5,7},{7,5},{8,10},{10,8},{9,1... | collective-permute-start | bytes 4718600 | tf_op jit(solution)/shard_map/ppermute | solution.py:1117
  44.0 1.9 copy-start.3
  44.0 41.1 %collective-permute-start.7 = (bf16[512,1536]{1,0:T(8,128)(2,1)S(1)}, bf16[512,1536]{1,0:T(8,128)(2,1)}, u32[]{:S(2)}, u32[]{:S(2)}) collective-permute-start(bf16[512,1536]{1,0:T(8,128)(2,1)S(1)} %collective-permute-done.c0.refs_6_.refs_16_), channel_id=1, source_target_pairs={{0,1},{1,0},{2,3},{3,2},{4,5},{5,4},{6,7},{7,6},{8,9},{9,8},{10,11... | collective-permute-start | bytes 4718600 | tf_op jit(solution)/shard_map/ppermute | solution.py:1113
  45.9 0.7 copy-start.10
  46.6 1.1 copy-start.4
  82.1 6.7 copy-start.8
  84.6 4.2 copy-start.5
  84.6 4.2 collective-permute-start.6
  84.6 4.2 collective-permute-start.8
  85.1 284.2 %collective-permute-start.9 = (f32[512,20]{1,0:T(8,128)}, f32[512,20]{1,0:T(8,128)S(1)}, u32[]{:S(2)}, u32[]{:S(2)}) collective-permute-start(f32[512,20]{1,0:T(8,128)} %get-tuple-element.93), channel_id=1, source_target_pairs={{0,1},{1,0},{2,3},{3,2},{4,5},{5,4},{6,7},{7,6},{8,9},{9,8},{10,11... | collective-permute-start | bytes 122888 | tf_op jit(solution)/shard_map/ppermute | solution.py:1113
  88.7 0.7 copy-start.11
  89.4 1.2 copy-start.6
  124.7 239.6 %collective-permute-start.10 = (f32[512,20]{1,0:T(8,128)}, f32[512,20]{1,0:T(8,128)S(1)}, u32[]{:S(2)}, u32[]{:S(2)}) collective-permute-start(f32[512,20]{1,0:T(8,128)} %get-tuple-element.95), channel_id=1, source_target_pairs={{0,1},{1,0},{2,3},{3,2},{4,5},{5,4},{6,7},{7,6},{8,9},{9,8},{10,11... | collective-permute-start | bytes 122888 | tf_op jit(solution)/shard_map/ppermute | solution.py:1113
  154.2 210.1 %copy-start.1 = (f32[512,20]{1,0:T(8,128)S(1)}, f32[512,20]{1,0:T(8,128)}, u32[]{:S(2)}) copy-start(f32[512,20]{1,0:T(8,128)} %get-tuple-element.94) | copy-start | bytes 122884
  154.2 210.8 %copy-start = (f32[512,1536]{1,0:T(8,128)S(1)}, f32[512,1536]{1,0:T(8,128)}, u32[]{:S(2)}) copy-start(f32[512,1536]{1,0:T(8,128)} %get-tuple-element.67.resid) | copy-start | bytes 9437188
  364.3 6.4 collective-permute-start.11
  369.2 1.5 copy-start.7
  370.7 0.7 copy-start.9

commit v6 on v5

--- a/solution.py
+++ b/solution.py
@@ -52,10 +52,27 @@
 VMEM_BYTES = 56 * 2**20
 
 
-def expert_kernel(tile, h0, h1, c0, c1, gates0, gates1, w_gate, w_up, w_down, gh, dg, du, d_router0, d_router1):
+def expert_tile(entries, cotangents, gates, mine, w_gate, w_up, w_down):
+    gate_pre = contract(entries, w_gate, 1, 0)
+    up_pre = contract(entries, w_up, 1, 0)
+    back = contract(cotangents, w_down, 1, 1)
+    column = jnp.sum(jnp.where(mine, gates, 0.0), 1, keepdims=True)
+    sigma = jax.nn.sigmoid(gate_pre)
+    swish = gate_pre * sigma
+    hidden = (swish * up_pre).astype(jnp.bfloat16).astype(jnp.float32)
+    d_hidden = column * back
+    return (
+        (column * hidden).astype(jnp.bfloat16),
+        (d_hidden * up_pre * (sigma * (1.0 + gate_pre * (1.0 - sigma)))).astype(jnp.bfloat16),
+        (d_hidden * swish).astype(jnp.bfloat16),
+        jnp.sum(hidden * back, 1, keepdims=True),
+    )
+
+
+def expert_kernel(tile, held, h0, h1, c0, c1, gates0, gates1, w_gate, w_up, w_down, gh, dg, du, d_router0, d_router1):
     e = pl.program_id(0)
     tokens, lanes = gates0.shape
-    expert = lax.axis_index("ep") * pl.num_programs(0) + e
+    expert = lax.axis_index("ep") * held + e
     lane = lax.broadcasted_iota(jnp.int32, (tile, lanes), 1)
 
     @pl.when(e == 0)
@@ -70,42 +87,30 @@
         for start in range(0, tokens, tile):
             rows = slice(start, start + tile)
             out = slice(base + start, base + start + tile)
-            entries = rows_h[rows, :]
-            gate_pre = contract(entries, w_gate[0], 1, 0)
-            up_pre = contract(entries, w_up[0], 1, 0)
-            back = contract(rows_c[rows, :], w_down[0], 1, 1)
-            column = jnp.sum(jnp.where(lane == expert, gates[rows, :], 0.0), 1, keepdims=True)
-            sigma = jax.nn.sigmoid(gate_pre)
-            swish = gate_pre * sigma
-            hidden = (swish * up_pre).astype(jnp.bfloat16).astype(jnp.float32)
-            d_router[rows, :] = jnp.where(
-                lane == expert, jnp.sum(hidden * back, 1, keepdims=True), d_router[rows, :]
+            results = expert_tile(
+                rows_h[rows, :], rows_c[rows, :], gates[rows, :], lane == expert, w_gate[0], w_up[0], w_down[0]
             )
-            d_hidden = column * back
-            dg[0, out, :] = (
-                d_hidden * up_pre * (sigma * (1.0 + gate_pre * (1.0 - sigma)))
-            ).astype(jnp.bfloat16)
-            du[0, out, :] = (d_hidden * swish).astype(jnp.bfloat16)
-            gh[0, out, :] = (column * hidden).astype(jnp.bfloat16)
-
-
-def expert_pass(hs, cots, gates, w_gate, w_up, w_down):
+            gh[0, out, :], dg[0, out, :], du[0, out, :] = results[:3]
+            d_router[rows, :] = jnp.where(lane == expert, results[3], d_router[rows, :])
+
+
+def expert_pass(many, hs, cots, gates, w_gate, w_up, w_down):
     count, width = hs[0].shape
     tokens = 2 * count
     held, _, hidden_units = w_gate.shape
-    part = jax.ShapeDtypeStruct((held, tokens, hidden_units), jnp.bfloat16)
+    part = jax.ShapeDtypeStruct((many, tokens, hidden_units), jnp.bfloat16)
     gate_shape = gates[0].shape
     return pl.pallas_call(
-        functools.partial(expert_kernel, 256),
-        grid=(held,),
+        functools.partial(expert_kernel, 256, held),
+        grid=(many,),
         in_specs=[whole(a) for a in (*hs, *cots, *gates)] + [each(a) for a in (w_gate, w_up, w_down)],
         out_specs=[each(part)] * 3 + [pl.BlockSpec(gate_shape, lambda e: (0, 0))] * 2,
         out_shape=[part] * 3 + [jax.ShapeDtypeStruct(gate_shape, jnp.float32)] * 2,
         compiler_params=pltpu.CompilerParams(vmem_limit_bytes=VMEM_BYTES),
         cost_estimate=pl.CostEstimate(
-            flops=6 * held * tokens * width * hidden_units,
-            bytes_accessed=6 * held * width * hidden_units,
-            transcendentals=held * tokens * hidden_units,
+            flops=6 * many * tokens * width * hidden_units,
+            bytes_accessed=6 * many * width * hidden_units,
+            transcendentals=many * tokens * hidden_units,
         ),
         name="expert_pass",
     )(*hs, *cots, *gates, w_gate, w_up, w_down)
@@ -214,6 +219,14 @@
     )
 
 
+IN_VMEM = pl.BlockSpec(memory_space=pltpu.VMEM)
+IN_PLACE = pl.BlockSpec(memory_space=pl.ANY)
+
+
+def moves(semaphores, *pairs):
+    return [pltpu.make_async_copy(source, target, semaphores.at[k]) for k, (source, target) in enumerate(pairs)]
+
+
 def chosen_of(routes, shape):
     expert = lax.broadcasted_iota(jnp.int32, shape, 1)
     picks = routes[...].T
@@ -224,17 +237,32 @@
 
 
 def attention_kernel(
-    tokens, norm_attn, w_query, w_key, w_value, cosine, sine, w_out, norm_ffn, w_router, routes,
-    normed, queries, keys, values, log_totals, attn, resid, h_two, probs, combine,
+    tokens, norm_attn, w_query_in, w_key_in, w_value_in, cosine, sine, w_out_in, norm_ffn, w_router, routes,
+    normed_out, queries_out, keys_out, values_out, log_totals, attn_out, resid_out, h_two, probs, combine,
+    w_query, w_key, w_value, w_out, normed, queries, keys, values, attn, resid, arrived, left,
 ):
     count, width = tokens.shape
+    weights = moves(
+        arrived, (w_query_in, w_query), (w_key_in, w_key), (w_value_in, w_value), (w_out_in, w_out)
+    )
+    results = moves(
+        left, (normed, normed_out), (queries, queries_out), (keys, keys_out), (values, values_out), (attn, attn_out),
+        (resid, resid_out),
+    )
+    for weight in weights:
+        weight.start()
     field = tokens[...].astype(jnp.float32)
     inverse = lax.rsqrt(jnp.mean(field * field, -1, keepdims=True) + epsilon)
     first = (field * inverse * norm_attn[...].astype(jnp.float32)).astype(jnp.bfloat16)
     normed[...] = first
+    results[0].start()
+    for weight in weights[:3]:
+        weight.wait()
     queries[...] = rotate(contract(first, w_query[...], 1, 0), cosine[...], sine[...], 1).astype(jnp.bfloat16)
     keys[...] = rotate(contract(first, w_key[...], 1, 0), cosine[...], sine[...], 1).astype(jnp.bfloat16)
     values[...] = contract(first, w_value[...], 1, 0).astype(jnp.bfloat16)
+    for result in results[1:4]:
+        result.start()
     groups = keys.shape[1] // HEAD_SIZE
     per_group = queries.shape[1] // keys.shape[1]
     lane = lax.broadcasted_iota(jnp.int32, (BLOCK, log_totals.shape[1]), 1)
@@ -258,8 +286,11 @@
                 attn[rows, head * HEAD_SIZE : (head + 1) * HEAD_SIZE] = mix[part]
                 logs = jnp.where(lane == head, log_sum[part], logs)
         log_totals[rows, :] = logs
+    results[4].start()
+    weights[3].wait()
     total = field + contract(attn[...], w_out[...], 1, 0)
     resid[...] = total
+    results[5].start()
     inverse = lax.rsqrt(jnp.mean(total * total, -1, keepdims=True) + epsilon)
     second = (total * inverse * norm_ffn[...].astype(jnp.float32)).astype(jnp.bfloat16)
     h_two[...] = second
@@ -268,6 +299,8 @@
     soft = shifted / jnp.sum(shifted, -1, keepdims=True)
     probs[...] = soft
     combine[...] = jnp.where(chosen_of(routes, logits.shape), soft, 0.0)
+    for result in results:
+        result.wait()
 
 
 LANES = 128
@@ -292,6 +325,21 @@
             shape((count, experts), jnp.float32),
             shape((count, experts), jnp.float32),
         ],
+        in_specs=[IN_VMEM] * 2 + [IN_PLACE] * 3 + [IN_VMEM] * 2 + [IN_PLACE] + [IN_VMEM] * 3,
+        out_specs=[IN_PLACE] * 4 + [IN_VMEM] + [IN_PLACE] * 2 + [IN_VMEM] * 3,
+        scratch_shapes=[
+            pltpu.VMEM(weight.shape, weight.dtype) for weight in (w_query, w_key, w_value, w_out)
+        ]
+        + [
+            pltpu.VMEM((count, width), jnp.bfloat16),
+            pltpu.VMEM((count, width), jnp.bfloat16),
+            pltpu.VMEM((count, key_width), jnp.bfloat16),
+            pltpu.VMEM((count, key_width), jnp.bfloat16),
+            pltpu.VMEM((count, width), jnp.bfloat16),
+            pltpu.VMEM((count, width), jnp.float32),
+            pltpu.SemaphoreType.DMA((4,)),
+            pltpu.SemaphoreType.DMA((6,)),
+        ],
         compiler_params=pltpu.CompilerParams(vmem_limit_bytes=VMEM_BYTES),
         cost_estimate=pl.CostEstimate(
             flops=6 * count * width * width, bytes_accessed=8 * width * width, transcendentals=24 * count * count
@@ -307,13 +355,16 @@
     return jnp.where(first, row, 0.0).T.astype(jnp.bfloat16)
 
 
-def attention_back_kernel(
-    dh_own, dh_near, dh_far, router_own, router_near, router_far, routes, probs, resid, norm_ffn, cotangent, w_router, w_out, h_two, attn,
-    queries, keys, values, log_totals, cosine, sine,
-    d_resid, d_pre, grad_out, d_branch, d_attn, d_queries, d_keys, d_values,
+def branch_back_kernel(
+    dh_own, dh_near, dh_far, router_own, router_near, router_far, routes, probs, resid, norm_ffn, cotangent, w_router, w_out_in, h_two_in, attn_in,
+    d_resid_out, grad_out_out, d_attn, w_out, h_two, attn, d_resid, grad_out, d_branch, arrived, left,
 ):
     count, width = resid.shape
     experts = probs.shape[1]
+    inputs = moves(arrived, (w_out_in, w_out), (h_two_in, h_two), (attn_in, attn))
+    results = moves(left, (d_resid, d_resid_out), (grad_out, grad_out_out))
+    for copy in inputs:
+        copy.start()
     soft = probs[...]
     to_router = jnp.where(
         chosen_of(routes, soft.shape), router_own[...] + router_near[...] + router_far[...], 0.0
@@ -333,12 +384,24 @@
         scaled - normal * jnp.mean(scaled * normal, -1, keepdims=True)
     )
     d_resid[...] = back
+    results[0].start()
     d_branch[...] = back.astype(jnp.bfloat16)
+    for copy in inputs:
+        copy.wait()
     grad_out[:, :width] = contract(attn[...], d_branch[...], 0, 0).astype(jnp.bfloat16)
     d_logits = jnp.concatenate([d_logits, jnp.zeros((count, LANES - experts), jnp.bfloat16)], 1)
     grad_out[:, width : width + LANES] = contract(h_two[...], d_logits, 0, 0).astype(jnp.bfloat16)
     grad_out[:, width + LANES :] = as_lane(jnp.sum(d_normed * normal, 0, keepdims=True))
+    results[1].start()
     d_attn[...] = contract(d_branch[...], w_out[...], 1, 1).astype(jnp.bfloat16)
+    for copy in results:
+        copy.wait()
+
+
+def attention_back_kernel(
+    d_attn, queries, keys, values, log_totals, cosine, sine, d_pre, d_queries, d_keys, d_values
+):
+    count, width = queries.shape
     groups = keys.shape[1] // HEAD_SIZE
     per_group = queries.shape[1] // keys.shape[1]
     factor = HEAD_SIZE ** (-0.5)
@@ -381,53 +444,99 @@
     d_pre[:, width + key_width :] = d_values[...].astype(jnp.bfloat16)
 
 
-def attention_back(dh_own, dh_near, dh_far, router_own, router_near, router_far, routes, probs, resid, norm_ffn, cotangent, w_router, w_out, h_two, attn,
-                   queries, keys, values, log_totals, cosine, sine):
+def branch_back(dh_own, dh_near, dh_far, router_own, router_near, router_far, routes, probs, resid, norm_ffn, cotangent,
+                w_router, w_out, h_two, attn):
     count, width = resid.shape
-    key_width = keys.shape[1]
     shape = jax.ShapeDtypeStruct
     return pl.pallas_call(
-        attention_back_kernel,
+        branch_back_kernel,
         out_shape=[
             shape((count, width), jnp.float32),
-            shape((count, width + 2 * key_width), jnp.bfloat16),
             shape((width, width + 2 * LANES), jnp.bfloat16),
+            shape((count, width), jnp.bfloat16),
         ],
+        in_specs=[IN_VMEM] * 12 + [IN_PLACE] * 3,
+        out_specs=[IN_PLACE] * 2 + [IN_VMEM],
         scratch_shapes=[
+            pltpu.VMEM(w_out.shape, jnp.bfloat16),
             pltpu.VMEM((count, width), jnp.bfloat16),
             pltpu.VMEM((count, width), jnp.bfloat16),
+            pltpu.VMEM((count, width), jnp.float32),
+            pltpu.VMEM((width, width + 2 * LANES), jnp.bfloat16),
+            pltpu.VMEM((count, width), jnp.bfloat16),
+            pltpu.SemaphoreType.DMA((3,)),
+            pltpu.SemaphoreType.DMA((2,)),
+        ],
+        compiler_params=pltpu.CompilerParams(vmem_limit_bytes=VMEM_BYTES),
+        cost_estimate=pl.CostEstimate(
+            flops=4 * count * width * width, bytes_accessed=8 * width * width, transcendentals=0
+        ),
+        name="branch_back",
+    )(
+        dh_own, dh_near, dh_far, router_own, router_near, router_far, routes.T, probs, resid, norm_ffn[None], cotangent,
+        w_router.T, w_out, h_two, attn,
+    )
+
+
+def attention_back(d_attn, queries, keys, values, log_totals, cosine, sine):
+    count, width = queries.shape
+    key_width = keys.shape[1]
+    return pl.pallas_call(
+        attention_back_kernel,
+        out_shape=jax.ShapeDtypeStruct((count, width + 2 * key_width), jnp.bfloat16),
+        scratch_shapes=[
             pltpu.VMEM((count, width), jnp.float32),
             pltpu.VMEM((count, key_width), jnp.float32),
             pltpu.VMEM((count, key_width), jnp.float32),
         ],
         compiler_params=pltpu.CompilerParams(vmem_limit_bytes=VMEM_BYTES),
         cost_estimate=pl.CostEstimate(
-            flops=10 * count * width * width, bytes_accessed=8 * width * width, transcendentals=24 * count * count
+            flops=8 * count * width * width, bytes_accessed=4 * width * width, transcendentals=24 * count * count
         ),
         name="attention_back",
-    )(
-        dh_own, dh_near, dh_far, router_own, router_near, router_far, routes.T, probs, resid, norm_ffn[None], cotangent,
-        w_router.T, w_out, h_two, attn, queries, keys, values, log_totals, cosine, sine,
-    )
-
-
-def input_kernel(d_pre, normed, tokens, norm_attn, d_resid, w_query, w_key, w_value, d_input, grads):
+    )(d_attn, queries, keys, values, log_totals, cosine, sine)
+
+
+def input_kernel(
+    d_pre, normed, tokens_in, norm_attn, d_resid_in, w_query_in, w_key_in, w_value_in, d_input, grads_out,
+    tokens, d_resid, w_query, w_key, w_value, grads, arrived, left,
+):
     width, key_width = w_query.shape[1], w_key.shape[1]
-    entries = d_pre[...]
+    inputs = moves(
+        arrived, (w_query_in, w_query), (w_key_in, w_key), (w_value_in, w_value), (tokens_in, tokens), (d_resid_in, d_resid)
+    )
+    for copy in inputs:
+        copy.start()
+    wide = d_pre.shape[1]
+    results = moves(
+        left,
+        *[
+            (grads.at[:, pl.ds(start, key_width)], grads_out.at[:, pl.ds(start, key_width)])
+            for start in range(0, wide, key_width)
+        ],
+        (grads.at[:, pl.ds(wide, 2 * LANES)], grads_out.at[:, pl.ds(wide, 2 * LANES)]),
+    )
+    for k, start in enumerate(range(0, wide, key_width)):
+        cut = slice(start, start + key_width)
+        grads[:, cut] = contract(normed[...], d_pre[:, cut], 0, 0).astype(jnp.bfloat16)
+        results[k].start()
+    for copy in inputs:
+        copy.wait()
     d_normed = (
-        contract(entries[:, :width], w_query[...], 1, 1)
-        + contract(entries[:, width : width + key_width], w_key[...], 1, 1)
-        + contract(entries[:, width + key_width :], w_value[...], 1, 1)
+        contract(d_pre[:, :width], w_query[...], 1, 1)
+        + contract(d_pre[:, width : width + key_width], w_key[...], 1, 1)
+        + contract(d_pre[:, width + key_width :], w_value[...], 1, 1)
     )
     field = tokens[...].astype(jnp.float32)
     inverse = lax.rsqrt(jnp.mean(field * field, -1, keepdims=True) + epsilon)
     normal = field * inverse
     scaled = d_normed * norm_attn[...].astype(jnp.float32)
-    d_input[...] = d_resid[...] + inverse * (scaled - normal * jnp.mean(scaled * normal, -1, keepdims=True))
-    wide = entries.shape[1]
-    grads[:, :wide] = contract(normed[...], entries, 0, 0).astype(jnp.bfloat16)
     grads[:, wide : wide + LANES] = as_lane(jnp.sum(d_normed * normal, 0, keepdims=True))
     grads[:, wide + LANES :] = jnp.zeros((width, LANES), jnp.bfloat16)
+    results[-1].start()
+    d_input[...] = d_resid[...] + inverse * (scaled - normal * jnp.mean(scaled * normal, -1, keepdims=True))
+    for copy in results:
+        copy.wait()
 
 
 def input_back(d_pre, normed, tokens, norm_attn, d_resid, w_query, w_key, w_value):
@@ -439,6 +548,16 @@
             shape((count, width), jnp.float32),
             shape((width, d_pre.shape[1] + 2 * LANES), jnp.bfloat16),
         ],
+        in_specs=[IN_VMEM] * 2 + [IN_PLACE, IN_VMEM] + [IN_PLACE] * 4,
+        out_specs=[IN_VMEM, IN_PLACE],
+        scratch_shapes=[
+            pltpu.VMEM((count, width), jnp.bfloat16),
+            pltpu.VMEM((count, width), jnp.float32),
+            *[pltpu.VMEM(weight.shape, jnp.bfloat16) for weight in (w_query, w_key, w_value)],
+            pltpu.VMEM((width, d_pre.shape[1] + 2 * LANES), jnp.bfloat16),
+            pltpu.SemaphoreType.DMA((5,)),
+            pltpu.SemaphoreType.DMA((d_pre.shape[1] // w_key.shape[1] + 1,)),
+        ],
         compiler_params=pltpu.CompilerParams(vmem_limit_bytes=VMEM_BYTES),
         cost_estimate=pl.CostEstimate(
             flops=8 * count * width * width, bytes_accessed=12 * width * width, transcendentals=0
@@ -479,7 +598,7 @@
     pl.semaphore_wait(barrier, 4)
 
 
-def ring_tools(count, shapes, sources, sums, held, terms, semaphores):
+def ring_tools(count, shapes, sources, sums, held, terms, semaphores, start=0, initial=()):
     arrived, sent, loaded, stored, credit = semaphores
     rank, after, before = ring_place(count)
     hops = 2 * (count - 1)
@@ -509,13 +628,16 @@
             loaded.at[2 * index + way, hop % 2],
         )
 
+    started = initial[0].shape[0] if initial else 0
+
+    def begins(index):
+        return start if index < started else 0
+
     def first(index, way):
         chunk = (rank + 1) % count if way else (rank + count - 1) % count
-        return pltpu.make_async_copy(
-            sources[index].at[chunk, :, columns(index, way)],
-            held[index].at[way, SLOTS - 1],
-            stored.at[2 * index + way, SLOTS - 1],
-        )
+        source = initial[way].at[index] if index < started else sources[index].at[chunk, :, columns(index, way)]
+        slot = (begins(index) + SLOTS - 1) % SLOTS
+        return pltpu.make_async_copy(source, held[index].at[way, slot], stored.at[2 * index + way, slot])
 
     def store(index, way, hop):
         step = hop - (count - 2)
@@ -535,18 +657,18 @@
         for index, way in streams:
             first(index, way).start()
         for index, way in streams:
-            load(index, way, 0).start()
-            load(index, way, 1).start()
+            load(index, way, begins(index)).start()
+            load(index, way, begins(index) + 1).start()
         for index, way in streams:
             first(index, way).wait()
-            send(index, way, 0).start()
+            send(index, way, begins(index)).start()
 
     def take(index, way, hop):
         send(index, way, hop).wait_recv()
         send(index, way, hop).wait_send()
 
     def pass_on(index, way, hop):
-        @pl.when(hop + 1 >= 2)
+        @pl.when(hop + 1 >= begins(index) + 2)
         def _():
             pl.semaphore_wait(credit.at[2 * index + way], 1)
 
@@ -602,9 +724,10 @@
     return [(index, way) for index in indices for way in (0, 1)]
 
 
-def ring_kernel(count, many, lag, shapes, *refs):
+def ring_kernel(count, many, lag, start, shapes, *refs):
     dense = len(shapes) - many
-    inputs, outputs, rest = refs[: 1 + dense], refs[1 + dense : 2 + 2 * dense], refs[2 + 2 * dense :]
+    inputs, initial, refs = refs[: 1 + dense], refs[1 + dense : 3 + dense], refs[3 + dense :]
+    outputs, rest = refs[: 1 + dense], refs[1 + dense :]
     total = len(shapes)
     held, terms, rest = rest[:total], rest[total : 2 * total], rest[2 * total :]
     own, near, far, joined, rest = (
@@ -617,7 +740,9 @@
     holder, core, chip, far_core = group_places()
     hops = 2 * (count - 1)
     greet(after, before, core, chip)
-    begin, add_step, hand_step, end = ring_tools(count, shapes, sources, sums, held, terms, rest[5:])
+    begin, add_step, hand_step, end = ring_tools(
+        count, shapes, sources, sums, held, terms, rest[5:], start, initial
+    )
 
     def block(k, index):
         rows = own[k].shape[1]
@@ -686,7 +811,7 @@
             to_core(k, part).start()
             own_block(k, part).start()
     begin(early_streams)
-    ends = sorted({0, 1, lag, count - 1, hops, lag + count - 1, lag + hops})
+    ends = sorted({0, 1, lag, count - 1 - start, hops - start, lag + count - 1, lag + hops})
     for low, high in zip(ends[:-1], ends[1:]):
         if low == 1:
             send_far()
@@ -695,18 +820,18 @@
             begin(late_streams)
 
         def ticks(tick, carry, low=low):
-            for streams, start in ((early_streams, 0), (late_streams, lag)):
-                if start <= low < start + count - 1:
-                    add_step(streams, tick - start)
-                elif start + count - 1 <= low < start + hops:
-                    hand_step(streams, tick - start)
+            for streams, zero in ((early_streams, -start), (late_streams, lag)):
+                if max(zero, 0) <= low < zero + count - 1:
+                    add_step(streams, tick - zero)
+                elif zero + count - 1 <= low < zero + hops:
+                    hand_step(streams, tick - zero)
             return carry
 
         lax.fori_loop(low, high, ticks, 0)
     end(early_streams + late_streams)
 
 
-def ring_sum(late, partials):
+def ring_sum(late, partials, start, initial):
     many, count = late.shape[:2]
     quarters = [(partial.shape[0] // 4, partial.shape[1]) for partial in partials]
     cuts = [(-(-rows // (8 * count)) * 8, columns) for rows, columns in quarters]
@@ -716,10 +841,10 @@
     size = late.size + sum(partial.size for partial in partials)
     dma = pltpu.SemaphoreType.DMA
     return pl.pallas_call(
-        functools.partial(ring_kernel, count, many, 5, shapes),
+        functools.partial(ring_kernel, count, many, 5, start, shapes),
         out_shape=[jax.ShapeDtypeStruct(late.shape, late.dtype)]
         + [jax.ShapeDtypeStruct((count,) + cut, late.dtype) for cut in cuts],
-        in_specs=[pl.BlockSpec(memory_space=pl.ANY)] * (1 + dense),
+        in_specs=[pl.BlockSpec(memory_space=pl.ANY)] * (3 + dense),
         out_specs=[pl.BlockSpec(memory_space=pl.ANY)] * (1 + dense),
         scratch_shapes=[pltpu.VMEM((2, SLOTS) + half, jnp.bfloat16) for half in halves]
         + [pltpu.VMEM((2, 2) + half, jnp.bfloat16) for half in halves]
@@ -744,20 +869,62 @@
         ),
         cost_estimate=pl.CostEstimate(flops=2 * size, bytes_accessed=8 * size, transcendentals=0),
         name="ring_sum",
-    )(late, *partials)
+    )(late, *partials, *initial)
+
+
+def chunk_kernel(chunks, forth, back, *refs):
+    for term, held, out in zip((forth, back), refs[:-2] or (None, None), refs[-2:]):
+        if held is None:
+            out[...] = term[:, 0]
+        else:
+            out[...] = (term[:, 0].astype(jnp.float32) + held[...].astype(jnp.float32)).astype(out.dtype)
+
+
+def ring_chunks(units, step, held=()):
+    many, count, rows, columns = units.shape
+    rank, _, _ = ring_place(count)
+    chunks = jnp.stack([(rank + count - step) % count, (rank + step) % count])
+    half = columns // 2
+    block = pl.BlockSpec((many, rows, half), lambda e, chunks: (0, 0, 0))
+    return pl.pallas_call(
+        chunk_kernel,
+        grid_spec=pltpu.PrefetchScalarGridSpec(
+            num_scalar_prefetch=1,
+            grid=(1,),
+            in_specs=[
+                pl.BlockSpec((many, 1, rows, half), lambda e, chunks: (0, chunks[0], 0, 0)),
+                pl.BlockSpec((many, 1, rows, half), lambda e, chunks: (0, chunks[1], 0, 1)),
+            ]
+            + [block] * len(held),
+            out_specs=[block] * 2,
+        ),
+        out_shape=[jax.ShapeDtypeStruct((many, rows, half), units.dtype)] * 2,
+        compiler_params=pltpu.CompilerParams(vmem_limit_bytes=VMEM_BYTES),
+        name="ring_chunks",
+    )(chunks, units, units, *held)
+
+
+def ring_hop(parts, count):
+    places = [ring_device(place, count) for place in range(count)]
+    pairs = [(places[k], places[(k + 1) % count]) for k in range(count)]
+    turned = [(b, a) for a, b in pairs]
+    return lax.ppermute(parts[0], "rep", pairs), lax.ppermute(parts[1], "rep", turned)
 
 
 def overlap_kernel(count, first, shapes, *refs):
     unit, near, far, (w_gate, w_up, w_down), hs, cots = (
         refs[0], refs[1:4], refs[4:7], refs[7:10], refs[10:14], refs[14:18]
     )
-    unit_sum, grads, outs, refs = refs[18], refs[19], refs[20:26], refs[26:]
+    gates, router_so_far, refs = refs[18:20], refs[20:22], refs[22:]
+    unit_sum, grads, outs, router_far, rest_far, refs = refs[0], refs[1], refs[2:8], refs[8], refs[9:12], refs[12:]
     many = len(shapes)
     held_slots, terms, refs = refs[:many], refs[many : 2 * many], refs[2 * many :]
     (
         left_a, left_b, right_a, right_b, right_c, total, total_w, stage, stage_w, from_core, from_chip,
-        ready, core_sent, core_arrived, chip_sent, chip_arrived, out_done, grads_done,
-    ) = refs[:18]
+        gate_rows, router, router_core, router_chip,
+        ready, core_sent, core_arrived, chip_sent, chip_arrived, out_done, grads_done, rows_ready, rest_done,
+        router_sent, router_arrived,
+    ) = refs[:26]
     held = w_gate.shape[0]
     tokens = hs[0].shape[0]
     _, after, before = ring_place(count)
@@ -772,7 +939,7 @@
         [unit_sum.at[k] for k in range(many)],
         held_slots,
         terms,
-        refs[18:],
+        refs[26:],
     )
 
     def tick(hop):
@@ -782,24 +949,39 @@
     def copies(bank, *pairs):
         return [pltpu.make_async_copy(source, target, ready.at[bank, k]) for source, target, k in pairs]
 
-    def load_dh(side, e, bank):
+    def dh_copies(side, e, place, bank):
         return copies(
             bank,
-            (side[1].at[e], left_a.at[bank], 0),
-            (side[2].at[e], left_b.at[bank], 1),
+            (side[1].at[place], left_a.at[bank], 0),
+            (side[2].at[place], left_b.at[bank], 1),
             (w_gate.at[e], right_a.at[bank], 2),
             (w_up.at[e], right_b.at[bank], 3),
         )
 
-    def load_y(side, e, bank):
-        return copies(bank, (side[0].at[e], left_a.at[bank], 0), (w_down.at[e], right_c.at[bank], 4))
+    def y_copies(side, e, place, bank):
+        return copies(bank, (side[0].at[place], left_a.at[bank], 0), (w_down.at[e], right_c.at[bank], 4))
+
+    def load_sum(make, is_far, e, bank):
+        if is_far:
+            pl.when(e < first)(lambda: begin_all(make(far, e, e, bank)))
+            pl.when(e >= first)(lambda: begin_all(make(rest_far, e, e - first, bank)))
+        else:
+            begin_all(make(near, e, e, bank))
 
     def load_w(e, kind, part, bank):
-        side = (near, far)[part // 2]
         rows = pl.ds((part % 2) * tokens, tokens)
-        right = side[(1, 2, 0)[kind]].at[e, rows, :]
+        source = (1, 2, 0)[kind]
+        right = rest_far[source].at[e - first, rows, :] if part // 2 else near[source].at[e, rows, :]
         left = (hs, hs, cots)[kind][part]
         return copies(bank, (right, left_a.at[bank, pl.ds(0, tokens), :], 0), (left, right_c.at[bank], 4))
+
+    def load_expert(e, bank):
+        return copies(
+            bank,
+            (w_gate.at[e], right_a.at[bank], 2),
+            (w_up.at[e], right_b.at[bank], 3),
+            (w_down.at[e], right_c.at[bank], 4),
+        )
 
     def begin_all(made):
         for copy in made:
@@ -841,34 +1023,113 @@
     def far_out(k):
         return pltpu.make_async_copy(from_chip.at[k // 2], outs[3 * (k // 2) + 2], out_done.at[3 * (k // 2) + 2])
 
-    plans = [(load_dh, far), (load_dh, near), (load_y, far), (load_y, near)]
-    begin_all(load_dh(far, 0, 0))
+    far_rows = [
+        pltpu.make_async_copy(source, target, rows_ready.at[k])
+        for k, (source, target) in enumerate(
+            [(hs[2], stage.at[0, 0]), (hs[3], stage.at[0, 1]), (cots[2], stage.at[1, 0]), (cots[3], stage.at[1, 1])]
+            + [(gates[part], gate_rows.at[part]) for part in (0, 1)]
+            + [(router_so_far[part], router.at[part]) for part in (0, 1)]
+        )
+    ]
+    late = held - first
+    tile = tokens // 2
+    lane = lax.broadcasted_iota(jnp.int32, (tile, gates[0].shape[1]), 1)
+
+    def rest_out(e, part, kind):
+        slot = part % 2
+        return pltpu.make_async_copy(
+            left_b.at[slot, pl.ds(kind * tile, tile), :],
+            rest_far[kind].at[e, pl.ds(part * tile, tile), :],
+            rest_done.at[slot, kind],
+        )
+
+    begin_all(far_rows)
+    begin_all(load_expert(first, 0))
     begin(streams)
+    await_all(far_rows)
     hop = 0
-    for k, (loader, side) in enumerate(plans):
+
+    def one_expert(e, carry):
+        bank = e % 2
+        await_all(load_expert(e + first, bank))
+
+        @pl.when(e + 1 < late)
+        def _():
+            begin_all(load_expert(e + 1 + first, 1 - bank))
+
+        mine = lane == holder * held + first + e
+        for part in range(4):
+            block, rows = part // 2, slice((part % 2) * tile, (part % 2 + 1) * tile)
+            results = expert_tile(
+                stage[0, block, rows], stage[1, block, rows], gate_rows[block, rows], mine,
+                right_a[bank], right_b[bank], right_c[bank],
+            )
+            router[block, rows] = jnp.where(mine, results[3], router[block, rows])
+            for kind in range(3):
+                if part >= 2:
+                    rest_out(e, part, kind).wait()
+                else:
+                    pl.when(e > 0)(lambda: rest_out(e, part, kind).wait())
+                left_b[part % 2, kind * tile : (kind + 1) * tile] = results[kind]
+                rest_out(e, part, kind).start()
+
+        @pl.when(e >= 1)
+        def _():
+            tick(hop + e - 1)
+
+        return carry
+
+    lax.fori_loop(0, late, one_expert, 0)
+    hop += late - 1
+    for part in (2, 3):
+        for kind in range(3):
+            rest_out(late - 1, part, kind).wait()
+
+    def router_to_core():
+        return pltpu.make_async_remote_copy(
+            src_ref=router.at[1],
+            dst_ref=router_core,
+            send_sem=router_sent.at[0],
+            recv_sem=router_arrived.at[0],
+            device_id={"ep": core},
+        )
+
+    def router_to_chip():
+        return pltpu.make_async_remote_copy(
+            src_ref=router.at[0],
+            dst_ref=router_chip,
+            send_sem=router_sent.at[1],
+            recv_sem=router_arrived.at[1],
+            device_id={"ep": chip},
+        )
+
+    router_to_core().start()
+    plans = [(dh_copies, True), (dh_copies, False), (y_copies, True), (y_copies, False)]
+    load_sum(dh_copies, True, 0, 0)
+    for k, (make, is_far) in enumerate(plans):
         base = k * held
 
         def next_first(bank, k=k):
             if k + 1 < len(plans):
-                begin_all(plans[k + 1][0](plans[k + 1][1], 0, bank))
+                load_sum(*plans[k + 1], 0, bank)
             else:
                 begin_all(load_w(first, 0, 0, bank))
 
-        every = 2 if loader is load_dh else 3
-
-        def piece(e, carry, k=k, loader=loader, side=side, base=base, hop=hop, every=every, next_first=next_first):
+        every = 3 if make is dh_copies else held + 1
+
+        def piece(e, carry, k=k, make=make, is_far=is_far, base=base, hop=hop, every=every, next_first=next_first):
             bank = (base + e) % 2
-            await_all(loader(side, e, bank))
+            await_all(make(near, e, e, bank))
 
             @pl.when(e + 1 < held)
             def _():
-                begin_all(loader(side, e + 1, 1 - bank))
+                load_sum(make, is_far, e + 1, 1 - bank)
 
             @pl.when(e + 1 == held)
             def _():
                 next_first(1 - bank)
 
-            if loader is load_dh:
+            if make is dh_copies:
                 term = contract(left_a[bank], right_a[bank], 1, 1) + contract(left_b[bank], right_b[bank], 1, 1)
             else:
                 term = contract(left_a[bank], right_c[bank], 1, 0)
@@ -890,6 +1151,10 @@
                 @pl.when(e == 1)
                 def _():
                     send_chip(k - 1)
+                    if k == 1:
+                        router_to_core().wait_recv()
+                        router[0] += router_core[...]
+                        router_to_chip().start()
 
             return carry
 
@@ -950,7 +1215,6 @@
                 tick(hop + 2 * e + kind // 2)
         return carry
 
-    late = held - first
     lax.fori_loop(0, late, expert, 0)
     hop += 2 * late
 
@@ -966,6 +1230,12 @@
     for k in (0, 2):
         to_chip(k).wait_recv()
         far_out(k).start()
+    router_to_chip().wait_recv()
+    router_out = pltpu.make_async_copy(router_chip, router_far, rows_ready.at[0])
+    router_out.start()
+    router_to_core().wait_send()
+    router_to_chip().wait_send()
+    router_out.wait()
     for kind in (kinds - 2, kinds - 1):
         grads_out(late - 1, kind).wait()
     own_out(3).wait()
@@ -978,7 +1248,7 @@
         far_out(k).wait()
 
 
-def overlap(unit, near, far, w_gate, w_up, w_down, hs, cots, first):
+def overlap(unit, near, far, w_gate, w_up, w_down, hs, cots, gates, router_so_far, first):
     many, count, rows3, columns = unit.shape
     tokens, width = hs[0].shape
     held = w_gate.shape[0]
@@ -990,16 +1260,20 @@
         return pltpu.VMEM(shape, jnp.bfloat16)
 
     flops = 2 * tokens * width * columns * (4 * 3 * held + 12 * (held - first))
-    inputs = [unit, *near, *far, w_gate, w_up, w_down, *hs, *cots]
-    unit_sum, grads, *blocks = pl.pallas_call(
+    inputs = [unit, *near, *far, w_gate, w_up, w_down, *hs, *cots, *gates, *router_so_far]
+    late = held - first
+    small = gates[0].shape
+    unit_sum, grads, *blocks, router_far, _, _, _ = pl.pallas_call(
         functools.partial(overlap_kernel, count, first, [shape] * many),
         out_shape=[
             jax.ShapeDtypeStruct(unit.shape, unit.dtype),
             jax.ShapeDtypeStruct((held - first, count, 3, rows3 // 3, columns), jnp.bfloat16),
         ]
-        + [block] * 6,
+        + [block] * 6
+        + [jax.ShapeDtypeStruct(small, jnp.float32)]
+        + [jax.ShapeDtypeStruct((late, 2 * tokens, columns), jnp.bfloat16)] * 3,
         in_specs=[pl.BlockSpec(memory_space=pl.ANY)] * len(inputs),
-        out_specs=[pl.BlockSpec(memory_space=pl.ANY)] * 8,
+        out_specs=[pl.BlockSpec(memory_space=pl.ANY)] * 12,
         scratch_shapes=[
             *[buffers(2, SLOTS, *half)] * many,
             *[buffers(2, 2, *half)] * many,
@@ -1014,12 +1288,20 @@
             buffers(2, count, rows3 // 3, columns),
             buffers(4, tokens, width),
             buffers(2, tokens, width),
+            pltpu.VMEM((2,) + small, jnp.float32),
+            pltpu.VMEM((2,) + small, jnp.float32),
+            pltpu.VMEM(small, jnp.float32),
+            pltpu.VMEM(small, jnp.float32),
             dma((2, 5)),
             dma((4,)),
             dma((4,)),
             dma((2,)),
             dma((2,)),
             dma((6,)),
+            dma((2,)),
+            dma((8,)),
+            dma((2, 3)),
+            dma((2,)),
             dma((2,)),
             dma((2 * many, SLOTS)),
             dma((2 * many, SLOTS)),
@@ -1028,13 +1310,13 @@
             pltpu.SemaphoreType.REGULAR((2 * many,)),
         ],
         compiler_params=pltpu.CompilerParams(
-            collective_id=1, has_side_effects=True, vmem_limit_bytes=VMEM_BYTES
+            collective_id=1, has_side_effects=True, vmem_limit_bytes=60 * 2**20
         ),
         cost_estimate=pl.CostEstimate(flops=flops, bytes_accessed=8 * unit.size, transcendentals=0),
         name="overlap",
     )(*inputs)
     grads = grads.reshape(held - first, count, rows3, columns)
-    return unit_sum, grads, blocks[:3], blocks[3:]
+    return unit_sum, grads, blocks[:3], blocks[3:], router_far
 
 
 def finish_kernel(firsts, *refs):
@@ -1150,32 +1432,45 @@
     h_near = (h_two, swap_core(h_two))
     gates_near = (combine, swap_core(combine))
     h_far, gates_far = swap_chip(h_two), swap_chip(combine)
-    near = expert_pass(h_near, cot_near, gates_near, w_gate, w_up, w_down)
+    near = expert_pass(held, h_near, cot_near, gates_near, w_gate, w_up, w_down)
     near, h_far, gates_far = lax.optimization_barrier((near, h_far, gates_far))
     h_far = (h_far, swap_core(h_far))
     cot_far = (cot_far, swap_core(cot_far))
     gates_far = (gates_far, swap_core(gates_far))
-    far = expert_pass(h_far, cot_far, gates_far, w_gate, w_up, w_down)
+    far = expert_pass(EARLY, h_far, cot_far, gates_far, w_gate, w_up, w_down)
     ghs, dgs, dus = zip(near[:3], far[:3])
     hs, cots = h_near + h_far, cot_near + cot_far
 
     router_own, router_near = near[3], swap_core(near[4])
-    router_far = swap_chip(far[3] + swap_core(far[4]))
     early = weight_grads(replicas, 0, EARLY, hs, cots, ghs, dgs, dus)
-    early, late, (dh_own, dh_near, dh_far), (y_own, y_near, y_far) = overlap(
-        early, near[:3], far[:3], w_gate, w_up, w_down, hs, cots, EARLY
-    )
-    d_resid, d_pre, grad_out = attention_back(
-        dh_own, dh_near, dh_far, router_own, router_near, router_far, routes, probs, resid, norm_ffn, cotangent, w_router, w_out, h_two, attn,
-        queries, keys, values, log_totals, cosine, sine,
-    )
+    early, late, (dh_own, dh_near, dh_far), (y_own, y_near, y_far), router_far = overlap(
+        early, near[:3], far[:3], w_gate, w_up, w_down, hs, cots, gates_far, far[3:], EARLY
+    )
+    sent = ring_chunks(late, 1)
+    arrived = ring_hop(sent, replicas)
+    dh_own, sent = lax.optimization_barrier((dh_own, sent))
+    d_resid, grad_out, d_attn = branch_back(
+        dh_own, dh_near, dh_far, router_own, router_near, router_far, routes, probs, resid, norm_ffn, cotangent,
+        w_router, w_out, h_two, attn,
+    )
+    arrived, d_attn = lax.optimization_barrier((arrived, d_attn))
+    sent = ring_chunks(late, 2, arrived)
+    arrived = ring_hop(sent, replicas)
+    sent, d_attn = lax.optimization_barrier((sent, d_attn))
+    d_pre = attention_back(d_attn, queries, keys, values, log_totals, cosine, sine)
+    arrived, d_pre = lax.optimization_barrier((arrived, d_pre))
+    sent = ring_chunks(late, 3, arrived)
+    arrived = ring_hop(sent, replicas)
+    sent, d_pre = lax.optimization_barrier((sent, d_pre))
     d_input, grad_qkv = input_back(
         d_pre, normed, tokens, norm_attn, d_resid, w_query, key_projection, value_projection
     )
+    arrived, grad_qkv = lax.optimization_barrier((arrived, grad_qkv))
+    initial = ring_chunks(late, 4, arrived)
     mixed = (
         resid + y_own.astype(jnp.float32) + y_near.astype(jnp.float32) + y_far.astype(jnp.float32)
     ).astype(jnp.bfloat16)
-    late, sum_o, sum_qkv = ring_sum(late, [grad_out, grad_qkv])
+    late, sum_o, sum_qkv = ring_sum(late, [grad_out, grad_qkv], 3, initial)
     full_gate, full_up, full_down, sum_o, sum_q, sum_k, sum_v, extra_o, extra_qkv = finish(
         [early, late], [sum_o, sum_qkv], width, key_projection.shape[1]
     )

time: 820 us -> 768 us (0.937)
  Pallas kernels: 774 us -> 718 us
    pallas_call x4 -> x9, Pallas kernels: 452 us -> 399 us  [the longest x1 283 us: ring_sum(): pl.pallas_call(functools.partial(ring_kernel, count, many, 5, start, shap...]
  transfers between devices with their start and end apart: 12 -> 16, of which waited for: 4 -> 3; matrix products, arithmetic and copies ran while one was open for 1% -> 1% of each run, Pallas kernels for 42% -> 52%
where the time goes in v6:
time: 768 us; the launch traced here: 758 us
  Pallas kernels  718 us (93%)
  local copies, waits for them, and re-layouts  13.8 us (2%)
  starting transfers between devices  12.9 us (2%)
    pallas_call x1, Pallas kernels, ring_sum(): pl.pallas_call(functools.partial(ring_kernel, count, many, 5, start, shap...  283 us
    pallas_call x1, Pallas kernels, overlap(): pl.pallas_call(functools.partial(overlap_kernel, count, first, [shape] *...  210 us
    pallas_call x2, Pallas kernels, expert_pass(): pl.pallas_call(functools.partial(expert_kernel, 256, held), grid=(many,),...  51.9 us
    pallas_call x1, Pallas kernels, attention_back(): pl.pallas_call(attention_back_kernel, out_shape=jax.ShapeDtypeStruct((cou...  31.2 us
    pallas_call x1, Pallas kernels, finish(): pl.pallas_call(functools.partial(finish_kernel, firsts), grid=(experts, 4...  31 us
    pallas_call x1, Pallas kernels, attention_forward(): pl.pallas_call(attention_kernel, out_shape=[shape((count, width), jnp.bfl...  30.9 us
    pallas_call x1, Pallas kernels, weight_grads(): pl.pallas_call(weight_kernel, grid=(many, 3), in_specs=[whole(hs[0])] * 8...  29.1 us
    pallas_call x1, Pallas kernels, input_back(): pl.pallas_call(input_kernel, out_shape=[shape((count, width), jnp.float32...  17.9 us
  transfers between devices with their start and end apart: 16, of which 3 were waited for; matrix products, arithmetic and copies ran while one was open for 1% of the time, Pallas kernels for 52%

profile of v6, /device:TPU:0, one launch (start us, length us, event | category | flops | bytes accessed | tf_op | source)
XLA Modules:
  0.0 757.5 jit_solution(10509845956371751548)
XLA Ops:
  0.6 3.0 collective-permute-start
  3.6 1.3 broadcast_in_dim.4.norm_attn
  4.9 1.3 broadcast_in_dim.5.norm_ffn
  8.5 30.9 %attention_forward.1 = (bf16[512,1536]{1,0:T(8,128)(2,1)}, bf16[512,1536]{1,0:T(8,128)(2,1)}, bf16[512,512]{1,0:T(8,128)(2,1)}, bf16[512,512]{1,0:T(8,128)(2,1)}...) custom-call(bf16[512,1536]{1,0:T(8,128)(2,1)} %tokens_in.1, ...), custom_call_target="tpu_custom_call" | custom-call | flops 7247757312 | bytes 18874368 | tf_op jit(solution)/shard_map/attention_forward/pallas_call | solution.py:314
  40.5 1.7 collective-permute-start.5
  42.2 1.9 collective-permute-done.3.gates1
  45.9 34.5 %expert_pass.2 = (bf16[5,1024,512]{2,1,0:T(8,128)(2,1)}, bf16[5,1024,512]{2,1,0:T(8,128)(2,1)}, bf16[5,1024,512]{2,1,0:T(8,128)(2,1)}, f32[512,20]{1,0:T(8,128)}, f32[512,20]{1,0:T(8,128)}) custom-call(bf16[512,1536]{1,0:T(8,128)(2,1)} %get-tuple-element.91.h0.refs_0_.refs_10_.h_two_in, bf16[512,1536]{1,0:T(8,128)(2,1)} %copy-done.11, ...), custom_call_target="tpu_custom_call" | custom-call | flops 24159191040 | bytes 23592960 | tf_op jit(solution)/shard_map/expert_pass/pallas_call | solution.py:103
  80.5 2.2 collective-permute-done.5.gates0.refs_18_
  87.2 17.3 %expert_pass.3 = (bf16[2,1024,512]{2,1,0:T(8,128)(2,1)}, bf16[2,1024,512]{2,1,0:T(8,128)(2,1)}, bf16[2,1024,512]{2,1,0:T(8,128)(2,1)}, f32[512,20]{1,0:T(8,128)}, f32[512,20]{1,0:T(8,128)}) custom-call(bf16[512,1536]{1,0:T(8,128)(2,1)} %collective-permute-done.4.h0.refs_2_.refs_12_, bf16[512,1536]{1,0:T(8,128)(2,1)} %collective-permute-done.6.h1.refs_3_.refs_13_, ...), custom_call_target="tpu_custom_call" | custom-call | flops 9663676416 | bytes 9437184 | tf_op jit(solution)/shard_map/expert_pass/pallas_call | solution.py:103
  104.5 29.1 %weight_grads.1 = bf16[2,8,3,192,512]{4,3,2,1,0:T(8,128)(2,1)} custom-call(bf16[512,1536]{1,0:T(8,128)(2,1)} %get-tuple-element.91.h0.refs_0_.refs_10_.h_two_in, bf16[512,1536]{1,0:T(8,128)(2,1)} %copy-done.11, bf16[512,1536]{1,0:T(8,128)(2,1)} %collective-permute-done.4.h0.refs_2_.refs_12_, bf16[512,1536]{1,0:T(8,128)(2,1)} %collective-permute-done.6.h1.refs_3_.refs_13_, ...), custom_call_target="tpu_custom_call" | custom-call | flops 19327352832 | bytes 22020096 | tf_op jit(solution)/shard_map/weight_grads/pallas_call | solution.py:142
  133.7 210.0 %overlap.1 = (bf16[2,8,576,512]{3,2,1,0:T(8,128)(2,1)}, bf16[3,8,3,192,512]{4,3,2,1,0:T(8,128)(2,1)}, bf16[512,1536]{1,0:T(8,128)(2,1)}, bf16[512,1536]{1,0:T(8,...) custom-call(bf16[2,8,576,512]{3,2,1,0:T(8,128)(2,1)} %bitcast.24, ...), custom_call_target="tpu_custom_call" | custom-call | flops 77309411328 | bytes 37748736 | tf_op jit(solution)/shard_map/overlap/pallas_call | solution.py:1266
  343.6 3.4 ring_chunks.4
  350.0 17.6 %branch_back.1 = (f32[512,1536]{1,0:T(8,128)}, bf16[1536,1792]{1,0:T(8,128)(2,1)}, bf16[512,1536]{1,0:T(8,128)(2,1)}) custom-call(bf16[512,1536]{1,0:T(8,128)(2,1)} %get-tuple-element.116.dh_own, bf16[512,1536]{1,0:T(8,128)(2,1)} %get-tuple-element.117.dh_near, bf16[512,1536]{1,0:T(8,128)(2,1)} %get-tuple-element.118.dh_far, ...), custom_call_target="tpu_custom_call" | custom-call | flops 4831838208 | bytes 18874368 | tf_op jit(solution)/shard_map/branch_back/pallas_call | solution.py:451
  367.7 2.0 add_convert_fusion
  369.6 4.1 ring_chunks.5
  374.6 1.5 collective-permute-start.13
  376.1 31.2 %attention_back.1.d_pre = bf16[512,2560]{1,0:T(8,128)(2,1)} custom-call(bf16[512,1536]{1,0:T(8,128)(2,1)} %get-tuple-element.130.d_attn, bf16[512,1536]{1,0:T(8,128)(2,1)} %get-tuple-element.131.queries, bf16[512,512]{1,0:T(8,128)(2,1)} %get-tuple-element.132.keys, bf16[512,512]{1,0:T(8,128)(2,1)} %get-tuple-element.133.values, ...), custom_call_target="tpu_custom_call" | custom-call | flops 9663676416 | bytes 9437184 | tf_op jit(solution)/shard_map/attention_back/pallas_call | solution.py:484
  409.1 4.1 ring_chunks.6
  415.2 17.9 %input_back.1 = (f32[512,1536]{1,0:T(8,128)}, bf16[1536,2816]{1,0:T(8,128)(2,1)}) custom-call(bf16[512,2560]{1,0:T(8,128)(2,1)} %attention_back.1.d_pre, bf16[512,1536]{1,0:T(8,128)(2,1)} %get-tuple-element.141.normed, bf16[512,1536]{1,0:T(8,128)(2,1)} %tokens_in.1, bf16[1,1536]{1,0:T(2,128)(2,1)} %broadcast_in_dim.4.norm_attn, ...), custom_call_target="tpu_custom_call" | custom-call | flops 9663676416 | bytes 28311552 | tf_op jit(solution)/shard_map/input_back/pallas_call | solution.py:545
  434.3 4.1 ring_chunks.7
  438.4 282.8 %ring_sum.1 = (bf16[3,8,576,512]{3,2,1,0:T(8,128)(2,1)}, bf16[8,48,1792]{2,1,0:T(8,128)(2,1)}, bf16[8,48,2816]{2,1,0:T(8,128)(2,1)}) custom-call(bf16[3,8,576,512]{3,2,1,0:T(8,128)(2,1)} %bitcast.19, bf16[1536,1792]{1,0:T(8,128)(2,1)} %get-tuple-element.145.refs_1_, bf16[1536,2816]{1,0:T(8,128)(2,1)} %get-tuple-element.147.refs_2_, ...), custom_call_target="tpu_custom_call" | custom-call | flops 28311552 | bytes 113246208 | tf_op jit(solution)/shard_map/ring_sum/pallas_call | solution.py:843
  721.2 31.0 %finish.1 = (f32[5,1536,512]{2,1,0:T(8,128)}, f32[5,1536,512]{2,1,0:T(8,128)}, f32[5,512,1536]{2,1,0:T(8,128)}, f32[384,1536]{1,0:T(8,128)}, f32[384,1536]{1,0:T...) custom-call(bf16[2,8,576,512]{3,2,1,0:T(8,128)(2,1)} %get-tuple-element.144.refs_0_,, ...), custom_call_target="tpu_custom_call" | custom-call | tf_op jit(solution)/shard_map/finish/pallas_call | solution.py:1372
  753.1 1.7 slice_reduce_fusion
  755.5 1.7 slice_reduce_fusion.1
  (67 shorter events, 20.0 us)
Async XLA Ops:
  0.6 38.8 %collective-permute-start = (bf16[512,1536]{1,0:T(8,128)(2,1)}, bf16[512,1536]{1,0:T(8,128)(2,1)S(1)}, u32[]{:S(2)}, u32[]{:S(2)}) collective-permute-start(bf16[512,1536]{1,0:T(8,128)(2,1)} %cotangent.1), channel_id=1, source_target_pairs={{0,2},{2,0},{1,3},{3,1},{4,6},{6,4},{5,7},{7,5},{8,10},{10,8},{9,1... | collective-permute-start | bytes 4718600 | tf_op jit(solution)/shard_map/ppermute | solution.py:1399
  3.6 38.5 %collective-permute-start.2 = (bf16[512,1536]{1,0:T(8,128)(2,1)}, bf16[512,1536]{1,0:T(8,128)(2,1)S(1)}, u32[]{:S(2)}, u32[]{:S(2)}) collective-permute-start(bf16[512,1536]{1,0:T(8,128)(2,1)} %cotangent.1), channel_id=1, source_target_pairs={{0,1},{1,0},{2,3},{3,2},{4,5},{5,4},{6,7},{7,6},{8,9},{9,8},{10,11... | collective-permute-start | bytes 4718600 | tf_op jit(solution)/shard_map/ppermute | solution.py:1395
  39.5 41.0 %copy-start.9 = (bf16[512,1536]{1,0:T(8,128)(2,1)}, bf16[512,1536]{1,0:T(8,128)(2,1)S(1)}, u32[]{:S(2)}) copy-start(bf16[512,1536]{1,0:T(8,128)(2,1)S(1)} %collective-permute-done.c0.refs_6_.refs_16_) | copy-start | bytes 4718596
  39.5 4.6 collective-permute-start.1
  40.1 4.0 collective-permute-start.3
  40.1 42.6 %collective-permute-start.4 = (bf16[512,1536]{1,0:T(8,128)(2,1)}, bf16[512,1536]{1,0:T(8,128)(2,1)}, u32[]{:S(2)}, u32[]{:S(2)}) collective-permute-start(bf16[512,1536]{1,0:T(8,128)(2,1)} %get-tuple-element.91.h0.refs_0_.refs_10_.h_two_in), channel_id=1, source_target_pairs={{0,2},{2,0},{1,3},{3,1},{4,6},{6,4},{5,7},{7,5},{8,10},{10,8},{9,1... | collective-permute-start | bytes 4718600 | tf_op jit(solution)/shard_map/ppermute | solution.py:1399
  40.5 42.2 %collective-permute-start.5 = (f32[512,20]{1,0:T(8,128)}, f32[512,20]{1,0:T(8,128)S(1)}, u32[]{:S(2)}, u32[]{:S(2)}) collective-permute-start(f32[512,20]{1,0:T(8,128)} %get-tuple-element.92.gates0), channel_id=1, source_target_pairs={{0,2},{2,0},{1,3},{3,1},{4,6},{6,4},{5,7},{7,5},{8,10},{10,8},{9,1... | collective-permute-start | bytes 122888 | tf_op jit(solution)/shard_map/ppermute | solution.py:1399
  42.2 1.9 copy-start.10
  42.2 43.6 %collective-permute-start.7 = (bf16[512,1536]{1,0:T(8,128)(2,1)S(1)}, bf16[512,1536]{1,0:T(8,128)(2,1)}, u32[]{:S(2)}, u32[]{:S(2)}) collective-permute-start(bf16[512,1536]{1,0:T(8,128)(2,1)S(1)} %collective-permute-done.c0.refs_6_.refs_16_), channel_id=1, source_target_pairs={{0,1},{1,0},{2,3},{3,2},{4,5},{5,4},{6,7},{7,6},{8,9},{9,8},{10,11... | collective-permute-start | bytes 4718600 | tf_op jit(solution)/shard_map/ppermute | solution.py:1395
  82.7 3.8 copy-start.12
  82.7 3.8 collective-permute-start.6
  84.7 1.8 collective-permute-start.8
  85.7 263.6 %collective-permute-start.11 = (f32[512,20]{1,0:T(8,128)}, f32[512,20]{1,0:T(8,128)S(1)}, u32[]{:S(2)}, u32[]{:S(2)}) collective-permute-start(f32[512,20]{1,0:T(8,128)} %get-tuple-element.120), channel_id=1, source_target_pairs={{0,1},{1,0},{2,3},{3,2},{4,5},{5,4},{6,7},{7,6},{8,9},{9,8},{10,11... | collective-permute-start | bytes 122888 | tf_op jit(solution)/shard_map/ppermute | solution.py:1395
  347.1 22.6 %collective-permute-start.10 = (bf16[3,576,256]{2,1,0:T(8,128)(2,1)}, bf16[3,576,256]{2,1,0:T(8,128)(2,1)}, u32[]{:S(2)}, u32[]{:S(2)}) collective-permute-start(bf16[3,576,256]{2,1,0:T(8,128)(2,1)} %get-tuple-element.114), channel_id=1, source_target_pairs={{8,0},{16,8},{24,16},{28,24},{20,28},{12,20},{4,12},{0,4},{9,1},{1... | collective-permute-start | bytes 2654216 | tf_op jit(solution)/shard_map/ppermute | solution.py:911
  348.0 21.6 %collective-permute-start.9 = (bf16[3,576,256]{2,1,0:T(8,128)(2,1)}, bf16[3,576,256]{2,1,0:T(8,128)(2,1)}, u32[]{:S(2)}, u32[]{:S(2)}) collective-permute-start(bf16[3,576,256]{2,1,0:T(8,128)(2,1)} %get-tuple-element.113), channel_id=1, source_target_pairs={{0,8},{8,16},{16,24},{24,28},{28,20},{20,12},{12,4},{4,0},{1,9},{9... | collective-permute-start | bytes 2654216 | tf_op jit(solution)/shard_map/ppermute | solution.py:911
  350.0 17.6 %copy-start = (f32[512,1536]{1,0:T(8,128)S(1)}, f32[512,1536]{1,0:T(8,128)}, u32[]{:S(2)}) copy-start(f32[512,1536]{1,0:T(8,128)} %get-tuple-element.88.resid) | copy-start | bytes 9437188
  350.0 17.7 %copy-start.1 = (bf16[512,1536]{1,0:T(8,128)(2,1)S(1)}, bf16[512,1536]{1,0:T(8,128)(2,1)}, u32[]{:S(2)}) copy-start(bf16[512,1536]{1,0:T(8,128)(2,1)} %get-tuple-element.109) | copy-start | bytes 4718596
  350.0 17.7 %copy-start.2 = (bf16[512,1536]{1,0:T(8,128)(2,1)S(1)}, bf16[512,1536]{1,0:T(8,128)(2,1)}, u32[]{:S(2)}) copy-start(bf16[512,1536]{1,0:T(8,128)(2,1)} %get-tuple-element.110) | copy-start | bytes 4718596
  350.0 17.7 %copy-start.3 = (bf16[512,1536]{1,0:T(8,128)(2,1)S(1)}, bf16[512,1536]{1,0:T(8,128)(2,1)}, u32[]{:S(2)}) copy-start(bf16[512,1536]{1,0:T(8,128)(2,1)} %get-tuple-element.111) | copy-start | bytes 4718596
  373.7 33.6 %collective-permute-start.12 = (bf16[3,576,256]{2,1,0:T(8,128)(2,1)}, bf16[3,576,256]{2,1,0:T(8,128)(2,1)S(1)}, u32[]{:S(2)}, u32[]{:S(2)}) collective-permute-start(bf16[3,576,256]{2,1,0:T(8,128)(2,1)} %get-tuple-element.127), channel_id=1, source_target_pairs={{0,8},{8,16},{16,24},{24,28},{28,20},{20,12},{12,4},{4,0},{1,9},{9... | collective-permute-start | bytes 2654216 | tf_op jit(solution)/shard_map/ppermute | solution.py:911
  374.6 32.7 %collective-permute-start.13 = (bf16[3,576,256]{2,1,0:T(8,128)(2,1)}, bf16[3,576,256]{2,1,0:T(8,128)(2,1)S(1)}, u32[]{:S(2)}, u32[]{:S(2)}) collective-permute-start(bf16[3,576,256]{2,1,0:T(8,128)(2,1)} %get-tuple-element.128), channel_id=1, source_target_pairs={{8,0},{16,8},{24,16},{28,24},{20,28},{12,20},{4,12},{0,4},{9,1},{1... | collective-permute-start | bytes 2654216 | tf_op jit(solution)/shard_map/ppermute | solution.py:911
  413.2 19.9 %collective-permute-start.14 = (bf16[3,576,256]{2,1,0:T(8,128)(2,1)}, bf16[3,576,256]{2,1,0:T(8,128)(2,1)S(1)}, u32[]{:S(2)}, u32[]{:S(2)}) collective-permute-start(bf16[3,576,256]{2,1,0:T(8,128)(2,1)} %get-tuple-element.137), channel_id=1, source_target_pairs={{0,8},{8,16},{16,24},{24,28},{28,20},{20,12},{12,4},{4,0},{1,9},{9... | collective-permute-start | bytes 2654216 | tf_op jit(solution)/shard_map/ppermute | solution.py:911
  414.0 19.1 %collective-permute-start.15 = (bf16[3,576,256]{2,1,0:T(8,128)(2,1)}, bf16[3,576,256]{2,1,0:T(8,128)(2,1)S(1)}, u32[]{:S(2)}, u32[]{:S(2)}) collective-permute-start(bf16[3,576,256]{2,1,0:T(8,128)(2,1)} %get-tuple-element.138), channel_id=1, source_target_pairs={{8,0},{16,8},{24,16},{28,24},{20,28},{12,20},{4,12},{0,4},{9,1},{1... | collective-permute-start | bytes 2654216 | tf_op jit(solution)/shard_map/ppermute | solution.py:911
  433.1 1.2 copy-start.7
  (7 other events, 6.0 us)

commit v7 on v6

--- a/solution.py
+++ b/solution.py
@@ -942,9 +942,12 @@
         refs[26:],
     )
 
-    def tick(hop):
-        pl.when(hop < count - 1)(lambda: add_step(streams, hop))
-        pl.when((hop >= count - 1) & (hop < hops))(lambda: hand_step(streams, hop))
+    def tick(step):
+        hop = step // many
+        for k in range(many):
+            turn = step % many == k
+            pl.when(turn & (hop < count - 1))(lambda: add_step(both_ways([k]), hop))
+            pl.when(turn & (hop >= count - 1) & (hop < hops))(lambda: hand_step(both_ways([k]), hop))
 
     def copies(bank, *pairs):
         return [pltpu.make_async_copy(source, target, ready.at[bank, k]) for source, target, k in pairs]
@@ -1047,7 +1050,7 @@
     begin_all(load_expert(first, 0))
     begin(streams)
     await_all(far_rows)
-    hop = 0
+    step = 0
 
     def one_expert(e, carry):
         bank = e % 2
@@ -1072,15 +1075,16 @@
                     pl.when(e > 0)(lambda: rest_out(e, part, kind).wait())
                 left_b[part % 2, kind * tile : (kind + 1) * tile] = results[kind]
                 rest_out(e, part, kind).start()
-
-        @pl.when(e >= 1)
-        def _():
-            tick(hop + e - 1)
+            if part % 2 == 1:
+
+                @pl.when(e >= 1)
+                def _():
+                    tick(step + 2 * (e - 1) + part // 2)
 
         return carry
 
     lax.fori_loop(0, late, one_expert, 0)
-    hop += late - 1
+    step += 2 * (late - 1)
     for part in (2, 3):
         for kind in range(3):
             rest_out(late - 1, part, kind).wait()
@@ -1115,9 +1119,9 @@
             else:
                 begin_all(load_w(first, 0, 0, bank))
 
-        every = 3 if make is dh_copies else held + 1
-
-        def piece(e, carry, k=k, make=make, is_far=is_far, base=base, hop=hop, every=every, next_first=next_first):
+        every = 1 if make is dh_copies else 2
+
+        def piece(e, carry, k=k, make=make, is_far=is_far, base=base, step=step, every=every, next_first=next_first):
             bank = (base + e) % 2
             await_all(make(near, e, e, bank))
 
@@ -1144,7 +1148,7 @@
 
             @pl.when((e + 1) % every == 0)
             def _():
-                tick(hop + e // every)
+                tick(step + e // every)
 
             if k % 2 == 1:
 
@@ -1159,7 +1163,7 @@
             return carry
 
         lax.fori_loop(0, held, piece, 0)
-        hop += held // every
+        step += held // every
         if k >= 2:
             to_core(k - 2).wait_send()
             if k == 2:
@@ -1171,8 +1175,9 @@
         to_core(k).start()
         if k % 2 == 1:
             own_out(k).start()
-        tick(hop)
-        hop += 1
+        if make is y_copies:
+            tick(step)
+            step += 1
 
     kinds = 3
     base = len(plans) * held
@@ -1211,18 +1216,17 @@
             for j in range(count):
                 stage_w[slot, j] = total_w[j * rows : (j + 1) * rows].astype(jnp.bfloat16)
             grads_out(e, kind).start()
-            if kind != 1:
-                tick(hop + 2 * e + kind // 2)
+            tick(step + kinds * e + kind)
         return carry
 
     lax.fori_loop(0, late, expert, 0)
-    hop += 2 * late
-
-    def drain(step, carry):
-        tick(step)
+    step += kinds * late
+
+    def drain(later, carry):
+        tick(later)
         return carry
 
-    lax.fori_loop(hop, max(hop, hops), drain, 0)
+    lax.fori_loop(step, max(step, many * hops), drain, 0)
     end(streams)
     for k in (1, 3):
         to_core(k).wait_recv()

time: 768 us -> 760 us (0.990)
  Pallas kernels: 718 us -> 709 us
    pallas_call x1, Pallas kernels: 210 us -> 198 us  [overlap(): pl.pallas_call(functools.partial(overlap_kernel, count, first, [shape] *...]
  transfers between devices with their start and end apart: 16 -> 16, of which waited for: 3 -> 4; matrix products, arithmetic and copies ran while one was open for 1% -> 1% of each run, Pallas kernels for 52% -> 51%
where the time goes in v7:
time: 760 us; the launch traced here: 749 us
  Pallas kernels  709 us (93%)
  local copies, waits for them, and re-layouts  13.6 us (2%)
  starting transfers between devices  12.9 us (2%)
    pallas_call x1, Pallas kernels, ring_sum(): pl.pallas_call(functools.partial(ring_kernel, count, many, 5, start, shap...  286 us
    pallas_call x1, Pallas kernels, overlap(): pl.pallas_call(functools.partial(overlap_kernel, count, first, [shape] *...  198 us
    pallas_call x2, Pallas kernels, expert_pass(): pl.pallas_call(functools.partial(expert_kernel, 256, held), grid=(many,),...  51.9 us
    pallas_call x1, Pallas kernels, attention_back(): pl.pallas_call(attention_back_kernel, out_shape=jax.ShapeDtypeStruct((cou...  31.2 us
    pallas_call x1, Pallas kernels, finish(): pl.pallas_call(functools.partial(finish_kernel, firsts), grid=(experts, 4...  31 us
    pallas_call x1, Pallas kernels, attention_forward(): pl.pallas_call(attention_kernel, out_shape=[shape((count, width), jnp.bfl...  30.9 us
    pallas_call x1, Pallas kernels, weight_grads(): pl.pallas_call(weight_kernel, grid=(many, 3), in_specs=[whole(hs[0])] * 8...  29.1 us
    pallas_call x1, Pallas kernels, input_back(): pl.pallas_call(input_kernel, out_shape=[shape((count, width), jnp.float32...  17.9 us
  transfers between devices with their start and end apart: 16, of which 4 were waited for; matrix products, arithmetic and copies ran while one was open for 1% of the time, Pallas kernels for 51%

profile of v7, /device:TPU:0, one launch (start us, length us, event | category | flops | bytes accessed | tf_op | source)
XLA Modules:
  0.0 749.2 jit_solution(10430339819538986427)
XLA Ops:
  0.6 3.0 collective-permute-start
  8.5 30.9 %attention_forward.1 = (bf16[512,1536]{1,0:T(8,128)(2,1)}, bf16[512,1536]{1,0:T(8,128)(2,1)}, bf16[512,512]{1,0:T(8,128)(2,1)}, bf16[512,512]{1,0:T(8,128)(2,1)}...) custom-call(bf16[512,1536]{1,0:T(8,128)(2,1)} %tokens_in.1, ...), custom_call_target="tpu_custom_call" | custom-call | flops 7247757312 | bytes 18874368 | tf_op jit(solution)/shard_map/attention_forward/pallas_call | solution.py:314
  40.5 1.7 collective-permute-start.5
  42.2 1.9 collective-permute-done.3.gates1
  45.9 34.5 %expert_pass.2 = (bf16[5,1024,512]{2,1,0:T(8,128)(2,1)}, bf16[5,1024,512]{2,1,0:T(8,128)(2,1)}, bf16[5,1024,512]{2,1,0:T(8,128)(2,1)}, f32[512,20]{1,0:T(8,128)}, f32[512,20]{1,0:T(8,128)}) custom-call(bf16[512,1536]{1,0:T(8,128)(2,1)} %get-tuple-element.91.h0.refs_0_.refs_10_.h_two_in, bf16[512,1536]{1,0:T(8,128)(2,1)} %copy-done.11, ...), custom_call_target="tpu_custom_call" | custom-call | flops 24159191040 | bytes 23592960 | tf_op jit(solution)/shard_map/expert_pass/pallas_call | solution.py:103
  80.5 2.2 collective-permute-done.5.gates0.refs_18_
  87.2 17.3 %expert_pass.3 = (bf16[2,1024,512]{2,1,0:T(8,128)(2,1)}, bf16[2,1024,512]{2,1,0:T(8,128)(2,1)}, bf16[2,1024,512]{2,1,0:T(8,128)(2,1)}, f32[512,20]{1,0:T(8,128)}, f32[512,20]{1,0:T(8,128)}) custom-call(bf16[512,1536]{1,0:T(8,128)(2,1)} %collective-permute-done.4.h0.refs_2_.refs_12_, bf16[512,1536]{1,0:T(8,128)(2,1)} %collective-permute-done.6.h1.refs_3_.refs_13_, ...), custom_call_target="tpu_custom_call" | custom-call | flops 9663676416 | bytes 9437184 | tf_op jit(solution)/shard_map/expert_pass/pallas_call | solution.py:103
  104.5 29.1 %weight_grads.1 = bf16[2,8,3,192,512]{4,3,2,1,0:T(8,128)(2,1)} custom-call(bf16[512,1536]{1,0:T(8,128)(2,1)} %get-tuple-element.91.h0.refs_0_.refs_10_.h_two_in, bf16[512,1536]{1,0:T(8,128)(2,1)} %copy-done.11, bf16[512,1536]{1,0:T(8,128)(2,1)} %collective-permute-done.4.h0.refs_2_.refs_12_, bf16[512,1536]{1,0:T(8,128)(2,1)} %collective-permute-done.6.h1.refs_3_.refs_13_, ...), custom_call_target="tpu_custom_call" | custom-call | flops 19327352832 | bytes 22020096 | tf_op jit(solution)/shard_map/weight_grads/pallas_call | solution.py:142
  133.7 198.1 %overlap.1 = (bf16[2,8,576,512]{3,2,1,0:T(8,128)(2,1)}, bf16[3,8,3,192,512]{4,3,2,1,0:T(8,128)(2,1)}, bf16[512,1536]{1,0:T(8,128)(2,1)}, bf16[512,1536]{1,0:T(8,...) custom-call(bf16[2,8,576,512]{3,2,1,0:T(8,128)(2,1)} %bitcast.24, ...), custom_call_target="tpu_custom_call" | custom-call | flops 77309411328 | bytes 37748736 | tf_op jit(solution)/shard_map/overlap/pallas_call | solution.py:1270
  331.8 3.4 ring_chunks.4
  336.1 1.3 collective-permute-start.9
  338.1 17.6 %branch_back.1 = (f32[512,1536]{1,0:T(8,128)}, bf16[1536,1792]{1,0:T(8,128)(2,1)}, bf16[512,1536]{1,0:T(8,128)(2,1)}) custom-call(bf16[512,1536]{1,0:T(8,128)(2,1)} %get-tuple-element.116.dh_own, bf16[512,1536]{1,0:T(8,128)(2,1)} %get-tuple-element.117.dh_near, bf16[512,1536]{1,0:T(8,128)(2,1)} %get-tuple-element.118.dh_far, ...), custom_call_target="tpu_custom_call" | custom-call | flops 4831838208 | bytes 18874368 | tf_op jit(solution)/shard_map/branch_back/pallas_call | solution.py:451
  355.8 2.0 add_convert_fusion
  357.8 4.1 ring_chunks.5
  361.9 1.6 collective-permute-start.12
  364.3 31.2 %attention_back.1.d_pre = bf16[512,2560]{1,0:T(8,128)(2,1)} custom-call(bf16[512,1536]{1,0:T(8,128)(2,1)} %get-tuple-element.130.d_attn, bf16[512,1536]{1,0:T(8,128)(2,1)} %get-tuple-element.131.queries, bf16[512,512]{1,0:T(8,128)(2,1)} %get-tuple-element.132.keys, bf16[512,512]{1,0:T(8,128)(2,1)} %get-tuple-element.133.values, ...), custom_call_target="tpu_custom_call" | custom-call | flops 9663676416 | bytes 9437184 | tf_op jit(solution)/shard_map/attention_back/pallas_call | solution.py:484
  397.3 4.1 ring_chunks.6
  401.3 1.6 collective-permute-start.14
  403.4 17.9 %input_back.1 = (f32[512,1536]{1,0:T(8,128)}, bf16[1536,2816]{1,0:T(8,128)(2,1)}) custom-call(bf16[512,2560]{1,0:T(8,128)(2,1)} %attention_back.1.d_pre, bf16[512,1536]{1,0:T(8,128)(2,1)} %get-tuple-element.141.normed, bf16[512,1536]{1,0:T(8,128)(2,1)} %tokens_in.1, bf16[1,1536]{1,0:T(2,128)(2,1)} %broadcast_in_dim.4.norm_attn, ...), custom_call_target="tpu_custom_call" | custom-call | flops 9663676416 | bytes 28311552 | tf_op jit(solution)/shard_map/input_back/pallas_call | solution.py:545
  423.0 4.1 ring_chunks.7
  427.1 285.7 %ring_sum.1 = (bf16[3,8,576,512]{3,2,1,0:T(8,128)(2,1)}, bf16[8,48,1792]{2,1,0:T(8,128)(2,1)}, bf16[8,48,2816]{2,1,0:T(8,128)(2,1)}) custom-call(bf16[3,8,576,512]{3,2,1,0:T(8,128)(2,1)} %bitcast.19, bf16[1536,1792]{1,0:T(8,128)(2,1)} %get-tuple-element.145.refs_1_, bf16[1536,2816]{1,0:T(8,128)(2,1)} %get-tuple-element.147.refs_2_, ...), custom_call_target="tpu_custom_call" | custom-call | flops 28311552 | bytes 113246208 | tf_op jit(solution)/shard_map/ring_sum/pallas_call | solution.py:843
  712.8 31.0 %finish.1 = (f32[5,1536,512]{2,1,0:T(8,128)}, f32[5,1536,512]{2,1,0:T(8,128)}, f32[5,512,1536]{2,1,0:T(8,128)}, f32[384,1536]{1,0:T(8,128)}, f32[384,1536]{1,0:T...) custom-call(bf16[2,8,576,512]{3,2,1,0:T(8,128)(2,1)} %get-tuple-element.144.refs_0_,, ...), custom_call_target="tpu_custom_call" | custom-call | tf_op jit(solution)/shard_map/finish/pallas_call | solution.py:1376
  744.7 1.7 slice_reduce_fusion
  747.1 1.7 slice_reduce_fusion.1
  (67 shorter events, 20.2 us)
Async XLA Ops:
  0.6 38.8 %collective-permute-start = (bf16[512,1536]{1,0:T(8,128)(2,1)}, bf16[512,1536]{1,0:T(8,128)(2,1)S(1)}, u32[]{:S(2)}, u32[]{:S(2)}) collective-permute-start(bf16[512,1536]{1,0:T(8,128)(2,1)} %cotangent.1), channel_id=1, source_target_pairs={{0,2},{2,0},{1,3},{3,1},{4,6},{6,4},{5,7},{7,5},{8,10},{10,8},{9,1... | collective-permute-start | bytes 4718600 | tf_op jit(solution)/shard_map/ppermute | solution.py:1403
  3.6 38.5 %collective-permute-start.2 = (bf16[512,1536]{1,0:T(8,128)(2,1)}, bf16[512,1536]{1,0:T(8,128)(2,1)S(1)}, u32[]{:S(2)}, u32[]{:S(2)}) collective-permute-start(bf16[512,1536]{1,0:T(8,128)(2,1)} %cotangent.1), channel_id=1, source_target_pairs={{0,1},{1,0},{2,3},{3,2},{4,5},{5,4},{6,7},{7,6},{8,9},{9,8},{10,11... | collective-permute-start | bytes 4718600 | tf_op jit(solution)/shard_map/ppermute | solution.py:1399
  39.5 41.0 %copy-start.9 = (bf16[512,1536]{1,0:T(8,128)(2,1)}, bf16[512,1536]{1,0:T(8,128)(2,1)S(1)}, u32[]{:S(2)}) copy-start(bf16[512,1536]{1,0:T(8,128)(2,1)S(1)} %collective-permute-done.c0.refs_6_.refs_16_) | copy-start | bytes 4718596
  39.5 4.6 collective-permute-start.1
  40.1 4.0 collective-permute-start.3
  40.1 42.6 %collective-permute-start.4 = (bf16[512,1536]{1,0:T(8,128)(2,1)}, bf16[512,1536]{1,0:T(8,128)(2,1)}, u32[]{:S(2)}, u32[]{:S(2)}) collective-permute-start(bf16[512,1536]{1,0:T(8,128)(2,1)} %get-tuple-element.91.h0.refs_0_.refs_10_.h_two_in), channel_id=1, source_target_pairs={{0,2},{2,0},{1,3},{3,1},{4,6},{6,4},{5,7},{7,5},{8,10},{10,8},{9,1... | collective-permute-start | bytes 4718600 | tf_op jit(solution)/shard_map/ppermute | solution.py:1403
  40.5 42.2 %collective-permute-start.5 = (f32[512,20]{1,0:T(8,128)}, f32[512,20]{1,0:T(8,128)S(1)}, u32[]{:S(2)}, u32[]{:S(2)}) collective-permute-start(f32[512,20]{1,0:T(8,128)} %get-tuple-element.92.gates0), channel_id=1, source_target_pairs={{0,2},{2,0},{1,3},{3,1},{4,6},{6,4},{5,7},{7,5},{8,10},{10,8},{9,1... | collective-permute-start | bytes 122888 | tf_op jit(solution)/shard_map/ppermute | solution.py:1403
  42.2 1.9 copy-start.10
  42.2 43.6 %collective-permute-start.7 = (bf16[512,1536]{1,0:T(8,128)(2,1)S(1)}, bf16[512,1536]{1,0:T(8,128)(2,1)}, u32[]{:S(2)}, u32[]{:S(2)}) collective-permute-start(bf16[512,1536]{1,0:T(8,128)(2,1)S(1)} %collective-permute-done.c0.refs_6_.refs_16_), channel_id=1, source_target_pairs={{0,1},{1,0},{2,3},{3,2},{4,5},{5,4},{6,7},{7,6},{8,9},{9,8},{10,11... | collective-permute-start | bytes 4718600 | tf_op jit(solution)/shard_map/ppermute | solution.py:1399
  44.8 1.2 copy-start.11
  82.7 3.8 copy-start.12
  82.7 3.8 collective-permute-start.6
  84.7 1.8 collective-permute-start.8
  85.7 251.8 %collective-permute-start.11 = (f32[512,20]{1,0:T(8,128)}, f32[512,20]{1,0:T(8,128)S(1)}, u32[]{:S(2)}, u32[]{:S(2)}) collective-permute-start(f32[512,20]{1,0:T(8,128)} %get-tuple-element.120), channel_id=1, source_target_pairs={{0,1},{1,0},{2,3},{3,2},{4,5},{5,4},{6,7},{7,6},{8,9},{9,8},{10,11... | collective-permute-start | bytes 122888 | tf_op jit(solution)/shard_map/ppermute | solution.py:1399
  335.2 22.6 %collective-permute-start.10 = (bf16[3,576,256]{2,1,0:T(8,128)(2,1)}, bf16[3,576,256]{2,1,0:T(8,128)(2,1)}, u32[]{:S(2)}, u32[]{:S(2)}) collective-permute-start(bf16[3,576,256]{2,1,0:T(8,128)(2,1)} %get-tuple-element.114), channel_id=1, source_target_pairs={{8,0},{16,8},{24,16},{28,24},{20,28},{12,20},{4,12},{0,4},{9,1},{1... | collective-permute-start | bytes 2654216 | tf_op jit(solution)/shard_map/ppermute | solution.py:911
  336.1 21.7 %collective-permute-start.9 = (bf16[3,576,256]{2,1,0:T(8,128)(2,1)}, bf16[3,576,256]{2,1,0:T(8,128)(2,1)}, u32[]{:S(2)}, u32[]{:S(2)}) collective-permute-start(bf16[3,576,256]{2,1,0:T(8,128)(2,1)} %get-tuple-element.113), channel_id=1, source_target_pairs={{0,8},{8,16},{16,24},{24,28},{28,20},{20,12},{12,4},{4,0},{1,9},{9... | collective-permute-start | bytes 2654216 | tf_op jit(solution)/shard_map/ppermute | solution.py:911
  338.1 17.6 %copy-start = (f32[512,1536]{1,0:T(8,128)S(1)}, f32[512,1536]{1,0:T(8,128)}, u32[]{:S(2)}) copy-start(f32[512,1536]{1,0:T(8,128)} %get-tuple-element.88.resid) | copy-start | bytes 9437188
  338.1 17.6 %copy-start.1 = (bf16[512,1536]{1,0:T(8,128)(2,1)S(1)}, bf16[512,1536]{1,0:T(8,128)(2,1)}, u32[]{:S(2)}) copy-start(bf16[512,1536]{1,0:T(8,128)(2,1)} %get-tuple-element.109) | copy-start | bytes 4718596
  338.1 17.7 %copy-start.2 = (bf16[512,1536]{1,0:T(8,128)(2,1)S(1)}, bf16[512,1536]{1,0:T(8,128)(2,1)}, u32[]{:S(2)}) copy-start(bf16[512,1536]{1,0:T(8,128)(2,1)} %get-tuple-element.110) | copy-start | bytes 4718596
  338.1 17.7 %copy-start.3 = (bf16[512,1536]{1,0:T(8,128)(2,1)S(1)}, bf16[512,1536]{1,0:T(8,128)(2,1)}, u32[]{:S(2)}) copy-start(bf16[512,1536]{1,0:T(8,128)(2,1)} %get-tuple-element.111) | copy-start | bytes 4718596
  361.9 33.6 %collective-permute-start.12 = (bf16[3,576,256]{2,1,0:T(8,128)(2,1)}, bf16[3,576,256]{2,1,0:T(8,128)(2,1)S(1)}, u32[]{:S(2)}, u32[]{:S(2)}) collective-permute-start(bf16[3,576,256]{2,1,0:T(8,128)(2,1)} %get-tuple-element.127), channel_id=1, source_target_pairs={{0,8},{8,16},{16,24},{24,28},{28,20},{20,12},{12,4},{4,0},{1,9},{9... | collective-permute-start | bytes 2654216 | tf_op jit(solution)/shard_map/ppermute | solution.py:911
  363.4 32.0 %collective-permute-start.13 = (bf16[3,576,256]{2,1,0:T(8,128)(2,1)}, bf16[3,576,256]{2,1,0:T(8,128)(2,1)S(1)}, u32[]{:S(2)}, u32[]{:S(2)}) collective-permute-start(bf16[3,576,256]{2,1,0:T(8,128)(2,1)} %get-tuple-element.128), channel_id=1, source_target_pairs={{8,0},{16,8},{24,16},{28,24},{20,28},{12,20},{4,12},{0,4},{9,1},{1... | collective-permute-start | bytes 2654216 | tf_op jit(solution)/shard_map/ppermute | solution.py:911
  401.3 19.9 %collective-permute-start.14 = (bf16[3,576,256]{2,1,0:T(8,128)(2,1)}, bf16[3,576,256]{2,1,0:T(8,128)(2,1)S(1)}, u32[]{:S(2)}, u32[]{:S(2)}) collective-permute-start(bf16[3,576,256]{2,1,0:T(8,128)(2,1)} %get-tuple-element.137), channel_id=1, source_target_pairs={{0,8},{8,16},{16,24},{24,28},{28,20},{20,12},{12,4},{4,0},{1,9},{9... | collective-permute-start | bytes 2654216 | tf_op jit(solution)/shard_map/ppermute | solution.py:911
  402.9 19.1 %collective-permute-start.15 = (bf16[3,576,256]{2,1,0:T(8,128)(2,1)}, bf16[3,576,256]{2,1,0:T(8,128)(2,1)S(1)}, u32[]{:S(2)}, u32[]{:S(2)}) collective-permute-start(bf16[3,576,256]{2,1,0:T(8,128)(2,1)} %get-tuple-element.138), channel_id=1, source_target_pairs={{8,0},{16,8},{24,16},{28,24},{20,28},{12,20},{4,12},{0,4},{9,1},{1... | collective-permute-start | bytes 2654216 | tf_op jit(solution)/shard_map/ppermute | solution.py:911
  (7 other events, 5.7 us)

commit v8 on v7

--- a/solution.py
+++ b/solution.py
@@ -71,7 +71,7 @@
 
 def expert_kernel(tile, held, h0, h1, c0, c1, gates0, gates1, w_gate, w_up, w_down, gh, dg, du, d_router0, d_router1):
     e = pl.program_id(0)
-    tokens, lanes = gates0.shape
+    lanes, tokens = gates0.shape
     expert = lax.axis_index("ep") * held + e
     lane = lax.broadcasted_iota(jnp.int32, (tile, lanes), 1)
 
@@ -88,7 +88,7 @@
             rows = slice(start, start + tile)
             out = slice(base + start, base + start + tile)
             results = expert_tile(
-                rows_h[rows, :], rows_c[rows, :], gates[rows, :], lane == expert, w_gate[0], w_up[0], w_down[0]
+                rows_h[rows, :], rows_c[rows, :], gates[:, rows].T, lane == expert, w_gate[0], w_up[0], w_down[0]
             )
             gh[0, out, :], dg[0, out, :], du[0, out, :] = results[:3]
             d_router[rows, :] = jnp.where(lane == expert, results[3], d_router[rows, :])
@@ -99,7 +99,7 @@
     tokens = 2 * count
     held, _, hidden_units = w_gate.shape
     part = jax.ShapeDtypeStruct((many, tokens, hidden_units), jnp.bfloat16)
-    gate_shape = gates[0].shape
+    gate_shape = gates[0].shape[::-1]
     return pl.pallas_call(
         functools.partial(expert_kernel, 256, held),
         grid=(many,),
@@ -298,7 +298,7 @@
     shifted = jnp.exp(logits - jnp.max(logits, -1, keepdims=True))
     soft = shifted / jnp.sum(shifted, -1, keepdims=True)
     probs[...] = soft
-    combine[...] = jnp.where(chosen_of(routes, logits.shape), soft, 0.0)
+    combine[...] = jnp.where(chosen_of(routes, logits.shape), soft, 0.0).T
     for result in results:
         result.wait()
 
@@ -323,7 +323,7 @@
             shape((count, width), jnp.float32),
             shape((count, width), jnp.bfloat16),
             shape((count, experts), jnp.float32),
-            shape((count, experts), jnp.float32),
+            shape((experts, count), jnp.float32),
         ],
         in_specs=[IN_VMEM] * 2 + [IN_PLACE] * 3 + [IN_VMEM] * 2 + [IN_PLACE] + [IN_VMEM] * 3,
         out_specs=[IN_PLACE] * 4 + [IN_VMEM] + [IN_PLACE] * 2 + [IN_VMEM] * 3,
@@ -1036,7 +1036,7 @@
     ]
     late = held - first
     tile = tokens // 2
-    lane = lax.broadcasted_iota(jnp.int32, (tile, gates[0].shape[1]), 1)
+    lane = lax.broadcasted_iota(jnp.int32, (tile, gates[0].shape[0]), 1)
 
     def rest_out(e, part, kind):
         slot = part % 2
@@ -1064,7 +1064,7 @@
         for part in range(4):
             block, rows = part // 2, slice((part % 2) * tile, (part % 2 + 1) * tile)
             results = expert_tile(
-                stage[0, block, rows], stage[1, block, rows], gate_rows[block, rows], mine,
+                stage[0, block, rows], stage[1, block, rows], gate_rows[block, :, rows].T, mine,
                 right_a[bank], right_b[bank], right_c[bank],
             )
             router[block, rows] = jnp.where(mine, results[3], router[block, rows])
@@ -1266,7 +1266,7 @@
     flops = 2 * tokens * width * columns * (4 * 3 * held + 12 * (held - first))
     inputs = [unit, *near, *far, w_gate, w_up, w_down, *hs, *cots, *gates, *router_so_far]
     late = held - first
-    small = gates[0].shape
+    small = router_so_far[0].shape
     unit_sum, grads, *blocks, router_far, _, _, _ = pl.pallas_call(
         functools.partial(overlap_kernel, count, first, [shape] * many),
         out_shape=[
@@ -1292,7 +1292,7 @@
             buffers(2, count, rows3 // 3, columns),
             buffers(4, tokens, width),
             buffers(2, tokens, width),
-            pltpu.VMEM((2,) + small, jnp.float32),
+            pltpu.VMEM((2,) + gates[0].shape, jnp.float32),
             pltpu.VMEM((2,) + small, jnp.float32),
             pltpu.VMEM(small, jnp.float32),
             pltpu.VMEM(small, jnp.float32),

time: 760 us -> 757 us (level)
  no operation moved by 1% of the time
where the time goes in v8:
time: 757 us; the launch traced here: 746 us
  Pallas kernels  709 us (94%)
  starting transfers between devices  13.3 us (2%)
  local copies, waits for them, and re-layouts  13.1 us (2%)
    pallas_call x1, Pallas kernels, ring_sum(): pl.pallas_call(functools.partial(ring_kernel, count, many, 5, start, shap...  286 us
    pallas_call x1, Pallas kernels, overlap(): pl.pallas_call(functools.partial(overlap_kernel, count, first, [shape] *...  198 us
    pallas_call x2, Pallas kernels, expert_pass(): pl.pallas_call(functools.partial(expert_kernel, 256, held), grid=(many,),...  51.7 us
    pallas_call x1, Pallas kernels, attention_back(): pl.pallas_call(attention_back_kernel, out_shape=jax.ShapeDtypeStruct((cou...  31.2 us
    pallas_call x1, Pallas kernels, finish(): pl.pallas_call(functools.partial(finish_kernel, firsts), grid=(experts, 4...  31 us
    pallas_call x1, Pallas kernels, attention_forward(): pl.pallas_call(attention_kernel, out_shape=[shape((count, width), jnp.bfl...  30.9 us
    pallas_call x1, Pallas kernels, weight_grads(): pl.pallas_call(weight_kernel, grid=(many, 3), in_specs=[whole(hs[0])] * 8...  29.1 us
    pallas_call x1, Pallas kernels, input_back(): pl.pallas_call(input_kernel, out_shape=[shape((count, width), jnp.float32...  17.9 us
  transfers between devices with their start and end apart: 16, of which 4 were waited for; matrix products, arithmetic and copies ran while one was open for 1% of the time, Pallas kernels for 51%

profile of v8, /device:TPU:0, one launch (start us, length us, event | category | flops | bytes accessed | tf_op | source)
XLA Modules:
  0.0 745.8 jit_solution(16082447288586778460)
XLA Ops:
  0.6 3.0 collective-permute-start
  3.6 1.3 broadcast_in_dim.4.norm_attn
  4.9 1.3 broadcast_in_dim.5.norm_ffn
  8.5 30.9 %attention_forward.1 = (bf16[512,1536]{1,0:T(8,128)(2,1)}, bf16[512,1536]{1,0:T(8,128)(2,1)}, bf16[512,512]{1,0:T(8,128)(2,1)}, bf16[512,512]{1,0:T(8,128)(2,1)}...) custom-call(bf16[512,1536]{1,0:T(8,128)(2,1)} %tokens_in.1, ...), custom_call_target="tpu_custom_call" | custom-call | flops 7247757312 | bytes 18874368 | tf_op jit(solution)/shard_map/attention_forward/pallas_call | solution.py:314
  40.5 1.6 collective-permute-start.5
  45.2 34.5 %expert_pass.2 = (bf16[5,1024,512]{2,1,0:T(8,128)(2,1)}, bf16[5,1024,512]{2,1,0:T(8,128)(2,1)}, bf16[5,1024,512]{2,1,0:T(8,128)(2,1)}, f32[512,20]{1,0:T(8,128)}, f32[512,20]{1,0:T(8,128)}) custom-call(bf16[512,1536]{1,0:T(8,128)(2,1)} %get-tuple-element.91.h0.refs_0_.refs_10_.h_two_in, bf16[512,1536]{1,0:T(8,128)(2,1)} %copy-done.11, ...), custom_call_target="tpu_custom_call" | custom-call | flops 24159191040 | bytes 23592960 | tf_op jit(solution)/shard_map/expert_pass/pallas_call | solution.py:103
  83.8 17.3 %expert_pass.3 = (bf16[2,1024,512]{2,1,0:T(8,128)(2,1)}, bf16[2,1024,512]{2,1,0:T(8,128)(2,1)}, bf16[2,1024,512]{2,1,0:T(8,128)(2,1)}, f32[512,20]{1,0:T(8,128)}, f32[512,20]{1,0:T(8,128)}) custom-call(bf16[512,1536]{1,0:T(8,128)(2,1)} %collective-permute-done.4.h0.refs_2_.refs_12_, bf16[512,1536]{1,0:T(8,128)(2,1)} %collective-permute-done.6.h1.refs_3_.refs_13_, ...), custom_call_target="tpu_custom_call" | custom-call | flops 9663676416 | bytes 9437184 | tf_op jit(solution)/shard_map/expert_pass/pallas_call | solution.py:103
  101.1 29.1 %weight_grads.1 = bf16[2,8,3,192,512]{4,3,2,1,0:T(8,128)(2,1)} custom-call(bf16[512,1536]{1,0:T(8,128)(2,1)} %get-tuple-element.91.h0.refs_0_.refs_10_.h_two_in, bf16[512,1536]{1,0:T(8,128)(2,1)} %copy-done.11, bf16[512,1536]{1,0:T(8,128)(2,1)} %collective-permute-done.4.h0.refs_2_.refs_12_, bf16[512,1536]{1,0:T(8,128)(2,1)} %collective-permute-done.6.h1.refs_3_.refs_13_, ...), custom_call_target="tpu_custom_call" | custom-call | flops 19327352832 | bytes 22020096 | tf_op jit(solution)/shard_map/weight_grads/pallas_call | solution.py:142
  130.2 198.1 %overlap.1 = (bf16[2,8,576,512]{3,2,1,0:T(8,128)(2,1)}, bf16[3,8,3,192,512]{4,3,2,1,0:T(8,128)(2,1)}, bf16[512,1536]{1,0:T(8,128)(2,1)}, bf16[512,1536]{1,0:T(8,...) custom-call(bf16[2,8,576,512]{3,2,1,0:T(8,128)(2,1)} %bitcast.24, ...), custom_call_target="tpu_custom_call" | custom-call | flops 77309411328 | bytes 37748736 | tf_op jit(solution)/shard_map/overlap/pallas_call | solution.py:1270
  328.4 3.4 ring_chunks.4
  332.5 1.5 collective-permute-start.9
  334.7 17.6 %branch_back.1 = (f32[512,1536]{1,0:T(8,128)}, bf16[1536,1792]{1,0:T(8,128)(2,1)}, bf16[512,1536]{1,0:T(8,128)(2,1)}) custom-call(bf16[512,1536]{1,0:T(8,128)(2,1)} %get-tuple-element.116.dh_own, bf16[512,1536]{1,0:T(8,128)(2,1)} %get-tuple-element.117.dh_near, bf16[512,1536]{1,0:T(8,128)(2,1)} %get-tuple-element.118.dh_far, ...), custom_call_target="tpu_custom_call" | custom-call | flops 4831838208 | bytes 18874368 | tf_op jit(solution)/shard_map/branch_back/pallas_call | solution.py:451
  352.4 2.0 add_convert_fusion
  354.4 4.1 ring_chunks.5
  358.4 1.6 collective-permute-start.12
  360.8 31.2 %attention_back.1.d_pre = bf16[512,2560]{1,0:T(8,128)(2,1)} custom-call(bf16[512,1536]{1,0:T(8,128)(2,1)} %get-tuple-element.130.d_attn, bf16[512,1536]{1,0:T(8,128)(2,1)} %get-tuple-element.131.queries, bf16[512,512]{1,0:T(8,128)(2,1)} %get-tuple-element.132.keys, bf16[512,512]{1,0:T(8,128)(2,1)} %get-tuple-element.133.values, ...), custom_call_target="tpu_custom_call" | custom-call | flops 9663676416 | bytes 9437184 | tf_op jit(solution)/shard_map/attention_back/pallas_call | solution.py:484
  393.8 4.1 ring_chunks.6
  397.9 1.6 collective-permute-start.14
  399.9 17.9 %input_back.1 = (f32[512,1536]{1,0:T(8,128)}, bf16[1536,2816]{1,0:T(8,128)(2,1)}) custom-call(bf16[512,2560]{1,0:T(8,128)(2,1)} %attention_back.1.d_pre, bf16[512,1536]{1,0:T(8,128)(2,1)} %get-tuple-element.141.normed, bf16[512,1536]{1,0:T(8,128)(2,1)} %tokens_in.1, bf16[1,1536]{1,0:T(2,128)(2,1)} %broadcast_in_dim.4.norm_attn, ...), custom_call_target="tpu_custom_call" | custom-call | flops 9663676416 | bytes 28311552 | tf_op jit(solution)/shard_map/input_back/pallas_call | solution.py:545
  419.7 4.1 ring_chunks.7
  423.8 285.5 %ring_sum.1 = (bf16[3,8,576,512]{3,2,1,0:T(8,128)(2,1)}, bf16[8,48,1792]{2,1,0:T(8,128)(2,1)}, bf16[8,48,2816]{2,1,0:T(8,128)(2,1)}) custom-call(bf16[3,8,576,512]{3,2,1,0:T(8,128)(2,1)} %bitcast.19, bf16[1536,1792]{1,0:T(8,128)(2,1)} %get-tuple-element.145.refs_1_, bf16[1536,2816]{1,0:T(8,128)(2,1)} %get-tuple-element.147.refs_2_, ...), custom_call_target="tpu_custom_call" | custom-call | flops 28311552 | bytes 113246208 | tf_op jit(solution)/shard_map/ring_sum/pallas_call | solution.py:843
  709.4 31.0 %finish.1 = (f32[5,1536,512]{2,1,0:T(8,128)}, f32[5,1536,512]{2,1,0:T(8,128)}, f32[5,512,1536]{2,1,0:T(8,128)}, f32[384,1536]{1,0:T(8,128)}, f32[384,1536]{1,0:T...) custom-call(bf16[2,8,576,512]{3,2,1,0:T(8,128)(2,1)} %get-tuple-element.144.refs_0_,, ...), custom_call_target="tpu_custom_call" | custom-call | tf_op jit(solution)/shard_map/finish/pallas_call | solution.py:1376
  741.3 1.7 slice_reduce_fusion
  743.7 1.7 slice_reduce_fusion.1
  (67 shorter events, 18.8 us)
Async XLA Ops:
  0.6 38.7 %collective-permute-start = (bf16[512,1536]{1,0:T(8,128)(2,1)}, bf16[512,1536]{1,0:T(8,128)(2,1)S(1)}, u32[]{:S(2)}, u32[]{:S(2)}) collective-permute-start(bf16[512,1536]{1,0:T(8,128)(2,1)} %cotangent.1), channel_id=1, source_target_pairs={{0,2},{2,0},{1,3},{3,1},{4,6},{6,4},{5,7},{7,5},{8,10},{10,8},{9,1... | collective-permute-start | bytes 4718600 | tf_op jit(solution)/shard_map/ppermute | solution.py:1403
  3.6 38.4 %collective-permute-start.2 = (bf16[512,1536]{1,0:T(8,128)(2,1)}, bf16[512,1536]{1,0:T(8,128)(2,1)S(1)}, u32[]{:S(2)}, u32[]{:S(2)}) collective-permute-start(bf16[512,1536]{1,0:T(8,128)(2,1)} %cotangent.1), channel_id=1, source_target_pairs={{0,1},{1,0},{2,3},{3,2},{4,5},{5,4},{6,7},{7,6},{8,9},{9,8},{10,11... | collective-permute-start | bytes 4718600 | tf_op jit(solution)/shard_map/ppermute | solution.py:1399
  39.4 40.3 %copy-start.9 = (bf16[512,1536]{1,0:T(8,128)(2,1)}, bf16[512,1536]{1,0:T(8,128)(2,1)S(1)}, u32[]{:S(2)}) copy-start(bf16[512,1536]{1,0:T(8,128)(2,1)S(1)} %collective-permute-done.c0.refs_6_.refs_16_) | copy-start | bytes 4718596
  39.4 4.0 collective-permute-start.1
  40.0 3.4 collective-permute-start.3
  40.1 39.6 %collective-permute-start.4 = (bf16[512,1536]{1,0:T(8,128)(2,1)}, bf16[512,1536]{1,0:T(8,128)(2,1)}, u32[]{:S(2)}, u32[]{:S(2)}) collective-permute-start(bf16[512,1536]{1,0:T(8,128)(2,1)} %get-tuple-element.91.h0.refs_0_.refs_10_.h_two_in), channel_id=1, source_target_pairs={{0,2},{2,0},{1,3},{3,1},{4,6},{6,4},{5,7},{7,5},{8,10},{10,8},{9,1... | collective-permute-start | bytes 4718600 | tf_op jit(solution)/shard_map/ppermute | solution.py:1403
  40.5 39.1 %collective-permute-start.5 = (f32[20,512]{1,0:T(8,128)}, f32[20,512]{1,0:T(8,128)S(1)}, u32[]{:S(2)}, u32[]{:S(2)}) collective-permute-start(f32[20,512]{1,0:T(8,128)} %get-tuple-element.92.gates0), channel_id=1, source_target_pairs={{0,2},{2,0},{1,3},{3,1},{4,6},{6,4},{5,7},{7,5},{8,10},{10,8},{9,1... | collective-permute-start | bytes 122888 | tf_op jit(solution)/shard_map/ppermute | solution.py:1403
  42.1 1.3 copy-start.10
  42.1 40.9 %collective-permute-start.7 = (bf16[512,1536]{1,0:T(8,128)(2,1)S(1)}, bf16[512,1536]{1,0:T(8,128)(2,1)}, u32[]{:S(2)}, u32[]{:S(2)}) collective-permute-start(bf16[512,1536]{1,0:T(8,128)(2,1)S(1)} %collective-permute-done.c0.refs_6_.refs_16_), channel_id=1, source_target_pairs={{0,1},{1,0},{2,3},{3,2},{4,5},{5,4},{6,7},{7,6},{8,9},{9,8},{10,11... | collective-permute-start | bytes 4718600 | tf_op jit(solution)/shard_map/ppermute | solution.py:1399
  44.0 1.2 copy-start.11
  79.7 3.8 copy-start.12
  79.7 3.8 collective-permute-start.6
  81.9 1.3 collective-permute-start.8
  82.6 251.4 %collective-permute-start.11 = (f32[512,20]{1,0:T(8,128)}, f32[512,20]{1,0:T(8,128)S(1)}, u32[]{:S(2)}, u32[]{:S(2)}) collective-permute-start(f32[512,20]{1,0:T(8,128)} %get-tuple-element.120), channel_id=1, source_target_pairs={{0,1},{1,0},{2,3},{3,2},{4,5},{5,4},{6,7},{7,6},{8,9},{9,8},{10,11... | collective-permute-start | bytes 122888 | tf_op jit(solution)/shard_map/ppermute | solution.py:1399
  331.8 22.6 %collective-permute-start.10 = (bf16[3,576,256]{2,1,0:T(8,128)(2,1)}, bf16[3,576,256]{2,1,0:T(8,128)(2,1)}, u32[]{:S(2)}, u32[]{:S(2)}) collective-permute-start(bf16[3,576,256]{2,1,0:T(8,128)(2,1)} %get-tuple-element.114), channel_id=1, source_target_pairs={{8,0},{16,8},{24,16},{28,24},{20,28},{12,20},{4,12},{0,4},{9,1},{1... | collective-permute-start | bytes 2654216 | tf_op jit(solution)/shard_map/ppermute | solution.py:911
  332.5 21.9 %collective-permute-start.9 = (bf16[3,576,256]{2,1,0:T(8,128)(2,1)}, bf16[3,576,256]{2,1,0:T(8,128)(2,1)}, u32[]{:S(2)}, u32[]{:S(2)}) collective-permute-start(bf16[3,576,256]{2,1,0:T(8,128)(2,1)} %get-tuple-element.113), channel_id=1, source_target_pairs={{0,8},{8,16},{16,24},{24,28},{28,20},{20,12},{12,4},{4,0},{1,9},{9... | collective-permute-start | bytes 2654216 | tf_op jit(solution)/shard_map/ppermute | solution.py:911
  334.7 17.6 %copy-start = (f32[512,1536]{1,0:T(8,128)S(1)}, f32[512,1536]{1,0:T(8,128)}, u32[]{:S(2)}) copy-start(f32[512,1536]{1,0:T(8,128)} %get-tuple-element.88.resid) | copy-start | bytes 9437188
  334.7 17.7 %copy-start.1 = (bf16[512,1536]{1,0:T(8,128)(2,1)S(1)}, bf16[512,1536]{1,0:T(8,128)(2,1)}, u32[]{:S(2)}) copy-start(bf16[512,1536]{1,0:T(8,128)(2,1)} %get-tuple-element.109) | copy-start | bytes 4718596
  334.7 17.7 %copy-start.2 = (bf16[512,1536]{1,0:T(8,128)(2,1)S(1)}, bf16[512,1536]{1,0:T(8,128)(2,1)}, u32[]{:S(2)}) copy-start(bf16[512,1536]{1,0:T(8,128)(2,1)} %get-tuple-element.110) | copy-start | bytes 4718596
  334.7 17.7 %copy-start.3 = (bf16[512,1536]{1,0:T(8,128)(2,1)S(1)}, bf16[512,1536]{1,0:T(8,128)(2,1)}, u32[]{:S(2)}) copy-start(bf16[512,1536]{1,0:T(8,128)(2,1)} %get-tuple-element.111) | copy-start | bytes 4718596
  358.4 33.6 %collective-permute-start.12 = (bf16[3,576,256]{2,1,0:T(8,128)(2,1)}, bf16[3,576,256]{2,1,0:T(8,128)(2,1)S(1)}, u32[]{:S(2)}, u32[]{:S(2)}) collective-permute-start(bf16[3,576,256]{2,1,0:T(8,128)(2,1)} %get-tuple-element.127), channel_id=1, source_target_pairs={{0,8},{8,16},{16,24},{24,28},{28,20},{20,12},{12,4},{4,0},{1,9},{9... | collective-permute-start | bytes 2654216 | tf_op jit(solution)/shard_map/ppermute | solution.py:911
  360.0 32.0 %collective-permute-start.13 = (bf16[3,576,256]{2,1,0:T(8,128)(2,1)}, bf16[3,576,256]{2,1,0:T(8,128)(2,1)S(1)}, u32[]{:S(2)}, u32[]{:S(2)}) collective-permute-start(bf16[3,576,256]{2,1,0:T(8,128)(2,1)} %get-tuple-element.128), channel_id=1, source_target_pairs={{8,0},{16,8},{24,16},{28,24},{20,28},{12,20},{4,12},{0,4},{9,1},{1... | collective-permute-start | bytes 2654216 | tf_op jit(solution)/shard_map/ppermute | solution.py:911
  397.9 19.9 %collective-permute-start.14 = (bf16[3,576,256]{2,1,0:T(8,128)(2,1)}, bf16[3,576,256]{2,1,0:T(8,128)(2,1)S(1)}, u32[]{:S(2)}, u32[]{:S(2)}) collective-permute-start(bf16[3,576,256]{2,1,0:T(8,128)(2,1)} %get-tuple-element.137), channel_id=1, source_target_pairs={{0,8},{8,16},{16,24},{24,28},{28,20},{20,12},{12,4},{4,0},{1,9},{9... | collective-permute-start | bytes 2654216 | tf_op jit(solution)/shard_map/ppermute | solution.py:911
  399.5 19.3 %collective-permute-start.15 = (bf16[3,576,256]{2,1,0:T(8,128)(2,1)}, bf16[3,576,256]{2,1,0:T(8,128)(2,1)S(1)}, u32[]{:S(2)}, u32[]{:S(2)}) collective-permute-start(bf16[3,576,256]{2,1,0:T(8,128)(2,1)} %get-tuple-element.138), channel_id=1, source_target_pairs={{8,0},{16,8},{24,16},{28,24},{20,28},{12,20},{4,12},{0,4},{9,1},{1... | collective-permute-start | bytes 2654216 | tf_op jit(solution)/shard_map/ppermute | solution.py:911
  (7 other events, 5.7 us)
